TPU v7x, 256 devices: a whole 4x4x8 slice. The times are simulated.
256 devices in a mesh: member: 4 (over x), region: 16 (over z, core), block: 4 (over y).
Axes of the slice: x: 4, y: 4, z: 8, core: 2. Of those that a mesh axis runs over, the one named last changes fastest.
Arguments:
- traffic_load: float32 [128, 524288], P('member', ('region', 'block')), may hold values from 0.05 to 0.7
- free_speed: float32 [524288], P(('region', 'block')), may hold values from 0.3 to 0.95
- wave_speed: float32 [524288], P(('region', 'block')), may hold values from 0.15 to 0.6
- jam_density: float32 [524288], P(('region', 'block')), may hold values from 0.8 to 1.2
- capacity_share: float32 [524288], P(('region', 'block')), may hold values from 0.5 to 1
- observation_cell: int32 [196608], P(('region', 'block')), may hold values from 0 to 2047
- obs_count: int32 [256], P(('region', 'block')), may hold values from 1 to 768, 98304 in all
- observation_value: float32 [196608], P(('region', 'block')), may hold values from 0 to 0.8
- observation_variance: float32 [196608], P(('region', 'block')), may hold values from 0.002 to 0.02
- observation_noise: float32 [128, 196608], P('member', ('region', 'block')), may hold values from -6 to 6
- block_lists: int32 [256, 3], P(('region', 'block')), may hold values from 0 to 255, as said below
Outputs:
- analysis: float32 [128, 524288], P('member', ('region', 'block'))
Inputs may be any that keep to these rules, and one draw needn't show every extreme that they name: `block_lists`: row b lists 3 different blocks, b itself among them, each within 4 blocks of b.
All inputs are finite; a program needn't handle non-finite values. No bound on the sum of `obs_count` on one device may be relied on, other than what follows from the above.
Results may differ from a plain program's by a relative error of at most 0.0003.
Values sent between devices are 32-bit elements; how exact they have to be, the bound alone decides.
No kernel may reach another device: no remote copies, remote signals or barrier semaphores. Data moves between devices by JAX's collectives and lax.ppermute only.
A program may use at most 64 MiB of HBM per device.

v0:
```python
import jax
import jax.numpy as jnp
from jax import lax
from jax.sharding import Mesh
from jax.sharding import PartitionSpec as P

REALIZATION_TALLY = 128
HORIZON_TICKS = 16
CELLS_PER_BLOCK = 2048
BLOCK_SLOTS = 768
REGION_BLOCK = ("region_0", "region_1", "block")
MEMBER_REGION_BLOCK = ("member", "region_0", "region_1", "block")


def with_halo(value, sides, width):
    edges = {}
    for axis, dim in sides:
        size, length = (lax.axis_size(axis), value.shape[dim])
        up = [(i, (i + 1) % size) for i in range(size - 1)]
        last = lax.slice_in_dim(value, length - width, length, axis=dim)
        leading = lax.slice_in_dim(value, 0, width, axis=dim)
        edges[dim] = (
            lax.ppermute(last, axis, up),
            lax.ppermute(leading, axis, [(b, a) for a, b in up]),
        )
    done = []
    for _, dim in sides:
        low, high = edges[dim]
        around = [(width, width) if d in done else (0, 0) for d in range(value.ndim)]
        value = jnp.concatenate([jnp.pad(low, around), value, jnp.pad(high, around)], axis=dim)
        done.append(dim)
    return value


def over_axes(value, axes):
    for axis in axes:
        value = lax.psum(value, axis)
    return value


def sent_together(arrays, axis, dim, along):
    ends, at = ([], 0)
    for a in arrays[:-1]:
        at += a.shape[along]
        ends.append(at)
    both = jnp.concatenate(arrays, axis=along)
    return tuple(jnp.split(lax.all_gather(both, axis, axis=dim, tiled=True), ends, axis=along))


def road_capacity(free_speed, wave_speed, jam_density, capacity_share):
    return capacity_share * free_speed * wave_speed * jam_density / (free_speed + wave_speed)


def block_products(left_side, right_side, weight, block_total):
    member_count = left_side.shape[0]
    left_blocks = (left_side * weight).reshape(member_count, block_total, -1)
    right_blocks = right_side.reshape(member_count, block_total, -1)
    return jnp.einsum("kbo,jbo->bkj", left_blocks, right_blocks, precision=lax.Precision.HIGHEST)


def body(
    traffic_load,
    free_speed,
    wave_speed,
    jam_density,
    capacity_share,
    observation_cell,
    obs_count,
    observation_value,
    observation_variance,
    observation_noise,
    block_lists,
):
    mem_local, cell_total = traffic_load.shape
    block_total = obs_count.shape[0]
    slot_total = observation_cell.shape[0]
    capacity = road_capacity(free_speed, wave_speed, jam_density, capacity_share)
    is_last = lax.axis_index(REGION_BLOCK) == lax.axis_size(REGION_BLOCK) - 1
    margin = HORIZON_TICKS
    state_wide = with_halo(traffic_load, ((REGION_BLOCK, 1),), margin)
    road_wide = with_halo(
        jnp.stack([free_speed, wave_speed, jam_density, capacity]), ((REGION_BLOCK, 1),), margin
    )
    speed_wide = road_wide[0]
    wave_wide = road_wide[1]
    jam_wide = road_wide[2]
    capacity_wide = road_wide[3]
    exit_mask = (jnp.arange(cell_total + 2 * margin) == cell_total + margin) & is_last
    exit_value = capacity[-1]

    def advance_wide(step_index, state):
        demand = jnp.minimum(speed_wide * state, capacity_wide)
        supply = jnp.minimum(capacity_wide, wave_wide * (jam_wide - state))
        supply = jnp.where(exit_mask[None, :], exit_value, supply)
        fluxes = jnp.minimum(demand[:, :-1], supply[:, 1:])
        updated = state[:, 1:-1] + fluxes[:, :-1] - fluxes[:, 1:]
        return state.at[:, 1:-1].set(updated)

    predicted_traffic_load = lax.fori_loop(0, HORIZON_TICKS, advance_wide, state_wide)[
        :, margin : margin + cell_total
    ]
    realization_total = lax.psum(jnp.sum(predicted_traffic_load, axis=0), "member")
    realization_average = realization_total / REALIZATION_TALLY
    realization_departure = predicted_traffic_load - realization_average
    slot_cell_index = (
        jnp.arange(slot_total, dtype=jnp.int32) // BLOCK_SLOTS * CELLS_PER_BLOCK + observation_cell
    )
    obs_anomaly = jnp.take(realization_departure, slot_cell_index, axis=1)
    obs_mean = jnp.take(realization_average, slot_cell_index)
    live_mask = (
        (jnp.arange(BLOCK_SLOTS, dtype=jnp.int32)[None, :] < obs_count[:, None])
        .reshape(-1)
        .astype(jnp.float32)
    )
    weight = live_mask / observation_variance
    misfit = observation_value - obs_mean
    obs_all, noise_all = (
        lax.all_to_all(obs_anomaly, "member", split_axis=1, concat_axis=0, tiled=True),
        lax.all_to_all(observation_noise, "member", split_axis=1, concat_axis=0, tiled=True),
    )
    slot_share = slot_total // lax.axis_size("member")
    slot_start = lax.axis_index("member") * slot_share
    slot_weight = lax.dynamic_slice_in_dim(weight, slot_start, slot_share)
    slot_live = lax.dynamic_slice_in_dim(live_mask, slot_start, slot_share)
    slot_var = lax.dynamic_slice_in_dim(observation_variance, slot_start, slot_share)
    slot_misfit = lax.dynamic_slice_in_dim(misfit, slot_start, slot_share)
    group_total = block_total // lax.axis_size("member")
    spread = jnp.sum(obs_all * obs_all, axis=0) / (REALIZATION_TALLY - 1)
    misfit_sum, spread_sum = (
        over_axes(jnp.sum(slot_misfit * slot_misfit * slot_weight), MEMBER_REGION_BLOCK),
        over_axes(jnp.sum(slot_live * (spread / slot_var + 1.0)), MEMBER_REGION_BLOCK),
    )
    inflation = jnp.sqrt(misfit_sum / spread_sum)
    perturbed = slot_misfit + jnp.sqrt(slot_var) * noise_all
    scaled = inflation * obs_all
    gram_part = block_products(scaled, scaled, slot_weight, group_total)
    cross_part = block_products(scaled, perturbed - scaled, slot_weight, group_total)
    gram_part, cross_part = sent_together((gram_part, cross_part), "member", 0, 1)
    neighbour_pairs = with_halo(
        jnp.stack([gram_part, cross_part]), ((REGION_BLOCK, 1),), block_total
    )
    first_block = (lax.axis_index(REGION_BLOCK) - 1) * block_total
    relative = block_lists - first_block
    selector = jnp.sum(
        (
            relative[:, :, None] == jnp.arange(3 * block_total, dtype=jnp.int32)[None, None, :]
        ).astype(jnp.float32),
        axis=1,
    )
    local_gram = jnp.einsum(
        "be,ekj->bkj", selector, neighbour_pairs[0], precision=lax.Precision.HIGHEST
    )
    local_cross = jnp.einsum(
        "be,ekj->bkj", selector, neighbour_pairs[1], precision=lax.Precision.HIGHEST
    )
    identity = (REALIZATION_TALLY - 1) * jnp.eye(REALIZATION_TALLY, dtype=jnp.float32)[None]
    system = identity + local_gram
    factors = jnp.linalg.cholesky(system)
    mixing = jax.vmap(lambda factor, target: jax.scipy.linalg.cho_solve((factor, True), target))(
        factors, local_cross
    )
    member_start = lax.axis_index("member") * mem_local
    own_columns = lax.dynamic_slice_in_dim(mixing, member_start, mem_local, 2)
    row_piece = lax.all_gather(realization_departure, "member", axis=0, tiled=True)
    row_count = row_piece.shape[0]
    piece_blocks = row_piece.reshape(row_count, block_total, CELLS_PER_BLOCK)
    change = (
        jnp.zeros((mem_local, block_total, CELLS_PER_BLOCK), jnp.float32)
        + jnp.einsum("kbc,bkj->jbc", piece_blocks, own_columns, precision=lax.Precision.HIGHEST)
    ).reshape(mem_local, cell_total)
    return realization_average + inflation * realization_departure + inflation * change


def solution(mesh):
    torus = Mesh(
        mesh.devices.reshape(mesh.shape["member"], 8, 2, mesh.shape["block"]),
        ("member", "region_0", "region_1", "block"),
    )
    in_specs = (
        P("member", REGION_BLOCK),
        P(REGION_BLOCK),
        P(REGION_BLOCK),
        P(REGION_BLOCK),
        P(REGION_BLOCK),
        P(REGION_BLOCK),
        P(REGION_BLOCK),
        P(REGION_BLOCK),
        P(REGION_BLOCK),
        P("member", REGION_BLOCK),
        P(REGION_BLOCK, None),
    )
    out_specs = P("member", REGION_BLOCK)
    return jax.shard_map(body, mesh=torus, in_specs=in_specs, out_specs=out_specs, check_vma=False)
```

profile of v0, /device:TPU:8, one launch (start us, length us, event | category | flops | bytes accessed | tf_op | source)
XLA Modules:
  0.0 372.5 jit_solution(5356749427524266633)
XLA Ops:
  8.4 3.5 collective-permute-start.2
  11.9 2.4 collective-permute-start.3
  15.1 3.5 collective-permute-start
  18.6 2.4 collective-permute-start.1
  22.6 1.6 collective-permute-done.1
  25.0 90.6 %while.15 = (s32[]{:T(128)}, f32[32,8224]{1,0:T(8,128)S(1)}, pred[]{:T(512)}, f32[1,8224]{1,0:T(1,128)S(1)}, f32[1,8224]{1,0:T(1,128)S(1)}, /*index=5*/f32[]{:T(...) while((s32[]{:T(128)}, f32[32,8224]{1,0:T(8,128)S(1)}, ...), condition=%wide.region_2.3_spmd.clone, body=%wide.region_1.2_spmd.clone.sunk | while | flops 2647714 | bytes 10195928 | solution.py:99
  26.7 1.3 fusion.57
  28.0 2.7 scatter.7
  32.3 1.3 fusion.57
  33.6 2.7 scatter.7
  38.0 1.3 fusion.57
  39.3 2.7 scatter.7
  43.7 1.3 fusion.57
  45.0 2.7 scatter.7
  49.3 1.3 fusion.57
  50.6 2.7 scatter.7
  55.0 1.3 fusion.57
  56.3 2.7 scatter.7
  60.6 1.3 fusion.57
  62.0 2.7 scatter.7
  66.3 1.3 fusion.57
  67.6 2.7 scatter.7
  72.0 1.3 fusion.57
  73.3 2.7 scatter.7
  77.6 1.3 fusion.57
  78.9 2.7 scatter.7
  83.3 1.3 fusion.57
  84.6 2.7 scatter.7
  89.0 1.3 fusion.57
  90.3 2.7 scatter.7
  94.6 1.3 fusion.57
  95.9 2.7 scatter.7
  100.3 1.3 fusion.57
  101.6 2.7 scatter.7
  106.0 1.3 fusion.57
  107.3 2.7 scatter.7
  111.6 1.3 fusion.57
  112.9 2.7 scatter.7
  116.0 17.1 %psum.63 = f32[8192]{0:T(1024)S(1)} all-reduce(f32[8192]{0:T(1024)S(1)} %slice_reduce_fusion), channel_id=1, replica_groups=mesh['member'=4,'region_0'=8,'region_1'=2,'block'=4] {'member'}, use_global_device_ids=true, to_apply=%region_4.5 | all-reduce | flops 8192 | bytes 65536 | tf_op jit(solution)/shard_map/psum | solution.py:102
  133.1 1.3 slice_subtract_fusion.2
  134.5 1.1 copy-done
  135.6 2.7 copy.76
  138.3 10.3 %gather_fusion.1 = f32[3072,32]{1,0:T(8,128)S(1)} fusion(f32[32,8192]{0,1:T(8,128)} %copy.76, s32[3072]{0:T(1024)S(1)} %broadcast_clamp_fusion), kind=kCustom, calls=%fused_computation.1 | custom fusion | bytes 798720 | tf_op jit(solution)/shard_map/jit(_take)/gather | solution.py:108
  149.8 3.5 all-to-all-start
  154.2 17.4 %gather_fusion = f32[3072]{0:T(1024)S(1)} fusion(f32[8192]{0:T(1024)S(1)} %broadcast_multiply_fusion.1, s32[3072]{0:T(1024)S(1)} %broadcast_clamp_fusion), kind=kCustom, calls=%fused_computation | custom fusion | bytes 36864 | tf_op jit(solution)/shard_map/jit(_take)/gather | solution.py:109
  171.6 4.8 %all-to-all-start.1 = ((f32[32,4,768]{2,0,1:T(8,128)}), f32[32,4,768]{2,0,1:T(8,128)S(1)}, u32[]{:S(2)}, u32[]{:S(2)}) async-start(f32[32,4,768]{2,0,1:T(8,128)} %bitcast.67), calls=%async_computation.1 | async-start | bytes 786432 | tf_op jit(solution)/shard_map/all_to_all | solution.py:119
  176.4 1.5 multiply_reduce_fusion.2
  177.9 13.0 %all-reduce.2 = (f32[]{:T(128)}, f32[]{:T(128)}) all-reduce(f32[]{:T(128)} %get-tuple-element.199, f32[]{:T(128)} %get-tuple-element.214), channel_id=1, replica_groups=mesh['member'=4,'region_0'=8,'region_1'=2,'block'=4] {'member'}, use_global_device_ids=true, to_apply=%region_6.7 | all-reduce | flops 2 | bytes 16 | tf_op jit(solution)/shard_map/psum | solution.py:37
  190.9 20.7 %all-reduce = (f32[]{:T(128)}, f32[]{:T(128)}) all-reduce(f32[]{:T(128)} %get-tuple-element.195, f32[]{:T(128)} %get-tuple-element.196), channel_id=1, replica_groups=mesh['member'=4,'region_0'=8,'region_1'=2,'block'=4] {'region_0'}, use_global_device_ids=true, to_apply=%region_7.8 | all-reduce | flops 2 | bytes 16 | tf_op jit(solution)/shard_map/psum | solution.py:37
  211.5 3.1 all-reduce.3
  214.7 10.9 %all-reduce.1 = (f32[]{:T(128)}, f32[]{:T(128)}) all-reduce(f32[]{:T(128)} %get-tuple-element.197, f32[]{:T(128)} %get-tuple-element.198), channel_id=1, replica_groups=mesh['member'=4,'region_0'=8,'region_1'=2,'block'=4] {'block'}, use_global_device_ids=true, to_apply=%region_9.10 | all-reduce | flops 2 | bytes 16 | tf_op jit(solution)/shard_map/psum | solution.py:37
  228.0 12.8 %all_gather.6 = f32[4,256,128]{2,1,0:T(8,128)S(1)} all-gather(f32[1,256,128]{2,1,0:T(8,128)S(1)} %pad_maximum_fusion.3), channel_id=1, replica_groups=mesh['member'=4,'region_0'=8,'region_1'=2,'block'=4] {'member'}, dimensions={0}, use_global_device_ids=true | all-gather | bytes 655360 | tf_op jit(solution)/shard_map/all_gather | solution.py:47
  242.0 1.9 collective-permute-start.4
  243.9 4.1 %collective-permute-start.5 = (f32[2,4,128,128]{3,1,2,0:T(4,128)S(1)}, f32[2,4,128,128]{3,1,2,0:T(4,128)}, u32[]{:S(2)}, u32[]{:S(2)}) collective-permute-start(f32[2,4,128,128]{3,1,2,0:T(4,128)S(1)} %pad_maximum_fusion.1), channel_id=1, source_target_pairs={{1,0},{2,1},{3,2},{4,3},{5,4},{6,5},{7,6},{8,7},{9,8},{10,9},{11,1... | collective-permute-start | bytes 1572872 | tf_op jit(solution)/shard_map/ppermute | solution.py:24
  249.0 5.4 %collective-permute-done.4 = f32[2,4,128,128]{3,1,2,0:T(4,128)S(1)} collective-permute-done((f32[2,4,128,128]{3,1,2,0:T(4,128)S(1)}, f32[2,4,128,128]{3,1,2,0:T(4,128)S(1)}, u32[]{:S(2)}, u32[]{:S(2)}) %collective-permute-start.4) | collective-permute-done | bytes 524320 | tf_op jit(solution)/shard_map/ppermute | solution.py:23
  255.2 1.2 collective-permute-done.5
  256.4 1.7 pad_maximum_fusion
  259.6 1.7 fusion.25
  261.3 47.7 %custom-call.11 = f32[4,128,128]{2,1,0:T(8,128)S(1)} custom-call(f32[4,128,128]{2,1,0:T(8,128)} %fusion.25), custom_call_target="Cholesky" | custom-call | tf_op jit(solution)/shard_map/jit(cholesky)/cholesky | solution.py:158
  309.9 40.1 %custom-call.12 = f32[4,1,128,128]{2,3,1,0:T(8,128)S(1)} custom-call(f32[4,1,128,128]{3,2,1,0:T(8,128)} %select_bitcast_fusion), custom_call_target="InvertDiagBlocksLowerTriangular" | custom-call | tf_op jit(solution)/shard_map/vmap(jit(_cho_solve))/triangular_solve | solution.py:159
  350.1 1.3 fusion.10
  352.7 5.6 %copy.88 = f32[128,8192]{0,1:T(8,128)} copy(f32[128,8192]{1,0:T(8,128)} %all-gather.2.cloned.1.call-done) | data formatting | bytes 8388608 | tf_op jit(solution)/shard_map/all_gather | solution.py:164
  358.2 6.0 %fusion.9 = f32[4,4,8,2048]{3,2,1,0:T(8,128)S(1)} fusion(f32[128,4,2048]{0,2,1:T(8,128)} %bitcast.71, f32[]{:T(128)S(6)} %sqrt.6, f32[4,128,128]{1,2,0:T(8,128)S(1)} %fusion.20, s32[]{:T(128)S(6)} %select_n.46), kind=kOutput, calls=%fused_computation.16 | convolution fusion | flops 402915328 | bytes 5308424 | tf_op jit(solution)/shard_map/kbc,bkj->jbc/dot_general | solution.py:169
  364.3 1.3 add_add_fusion
  (226 shorter events, 41.4 us)
Async XLA Ops:
  6.5 17.7 %copy-start.2 = (f32[32,8192]{1,0:T(8,128)S(1)}, f32[32,8192]{1,0:T(8,128)}, u32[]{:S(2)}) copy-start(f32[32,8192]{1,0:T(8,128)} %param.15) | copy-start | bytes 3145732
  6.5 346.1 %all-gather.2.cloned.1.call-start = ((), (), s32[]{:S(2)}) async-start(), calls=%async_computation.2 | async-start | bytes 5242880 | tf_op jit(solution)/shard_map/all_gather | solution.py:164
  8.4 13.8 %collective-permute-start.2 = (f32[4,16]{1,0:T(4,128)S(1)}, f32[4,16]{1,0:T(4,128)S(1)}, u32[]{:S(2)}, u32[]{:S(2)}) collective-permute-start(f32[4,16]{1,0:T(4,128)S(1)} %get-tuple-element.213), channel_id=1, source_target_pairs={{0,1},{1,2},{2,3},{3,4},{4,5},{5,6},{6,7},{7,8},{8,9},{9,10},{10,1... | collective-permute-start | bytes 776 | tf_op jit(solution)/shard_map/ppermute | solution.py:23
  11.9 10.3 %collective-permute-start.3 = (f32[4,16]{1,0:T(4,128)S(1)}, f32[4,16]{1,0:T(4,128)S(1)}, u32[]{:S(2)}, u32[]{:S(2)}) collective-permute-start(f32[4,16]{1,0:T(4,128)S(1)} %get-tuple-element.212), channel_id=1, source_target_pairs={{1,0},{2,1},{3,2},{4,3},{5,4},{6,5},{7,6},{8,7},{9,8},{10,9},{11,1... | collective-permute-start | bytes 776 | tf_op jit(solution)/shard_map/ppermute | solution.py:24
  15.1 7.5 %collective-permute-start = (f32[32,16]{1,0:T(8,128)S(1)}, f32[32,16]{1,0:T(8,128)S(1)}, u32[]{:S(2)}, u32[]{:S(2)}) collective-permute-start(f32[32,16]{1,0:T(8,128)S(1)} %get-tuple-element.205), channel_id=1, source_target_pairs={{0,1},{1,2},{2,3},{3,4},{4,5},{5,6},{6,7},{7,8},{8,9},{9,10},{10,1... | collective-permute-start | bytes 6152 | tf_op jit(solution)/shard_map/ppermute | solution.py:23
  18.6 5.6 %collective-permute-start.1 = (f32[32,16]{1,0:T(8,128)S(1)}, f32[32,16]{1,0:T(8,128)S(1)}, u32[]{:S(2)}, u32[]{:S(2)}) collective-permute-start(f32[32,16]{1,0:T(8,128)S(1)} %get-tuple-element.204), channel_id=1, source_target_pairs={{1,0},{2,1},{3,2},{4,3},{5,4},{6,5},{7,6},{8,7},{9,8},{10,9},{11,1... | collective-permute-start | bytes 6152 | tf_op jit(solution)/shard_map/ppermute | solution.py:24
  133.0 1.4 copy-start.5
  134.4 1.2 copy-start
  149.0 4.3 %copy-start.8 = (s32[4]{0:T(128)S(1)}, s32[4]{0:T(128)}, u32[]{:S(2)}) copy-start(s32[4]{0:T(128)} %param.21) | copy-start | bytes 52
  149.0 4.4 %copy-start.4 = (f32[32,3072]{1,0:T(8,128)S(1)}, f32[32,3072]{1,0:T(8,128)}, u32[]{:S(2)}) copy-start(f32[32,3072]{1,0:T(8,128)} %param.24) | copy-start | bytes 1179652
  149.8 21.8 %all-to-all-start = ((f32[32,4,768]{2,0,1:T(8,128)}), f32[32,4,768]{2,0,1:T(8,128)S(1)}, u32[]{:S(2)}, u32[]{:S(2)}) async-start(f32[32,4,768]{2,0,1:T(8,128)} %broadcast_select_fusion), calls=%async_computation | async-start | bytes 786432 | tf_op jit(solution)/shard_map/all_to_all | solution.py:118
  171.6 55.9 %all-to-all-start.1 = ((f32[32,4,768]{2,0,1:T(8,128)}), f32[32,4,768]{2,0,1:T(8,128)S(1)}, u32[]{:S(2)}, u32[]{:S(2)}) async-start(f32[32,4,768]{2,0,1:T(8,128)} %bitcast.67), calls=%async_computation.1 | async-start | bytes 786432 | tf_op jit(solution)/shard_map/all_to_all | solution.py:119
  240.8 7.3 %copy-start.7 = (s32[4,3]{1,0:T(4,128)S(1)}, s32[4,3]{1,0:T(4,128)}, u32[]{:S(2)}) copy-start(s32[4,3]{1,0:T(4,128)} %param.25) | copy-start | bytes 148
  241.2 0.7 copy-start.1
  242.0 12.4 %collective-permute-start.4 = (f32[2,4,128,128]{3,1,2,0:T(4,128)S(1)}, f32[2,4,128,128]{3,1,2,0:T(4,128)S(1)}, u32[]{:S(2)}, u32[]{:S(2)}) collective-permute-start(f32[2,4,128,128]{3,1,2,0:T(4,128)S(1)} %pad_maximum_fusion.1), channel_id=1, source_target_pairs={{0,1},{1,2},{2,3},{3,4},{4,5},{5,6},{6,7},{7,8},{8,9},{9,10},{10,1... | collective-permute-start | bytes 1572872 | tf_op jit(solution)/shard_map/ppermute | solution.py:23
  243.9 12.5 %collective-permute-start.5 = (f32[2,4,128,128]{3,1,2,0:T(4,128)S(1)}, f32[2,4,128,128]{3,1,2,0:T(4,128)}, u32[]{:S(2)}, u32[]{:S(2)}) collective-permute-start(f32[2,4,128,128]{3,1,2,0:T(4,128)S(1)} %pad_maximum_fusion.1), channel_id=1, source_target_pairs={{1,0},{2,1},{3,2},{4,3},{5,4},{6,5},{7,6},{8,7},{9,8},{10,9},{11,1... | collective-permute-start | bytes 1572872 | tf_op jit(solution)/shard_map/ppermute | solution.py:24
  248.3 9.8 %copy-start.6 = (f32[4,12]{1,0:T(4,128)}, f32[4,12]{1,0:T(4,128)S(1)}, u32[]{:S(2)}) copy-start(f32[4,12]{1,0:T(4,128)S(1)} %convert_reduce_fusion) | copy-start | bytes 580
  254.4 0.8 copy-start.3
Sparse Core Ops, SparseCore 0:
  134.5 60.4 all-gather.1
where the time goes:
time: 378 us; the launch traced here: 372 us
  other arithmetic  143 us (38%)
  local copies, waits for them, and re-layouts  91.3 us (24%)
  blocking collectives  77.6 us (21%)
  starting transfers between devices  25.9 us (7%)
  between operations  15.1 us (4%)
  matrix products  10.1 us (3%)
  waiting for transfers between devices  8.35 us (2%)
    another operation x4, other arithmetic, body(): factors = jnp.linalg.cholesky(system)  47.9 us
    psum x4, blocking collectives, over_axes(): value = lax.psum(value, axis)  47.7 us
    scatter x16, local copies, waits for them, and re-layouts, advance_wide(): return state.at[:, 1:-1].set(updated)  42.5 us
    another operation x3, other arithmetic, body(): jax.scipy.linalg.cho_solve((factor, True), target)  40.9 us
    another operation x17, other arithmetic  21.6 us
    gather x1, local copies, waits for them, and re-layouts, body(): obs_mean = jnp.take(realization_average, slot_cell_index)  17.4 us
    psum x1, blocking collectives, body(): lax.psum(jnp.sum(predicted_traffic_load, axis=0), 'member')  17.1 us
    min x16, other arithmetic, advance_wide(): fluxes = jnp.minimum(demand[:, :-1], supply[:, 1:])  15.8 us
  transfers between devices with their start and end apart: 9, of which 3 were waited for; matrix products, arithmetic and copies ran while one was open for 36% of the time, Pallas kernels for 0%

commit v1 on v0

v1 whole, which is shorter than its diff:
```python
import jax
import jax.numpy as jnp
from jax import lax
from jax.experimental import pallas as pl
from jax.experimental.pallas import tpu as pltpu
from jax.sharding import PartitionSpec as P

TALLY = 128
TICKS = 16
CELLS = 2048
SLOTS = 768
LANES = 128
RB = ("region", "block")
HIGHEST = lax.Precision.HIGHEST


def vmem(n):
    return [pl.BlockSpec(memory_space=pltpu.VMEM) for _ in range(n)]


def forecast_kernel(state_ref, low_ref, high_ref, road_ref, cell_ref, fore_ref, obs_ref, wide_ref, side_ref):
    rows, width = state_ref.shape
    full = width + 2 * LANES
    wide_ref[:, :LANES] = low_ref[:rows, :]
    wide_ref[:, LANES : LANES + width] = state_ref[...]
    wide_ref[:, LANES + width :] = high_ref[:rows, :]
    side_ref[0:4, :LANES] = low_ref[rows : rows + 4, :]
    side_ref[0:4, LANES : LANES + width] = road_ref[...]
    side_ref[0:4, LANES + width :] = high_ref[rows : rows + 4, :]

    def step(_, carry):
        for g in range(rows // 8):
            at = pl.ds(8 * g, 8)
            x = wide_ref[at, :]
            speed = side_ref[0:1, :]
            wave = side_ref[1:2, :]
            jam = side_ref[2:3, :]
            cap = side_ref[3:4, :]
            demand = jnp.minimum(speed * x, cap)
            supply = jnp.minimum(cap, wave * (jam - x))
            flux = jnp.minimum(demand, pltpu.roll(supply, full - 1, 1))
            wide_ref[at, :] = x + pltpu.roll(flux, 1, 1) - flux
        return carry

    lax.fori_loop(0, TICKS, step, 0)
    blocks = width // CELLS
    for b in range(blocks):
        fore_ref[b] = wide_ref[:, LANES + b * CELLS : LANES + (b + 1) * CELLS]

    def gather(q, carry):
        b = q // (SLOTS // LANES)
        cells = cell_ref[pl.ds(q, 1), :]
        lane = jnp.broadcast_to(cells & (LANES - 1), (8, LANES))
        tile = jnp.broadcast_to(cells >> 7, (8, LANES))
        acc = [jnp.zeros((8, LANES), jnp.float32) for _ in range(rows // 8)]
        for c in range(CELLS // LANES):
            hit = tile == c
            for g in range(rows // 8):
                piece = fore_ref[b, pl.ds(8 * g, 8), c * LANES : (c + 1) * LANES]
                got = jnp.take_along_axis(piece, lane, axis=1)
                acc[g] = jnp.where(hit, got, acc[g])
        for g in range(rows // 8):
            obs_ref[q, pl.ds(8 * g, 8), :] = acc[g]
        return carry

    lax.fori_loop(0, blocks * (SLOTS // LANES), gather, 0)


def forecast(state, low, high, road, cells):
    rows, width = state.shape
    blocks = width // CELLS
    chunks = blocks * SLOTS // LANES
    return pl.pallas_call(
        forecast_kernel,
        out_shape=(
            jax.ShapeDtypeStruct((blocks, rows, CELLS), jnp.float32),
            jax.ShapeDtypeStruct((chunks, rows, LANES), jnp.float32),
        ),
        in_specs=vmem(5),
        out_specs=tuple(vmem(2)),
        scratch_shapes=[
            pltpu.VMEM((rows, width + 2 * LANES), jnp.float32),
            pltpu.VMEM((8, width + 2 * LANES), jnp.float32),
        ],
        name="forecast",
    )(state, low, high, road, cells)


def products_kernel(obs_ref, noise_ref, slot_ref, count_ref, pair_ref, sum_ref):
    chunks = obs_ref.shape[1]
    pieces = [jnp.concatenate([obs_ref[m, q] for m in range(obs_ref.shape[0])], axis=0) for q in range(chunks)]
    noises = [jnp.concatenate([noise_ref[m, q] for m in range(noise_ref.shape[0])], axis=0) for q in range(chunks)]
    count = count_ref[0, 0]
    total_a = jnp.zeros((1, LANES), jnp.float32)
    total_b = jnp.zeros((1, LANES), jnp.float32)
    scaled, plain, moved = [], [], []
    for q in range(chunks):
        x = pieces[q]
        value = slot_ref[0, pl.ds(q, 1), :]
        variance = slot_ref[1, pl.ds(q, 1), :]
        mean = jnp.sum(x, axis=0, keepdims=True) / TALLY
        a = x - mean
        slot = lax.broadcasted_iota(jnp.int32, (1, LANES), 1) + q * LANES
        live = (slot < count).astype(jnp.float32)
        weight = live / variance
        misfit = value - mean
        spread = jnp.sum(a * a, axis=0, keepdims=True) / (TALLY - 1)
        total_a += misfit * misfit * weight
        total_b += live * (spread / variance + 1.0)
        scaled.append(a * weight)
        plain.append(a)
        moved.append(misfit + jnp.sqrt(variance) * noises[q])
    left = jnp.concatenate(scaled, axis=1)
    dims = (((1,), (1,)), ((), ()))
    pair_ref[0] = lax.dot_general(left, jnp.concatenate(plain, axis=1), dims, precision=HIGHEST, preferred_element_type=jnp.float32)
    pair_ref[1] = lax.dot_general(left, jnp.concatenate(moved, axis=1), dims, precision=HIGHEST, preferred_element_type=jnp.float32)
    row = lax.broadcasted_iota(jnp.int32, (8, LANES), 0)
    sum_a = jnp.sum(total_a, axis=1, keepdims=True)
    sum_b = jnp.sum(total_b, axis=1, keepdims=True)
    sum_ref[...] = jnp.where(row == 0, sum_a, jnp.where(row == 1, sum_b, 0.0))


def products(obs, noise, slots, count):
    return pl.pallas_call(
        products_kernel,
        out_shape=(
            jax.ShapeDtypeStruct((2, TALLY, TALLY), jnp.float32),
            jax.ShapeDtypeStruct((8, LANES), jnp.float32),
        ),
        in_specs=vmem(3) + [pl.BlockSpec(memory_space=pltpu.SMEM)],
        out_specs=tuple(vmem(2)),
        name="products",
    )(obs, noise, slots, count)


def solve_kernel(part_ref, sums_ref, mixing_ref, scale_ref):
    sums = jnp.sum(sums_ref[...], axis=0)
    scale = jnp.sqrt(sums[0:1, :] / sums[1:2, :])
    scale_ref[...] = jnp.broadcast_to(scale, (8, LANES))
    gram = part_ref[0, 0]
    cross = part_ref[0, 1]
    for m in range(1, part_ref.shape[0]):
        gram = gram + part_ref[m, 0]
        cross = cross + part_ref[m, 1]
    row = lax.broadcasted_iota(jnp.int32, (TALLY, TALLY), 0)
    lane = lax.broadcasted_iota(jnp.int32, (TALLY, TALLY), 1)
    eye = jnp.where(row == lane, jnp.float32(TALLY - 1), jnp.float32(0.0))
    system = eye + (scale * scale) * gram
    target = eye + scale * cross
    both = jnp.concatenate([system, target], axis=1)
    tiles = [both[8 * i : 8 * i + 8, :] for i in range(TALLY // 8)]
    sub = lax.broadcasted_iota(jnp.int32, (8, 2 * TALLY), 0)
    for k in range(TALLY // 8):
        panel = tiles[k]
        for j in range(8):
            at = 8 * k + j
            column = panel[:, at : at + 1]
            pivot_row = panel[j : j + 1, :]
            inverse = 1.0 / panel[j : j + 1, at : at + 1]
            pivot_row = pivot_row * inverse
            panel = jnp.where(sub == j, pivot_row, panel - column * pivot_row)
        for i in range(TALLY // 8):
            if i != k:
                tile = tiles[i]
                new = tile
                for j in range(8):
                    new = new - tile[:, 8 * k + j : 8 * k + j + 1] * panel[j : j + 1, :]
                tiles[i] = new
        tiles[k] = panel
    for i in range(TALLY // 8):
        mixing_ref[8 * i : 8 * i + 8, :] = tiles[i][:, TALLY:]


def solve(parts, sums):
    return pl.pallas_call(
        solve_kernel,
        out_shape=(
            jax.ShapeDtypeStruct((TALLY, TALLY), jnp.float32),
            jax.ShapeDtypeStruct((8, LANES), jnp.float32),
        ),
        in_specs=vmem(2),
        out_specs=tuple(vmem(2)),
        name="solve",
    )(parts, sums)


def analysis_kernel(fore_ref, mixing_ref, scale_ref, out_ref):
    groups = fore_ref.shape[0]
    state = jnp.concatenate([fore_ref[m] for m in range(groups)], axis=0)
    mean = jnp.sum(state, axis=0, keepdims=True) / TALLY
    anomaly = state - mean
    mixing = mixing_ref[...] * scale_ref[0:1, :]
    change = lax.dot_general(
        mixing, anomaly, (((0,), (0,)), ((), ())), precision=HIGHEST, preferred_element_type=jnp.float32
    )
    out = mean + change
    rows = fore_ref.shape[1]
    for m in range(groups):
        out_ref[m] = out[m * rows : (m + 1) * rows, :]


def analysis(fore, mixing, scale):
    return pl.pallas_call(
        analysis_kernel,
        out_shape=jax.ShapeDtypeStruct(fore.shape, jnp.float32),
        in_specs=vmem(3),
        out_specs=vmem(1)[0],
        name="analysis",
    )(fore, mixing, scale)


def shared_sums(value, axes):
    size = 1
    for axis in axes:
        size *= lax.axis_size(axis)
    copies = jnp.broadcast_to(value[None], (size,) + value.shape)
    return lax.all_to_all(copies, axes, 0, 0)


def body(load, free_speed, wave_speed, jam_density, capacity_share, cell, count, value, variance, noise, lists):
    rows, width = load.shape
    blocks = width // CELLS
    members = lax.axis_size("member")
    member = lax.axis_index("member")
    slab = lax.axis_index(RB)
    slabs = lax.axis_size(RB)
    up = [(i, i + 1) for i in range(slabs - 1)]
    down = [(b, a) for a, b in up]

    capacity = capacity_share * free_speed * wave_speed * jam_density / (free_speed + wave_speed)
    road = jnp.stack([free_speed, wave_speed, jam_density, capacity])
    edge_last = jnp.concatenate([load[:, width - TICKS :], road[:, width - TICKS :]], axis=0)
    edge_first = jnp.concatenate([load[:, :TICKS], road[:, :TICKS]], axis=0)
    low = lax.ppermute(edge_last, RB, up)
    high = lax.ppermute(edge_first, RB, down)
    beyond = jnp.concatenate(
        [jnp.zeros((rows + 1,)), jnp.array([1.0, 1000.0]), capacity[width - 1 :]]
    ).astype(jnp.float32)
    high = jnp.where(slab == slabs - 1, beyond[:, None], high)
    low = jnp.pad(low, ((0, 0), (LANES - TICKS, 0)))
    high = jnp.pad(high, ((0, 0), (0, LANES - TICKS)))

    per_block = SLOTS // LANES
    noise_out = noise.reshape(rows, blocks * per_block, LANES).transpose(1, 0, 2).reshape(blocks, per_block, rows, LANES)
    noise_all = lax.all_to_all(noise_out, "member", 0, 0)
    fore, obs = forecast(load, low, high, road, cell.reshape(blocks * per_block, LANES))
    obs_all = lax.all_to_all(obs.reshape(blocks, per_block, rows, LANES), "member", 0, 0)
    fore_all = lax.all_to_all(fore, "member", 0, 0)

    slots = jnp.stack([value, variance]).reshape(2, blocks, per_block, LANES)
    slots = lax.dynamic_index_in_dim(slots, member, 1, keepdims=False)
    own_count = lax.dynamic_slice_in_dim(count, member, 1).reshape(1, 1)
    pair, sums = products(obs_all, noise_all, slots, own_count)

    below = lax.ppermute(pair, RB, up)
    above = lax.ppermute(pair, RB, down)
    sums = jnp.sum(shared_sums(sums, ("member", "block")), axis=0)
    sums = shared_sums(sums, ("region",))

    names = (slab + jnp.arange(-1, 2, dtype=jnp.int32)) * blocks + member
    chosen = jnp.any(lists[:, None, :] == names[None, :, None], axis=2)
    chosen = chosen.astype(jnp.float32)[:, :, None, None, None]
    parts = chosen[:, 0] * below[None] + chosen[:, 1] * pair[None] + chosen[:, 2] * above[None]
    parts = lax.all_to_all(parts, "member", 0, 0)
    mixing, scale = solve(parts, sums)
    out = analysis(fore_all, mixing, scale)
    out = lax.all_to_all(out, "member", 0, 0)
    return out.transpose(1, 0, 2).reshape(rows, width)


def solution(mesh):
    in_specs = (
        P("member", RB), P(RB), P(RB), P(RB), P(RB), P(RB), P(RB), P(RB), P(RB), P("member", RB), P(RB, None),
    )
    return jax.shard_map(body, mesh=mesh, in_specs=in_specs, out_specs=P("member", RB), check_vma=False)
```

time: 378 us -> 144 us (0.38); the launches traced: 372 us -> 143 us
  other arithmetic: 143 us -> 2.8 us
  local copies, waits for them, and re-layouts: 91.3 us -> 11.8 us
  blocking collectives: 77.6 us -> 30.7 us
  Pallas kernels: 0 us -> 34.8 us
  starting transfers between devices: 25.9 us -> 41.1 us
  between operations: 15.1 us -> 0.21 us
  waiting for transfers between devices: 8.35 us -> 21.3 us
  matrix products: 10.1 us -> 0 us
    another operation x26 -> x1, other arithmetic: 111 us -> 0.13 us  [body(): road = jnp.stack([free_speed, wave_speed, jam_density, capacity])]
    psum x5 -> x0, blocking collectives: 64.8 us -> none  [the longest x4 47.7 us: over_axes(): value = lax.psum(value, axis)]
    scatter x16 -> x0, local copies, waits for them, and re-layouts: 42.5 us -> none  [advance_wide(): return state.at[:, 1:-1].set(updated)]
    pallas_call x0 -> x4, Pallas kernels: none -> 34.8 us  [the longest x1 16.1 us: forecast(): pl.pallas_call(forecast_kernel, out_shape=(jax.ShapeDtypeStruct((blocks,...]
    all_to_all x0 -> x2, blocking collectives: none -> 30.7 us  [the longest x1 17.4 us: body(): out = lax.all_to_all(out, 'member', 0, 0)]
    gather x3 -> x0, local copies, waits for them, and re-layouts: 28.1 us -> none  [the longest x1 17.4 us: body(): obs_mean = jnp.take(realization_average, slot_cell_index)]
    all_to_all x2 -> x5, waiting for transfers between devices: 0.01 us -> 21.3 us  [the longest x2 13.8 us: shared_sums(): return lax.all_to_all(copies, axes, 0, 0)]
    all_to_all x2 -> x5, starting transfers between devices: 8.23 us -> 29.2 us  [the longest x2 16.8 us: shared_sums(): return lax.all_to_all(copies, axes, 0, 0)]
  transfers between devices with their start and end apart: 9 -> 9, of which waited for: 3 -> 4; matrix products, arithmetic and copies ran while one was open for 36% -> 5% of each run, Pallas kernels for 0% -> 20%
where the time goes in v1:
time: 144 us; the launch traced here: 143 us
  starting transfers between devices  41.1 us (29%)
  Pallas kernels  34.8 us (24%)
  blocking collectives  30.7 us (21%)
  waiting for transfers between devices  21.3 us (15%)
  local copies, waits for them, and re-layouts  11.8 us (8%)
  other arithmetic  2.8 us (2%)
    all_to_all x1, blocking collectives, body(): out = lax.all_to_all(out, 'member', 0, 0)  17.4 us
    all_to_all x2, starting transfers between devices, shared_sums(): return lax.all_to_all(copies, axes, 0, 0)  16.8 us
    pallas_call x1, Pallas kernels, forecast(): pl.pallas_call(forecast_kernel, out_shape=(jax.ShapeDtypeStruct((blocks,...  16.1 us
    all_to_all x2, waiting for transfers between devices, shared_sums(): return lax.all_to_all(copies, axes, 0, 0)  13.8 us
    all_to_all x1, blocking collectives, body(): parts = lax.all_to_all(parts, 'member', 0, 0)  13.3 us
    pallas_call x1, Pallas kernels, solve(): pl.pallas_call(solve_kernel, out_shape=(jax.ShapeDtypeStruct((TALLY, TALL...  12.1 us
    unnamed x32, local copies, waits for them, and re-layouts  5.08 us
    all_to_all x1, starting transfers between devices, body(): lax.all_to_all(obs.reshape(blocks, per_block, rows, LANES), 'member', 0, 0)  4.8 us
  transfers between devices with their start and end apart: 9, of which 4 were waited for; matrix products, arithmetic and copies ran while one was open for 5% of the time, Pallas kernels for 20%

profile of v1, /device:TPU:8, one launch (start us, length us, event | category | flops | bytes accessed | tf_op | source)
XLA Modules:
  0.0 142.7 jit_solution(5058801517345093696)
XLA Ops:
  0.0 0.0 copy-start
  0.0 0.0 copy-start.7
  0.0 0.0 copy-start.8
  0.0 0.0 copy-start.9
  0.0 0.9 add_divide_fusion
  0.9 0.0 copy-done.7
  0.9 0.0 copy-done.8
  0.9 0.0 copy-done.9
  0.9 0.1 pad_maximum_fusion.road_ref
  1.1 0.0 copy-start.4
  1.1 0.1 fusion.3
  1.1 0.8 fusion.2
  2.0 4.1 %collective-permute-start.1 = (f32[36,16]{1,0:T(8,128)S(1)}, f32[36,16]{1,0:T(8,128)S(1)}, u32[]{:S(2)}, u32[]{:S(2)}) collective-permute-start(f32[36,16]{1,0:T(8,128)S(1)} %pad_maximum_fusion.2), channel_id=1, source_target_pairs={{1,0},{2,1},{3,2},{4,3},{5,4},{6,5},{7,6},{8,7},{9,8},{10,9},{11,1... | collective-permute-start | bytes 6920 | tf_op jit(solution)/shard_map/ppermute | solution.py:235
  6.1 1.9 %collective-permute-start = (f32[36,16]{1,0:T(8,128)S(1)}, f32[36,16]{1,0:T(8,128)S(1)}, u32[]{:S(2)}, u32[]{:S(2)}) collective-permute-start(f32[36,16]{1,0:T(8,128)S(1)} %pad_maximum_fusion.1), channel_id=1, source_target_pairs={{0,1},{1,2},{2,3},{3,4},{4,5},{5,6},{6,7},{7,8},{8,9},{9,10},{10,1... | collective-permute-start | bytes 6920 | tf_op jit(solution)/shard_map/ppermute | solution.py:234
  8.0 0.0 copy-done
  8.0 0.8 copy_bitcast_fusion
  8.8 0.0 copy-done.4
  8.8 4.1 %all-to-all-start.2 = ((f32[4,6,32,128]{3,2,1,0:T(8,128)}), f32[4,6,32,128]{3,2,1,0:T(8,128)S(1)}, u32[]{:S(2)}, u32[]{:S(2)}) async-start(f32[4,6,32,128]{3,2,1,0:T(8,128)} %bitcast.8), calls=%async_computation.2 | async-start | bytes 786432 | tf_op jit(solution)/shard_map/all_to_all | solution.py:245
  12.9 0.6 slice.33
  13.5 0.7 copy-done.14
  14.2 0.7 pad_maximum_fusion.3
  14.9 0.0 collective-permute-done.1
  14.9 0.1 broadcast_select_fusion
  14.9 0.6 pad.9.high_ref
  15.6 0.0 collective-permute-done
  15.6 0.7 pad.8.low_ref
  16.2 16.1 %forecast.1 = (f32[4,32,2048]{2,1,0:T(8,128)}, f32[24,32,128]{2,1,0:T(8,128)}) custom-call(f32[32,8192]{1,0:T(8,128)} %state_ref.1, f32[36,128]{1,0:T(8,128)} %pad.8.low_ref, f32[36,128]{1,0:T(8,128)} %pad.9.high_ref, f32[4,8192]{1,0:T(4,128)} %copy-done.4, s32[24,128]{1,0:T(8,128)} %bitcast.28), custom_call_target="tpu_custom_call" | custom-call | tf_op jit(solution)/shard_map/forecast/pallas_call | solution.py:73
  32.4 0.0 all-to-all-done.2.noise_ref
  32.4 0.7 copy-done.2
  33.1 4.8 %all-to-all-start.1 = ((f32[4,6,32,128]{3,2,1,0:T(8,128)}), f32[4,6,32,128]{3,2,1,0:T(8,128)S(1)}, u32[]{:S(2)}, u32[]{:S(2)}) async-start(f32[4,6,32,128]{3,2,1,0:T(8,128)} %bitcast.22), calls=%async_computation.1 | async-start | bytes 786432 | tf_op jit(solution)/shard_map/all_to_all | solution.py:247
  37.9 0.0 copy-done.10
  37.9 0.7 copy-done.11
  38.6 0.7 copy-done.15
  39.3 0.6 dynamic_slice.8
  39.9 0.6 fusion.1.slot_ref
  40.5 4.8 %all-to-all-done.1.obs_ref = f32[4,6,32,128]{3,2,1,0:T(8,128)S(1)} async-done(((f32[4,6,32,128]{3,2,1,0:T(8,128)}), f32[4,6,32,128]{3,2,1,0:T(8,128)S(1)}, u32[]{:S(2)}, u32[]{:S(2)}) %all-to-all-start.1) | async-done | bytes 393248 | tf_op jit(solution)/shard_map/all_to_all | solution.py:247
  45.3 0.7 copy-done.3
  46.1 3.2 %products.1 = (f32[2,128,128]{2,1,0:T(8,128)}, f32[8,128]{1,0:T(8,128)}) custom-call(f32[4,6,32,128]{3,2,1,0:T(8,128)} %copy-done.3, f32[4,6,32,128]{3,2,1,0:T(8,128)} %copy-done.2, f32[2,6,128]{2,1,0:T(8,128)} %fusion.1.slot_ref, s32[1,1]{1,0:T(1,128)} %bitcast.10.count_ref), custom_call_target="tpu_custom_call" | custom-call | tf_op jit(solution)/shard_map/products/pallas_call | solution.py:124
  49.3 3.5 %collective-permute-start.2 = (f32[2,128,128]{2,1,0:T(8,128)}, f32[2,128,128]{2,1,0:T(8,128)S(1)}, u32[]{:S(2)}, u32[]{:S(2)}) collective-permute-start(f32[2,128,128]{2,1,0:T(8,128)} %get-tuple-element.13), channel_id=1, source_target_pairs={{0,1},{1,2},{2,3},{3,4},{4,5},{5,6},{6,7},{7,8},{8,9},{9,10},{10,1... | collective-permute-start | bytes 393224 | tf_op jit(solution)/shard_map/ppermute | solution.py:255
  52.8 2.4 %collective-permute-start.3 = (f32[2,128,128]{2,1,0:T(8,128)}, f32[2,128,128]{2,1,0:T(8,128)S(1)}, u32[]{:S(2)}, u32[]{:S(2)}) collective-permute-start(f32[2,128,128]{2,1,0:T(8,128)} %get-tuple-element.13), channel_id=1, source_target_pairs={{1,0},{2,1},{3,2},{4,3},{5,4},{6,5},{7,6},{8,7},{9,8},{10,9},{11,1... | collective-permute-start | bytes 393224 | tf_op jit(solution)/shard_map/ppermute | solution.py:256
  55.1 0.0 copy-done.13
  55.2 0.2 compare_reduce_fusion
  55.4 0.1 copy.24
  55.5 0.6 copy-done.12
  56.1 0.6 broadcast_in_dim.16
  56.7 7.3 %all-to-all-start.4 = ((f32[16,8,128]{2,1,0:T(8,128)}), f32[16,8,128]{2,1,0:T(8,128)S(1)}, u32[]{:S(2)}, u32[]{:S(2)}) async-start(f32[16,8,128]{2,1,0:T(8,128)} %broadcast_in_dim.16), calls=%async_computation.4 | async-start | bytes 131072 | tf_op jit(solution)/shard_map/all_to_all | solution.py:217
  64.0 0.2 slice_reduce_fusion.2
  64.2 6.1 %all-to-all-done.4 = f32[16,8,128]{2,1,0:T(8,128)S(1)} async-done(((f32[16,8,128]{2,1,0:T(8,128)}), f32[16,8,128]{2,1,0:T(8,128)S(1)}, u32[]{:S(2)}, u32[]{:S(2)}) %all-to-all-start.4) | async-done | bytes 65568 | tf_op jit(solution)/shard_map/all_to_all | solution.py:217
  70.3 0.6 broadcast_in_dim.17
  71.0 9.5 %all-to-all-start.5 = ((f32[16,8,128]{2,1,0:T(8,128)}), f32[16,8,128]{2,1,0:T(8,128)S(1)}, u32[]{:S(2)}, u32[]{:S(2)}) async-start(f32[16,8,128]{2,1,0:T(8,128)} %broadcast_in_dim.17), calls=%async_computation.5 | async-start | bytes 131072 | tf_op jit(solution)/shard_map/all_to_all | solution.py:217
  80.5 0.0 collective-permute-done.2
  80.5 0.0 collective-permute-done.3
  80.5 0.0 copy-done.6
  80.5 0.2 multiply_add_fusion
  80.6 7.7 %all-to-all-done.5.sums_ref = f32[16,8,128]{2,1,0:T(8,128)S(1)} async-done(((f32[16,8,128]{2,1,0:T(8,128)}), f32[16,8,128]{2,1,0:T(8,128)S(1)}, u32[]{:S(2)}, u32[]{:S(2)}) %all-to-all-start.5) | async-done | bytes 65568 | tf_op jit(solution)/shard_map/all_to_all | solution.py:217
  88.3 13.3 %all_to_all.35.part_ref = f32[4,2,128,128]{3,2,1,0:T(8,128)} all-to-all(f32[4,2,128,128]{3,2,1,0:T(8,128)S(1)} %multiply_add_fusion), channel_id=1, replica_groups=mesh['member'=4,'region'=16,'block'=4] {'member'}, dimensions={0} | all-to-all | bytes 1048576 | tf_op jit(solution)/shard_map/all_to_all | solution.py:264
  101.7 0.0 copy-done.5
  101.7 3.5 %all-to-all-start = ((f32[4,32,2048]{2,1,0:T(8,128)}), f32[4,32,2048]{2,1,0:T(8,128)S(1)}, u32[]{:S(2)}, u32[]{:S(2)}) async-start(f32[4,32,2048]{2,1,0:T(8,128)} %get-tuple-element.11), calls=%async_computation | async-start | bytes 2097152 | tf_op jit(solution)/shard_map/all_to_all | solution.py:248
  105.2 12.1 %solve.1 = (f32[128,128]{1,0:T(8,128)}, f32[8,128]{1,0:T(8,128)}) custom-call(f32[4,2,128,128]{3,2,1,0:T(8,128)} %all_to_all.35.part_ref, f32[16,8,128]{2,1,0:T(8,128)} %copy-done.5), custom_call_target="tpu_custom_call" | custom-call | tf_op jit(solution)/shard_map/solve/pallas_call | solution.py:175
  117.3 2.7 %all-to-all-done.fore_ref = f32[4,32,2048]{2,1,0:T(8,128)S(1)} async-done(((f32[4,32,2048]{2,1,0:T(8,128)}), f32[4,32,2048]{2,1,0:T(8,128)S(1)}, u32[]{:S(2)}, u32[]{:S(2)}) %all-to-all-start) | async-done | bytes 1048608 | tf_op jit(solution)/shard_map/all_to_all | solution.py:248
  120.0 1.0 copy-done.1
  120.9 3.3 %analysis.1 = f32[4,32,2048]{2,1,0:T(8,128)} custom-call(f32[4,32,2048]{2,1,0:T(8,128)} %copy-done.1, f32[128,128]{1,0:T(8,128)} %get-tuple-element.15.mixing_ref, f32[8,128]{1,0:T(8,128)} %get-tuple-element.16.scale_ref), custom_call_target="tpu_custom_call" | custom-call | tf_op jit(solution)/shard_map/analysis/pallas_call | solution.py:203
  124.3 17.4 %all_to_all.36 = f32[4,32,2048]{2,1,0:T(8,128)S(1)} all-to-all(f32[4,32,2048]{2,1,0:T(8,128)} %analysis.1), channel_id=1, replica_groups=mesh['member'=4,'region'=16,'block'=4] {'member'}, dimensions={0} | all-to-all | bytes 2097152 | tf_op jit(solution)/shard_map/all_to_all | solution.py:267
  141.6 1.1 copy.28
  (19 shorter events, 0.1 us)
Async XLA Ops:
  0.0 8.0 %copy-start = (f32[32,3072]{1,0:T(8,128)S(1)}, f32[32,3072]{1,0:T(8,128)}, u32[]{:S(2)}) copy-start(f32[32,3072]{1,0:T(8,128)} %param.21) | copy-start | bytes 1179652
  0.0 0.9 copy-start.7
  0.0 0.9 copy-start.8
  0.0 0.9 copy-start.9
  1.1 7.7 %copy-start.4 = (f32[4,8192]{1,0:T(4,128)}, f32[4,8192]{1,0:T(4,128)S(1)}, u32[]{:S(2)}) copy-start(f32[4,8192]{1,0:T(4,128)S(1)} %pad_maximum_fusion.road_ref) | copy-start | bytes 393220
  2.0 12.9 %collective-permute-start.1 = (f32[36,16]{1,0:T(8,128)S(1)}, f32[36,16]{1,0:T(8,128)S(1)}, u32[]{:S(2)}, u32[]{:S(2)}) collective-permute-start(f32[36,16]{1,0:T(8,128)S(1)} %pad_maximum_fusion.2), channel_id=1, source_target_pairs={{1,0},{2,1},{3,2},{4,3},{5,4},{6,5},{7,6},{8,7},{9,8},{10,9},{11,1... | collective-permute-start | bytes 6920 | tf_op jit(solution)/shard_map/ppermute | solution.py:235
  6.1 9.5 %collective-permute-start = (f32[36,16]{1,0:T(8,128)S(1)}, f32[36,16]{1,0:T(8,128)S(1)}, u32[]{:S(2)}, u32[]{:S(2)}) collective-permute-start(f32[36,16]{1,0:T(8,128)S(1)} %pad_maximum_fusion.1), channel_id=1, source_target_pairs={{0,1},{1,2},{2,3},{3,4},{4,5},{5,6},{6,7},{7,8},{8,9},{9,10},{10,1... | collective-permute-start | bytes 6920 | tf_op jit(solution)/shard_map/ppermute | solution.py:234
  8.8 23.6 %all-to-all-start.2 = ((f32[4,6,32,128]{3,2,1,0:T(8,128)}), f32[4,6,32,128]{3,2,1,0:T(8,128)S(1)}, u32[]{:S(2)}, u32[]{:S(2)}) async-start(f32[4,6,32,128]{3,2,1,0:T(8,128)} %bitcast.8), calls=%async_computation.2 | async-start | bytes 786432 | tf_op jit(solution)/shard_map/all_to_all | solution.py:245
  13.5 0.7 copy-start.14
  32.4 0.7 copy-start.2
  32.4 5.5 %copy-start.10 = (f32[3072]{0:T(1024)S(1)}, f32[3072]{0:T(1024)}, u32[]{:S(2)}) copy-start(f32[3072]{0:T(1024)} %param.19) | copy-start | bytes 36868
  33.1 12.2 %all-to-all-start.1 = ((f32[4,6,32,128]{3,2,1,0:T(8,128)}), f32[4,6,32,128]{3,2,1,0:T(8,128)S(1)}, u32[]{:S(2)}, u32[]{:S(2)}) async-start(f32[4,6,32,128]{3,2,1,0:T(8,128)} %bitcast.22), calls=%async_computation.1 | async-start | bytes 786432 | tf_op jit(solution)/shard_map/all_to_all | solution.py:247
  37.9 0.7 copy-start.11
  38.6 0.7 copy-start.15
  45.3 0.8 copy-start.3
  46.1 9.1 %copy-start.13 = (s32[4,3]{1,0:T(4,128)S(1)}, s32[4,3]{1,0:T(4,128)}, u32[]{:S(2)}) copy-start(s32[4,3]{1,0:T(4,128)} %param.22) | copy-start | bytes 148
  49.3 31.2 %collective-permute-start.2 = (f32[2,128,128]{2,1,0:T(8,128)}, f32[2,128,128]{2,1,0:T(8,128)S(1)}, u32[]{:S(2)}, u32[]{:S(2)}) collective-permute-start(f32[2,128,128]{2,1,0:T(8,128)} %get-tuple-element.13), channel_id=1, source_target_pairs={{0,1},{1,2},{2,3},{3,4},{4,5},{5,6},{6,7},{7,8},{8,9},{9,10},{10,1... | collective-permute-start | bytes 393224 | tf_op jit(solution)/shard_map/ppermute | solution.py:255
  52.8 27.7 %collective-permute-start.3 = (f32[2,128,128]{2,1,0:T(8,128)}, f32[2,128,128]{2,1,0:T(8,128)S(1)}, u32[]{:S(2)}, u32[]{:S(2)}) collective-permute-start(f32[2,128,128]{2,1,0:T(8,128)} %get-tuple-element.13), channel_id=1, source_target_pairs={{1,0},{2,1},{3,2},{4,3},{5,4},{6,5},{7,6},{8,7},{9,8},{10,9},{11,1... | collective-permute-start | bytes 393224 | tf_op jit(solution)/shard_map/ppermute | solution.py:256
  55.4 0.7 copy-start.12
  56.7 13.6 %all-to-all-start.4 = ((f32[16,8,128]{2,1,0:T(8,128)}), f32[16,8,128]{2,1,0:T(8,128)S(1)}, u32[]{:S(2)}, u32[]{:S(2)}) async-start(f32[16,8,128]{2,1,0:T(8,128)} %broadcast_in_dim.16), calls=%async_computation.4 | async-start | bytes 131072 | tf_op jit(solution)/shard_map/all_to_all | solution.py:217
  64.2 16.3 %copy-start.6 = (f32[2,128,128]{2,1,0:T(8,128)S(1)}, f32[2,128,128]{2,1,0:T(8,128)}, u32[]{:S(2)}) copy-start(f32[2,128,128]{2,1,0:T(8,128)} %get-tuple-element.13) | copy-start | bytes 393220
  71.0 17.4 %all-to-all-start.5 = ((f32[16,8,128]{2,1,0:T(8,128)}), f32[16,8,128]{2,1,0:T(8,128)S(1)}, u32[]{:S(2)}, u32[]{:S(2)}) async-start(f32[16,8,128]{2,1,0:T(8,128)} %broadcast_in_dim.17), calls=%async_computation.5 | async-start | bytes 131072 | tf_op jit(solution)/shard_map/all_to_all | solution.py:217
  88.3 13.3 %copy-start.5 = (f32[16,8,128]{2,1,0:T(8,128)}, f32[16,8,128]{2,1,0:T(8,128)S(1)}, u32[]{:S(2)}) copy-start(f32[16,8,128]{2,1,0:T(8,128)S(1)} %all-to-all-done.5.sums_ref) | copy-start | bytes 196612
  101.7 18.3 %all-to-all-start = ((f32[4,32,2048]{2,1,0:T(8,128)}), f32[4,32,2048]{2,1,0:T(8,128)S(1)}, u32[]{:S(2)}, u32[]{:S(2)}) async-start(f32[4,32,2048]{2,1,0:T(8,128)} %get-tuple-element.11), calls=%async_computation | async-start | bytes 2097152 | tf_op jit(solution)/shard_map/all_to_all | solution.py:248
  120.0 1.0 copy-start.1

commit v2 on v1

v2 whole, which is shorter than its diff:
```python
import jax
import jax.numpy as jnp
from jax import lax
from jax.experimental import pallas as pl
from jax.experimental.pallas import tpu as pltpu
from jax.sharding import PartitionSpec as P

TALLY = 128
TICKS = 16
CELLS = 2048
SLOTS = 768
LANES = 128
GROUP = 4
PER_BLOCK = SLOTS // LANES
RB = ("region", "block")
ALL = ("member", "region", "block")
HIGHEST = lax.Precision.HIGHEST
VMEM = pl.BlockSpec(memory_space=pltpu.VMEM)
SMEM = pl.BlockSpec(memory_space=pltpu.SMEM)
HBM = pl.BlockSpec(memory_space=pltpu.HBM)


def room(mib):
    return pltpu.CompilerParams(vmem_limit_bytes=mib << 20)


PAIR = jax.ShapeDtypeStruct((2, TALLY, TALLY), jnp.float32)


def road_capacity(free_speed, wave_speed, jam_density, capacity_share):
    return capacity_share * free_speed * wave_speed * jam_density / (free_speed + wave_speed)


def edges_kernel(place_ref, state_ref, speed_ref, wave_ref, jam_ref, share_ref, noise_ref, *refs):
    last_ref, first_ref = refs[:2]
    noise_refs = refs[2 : 2 + GROUP]
    tile_refs = refs[2 + GROUP : 4 + GROUP]
    sem_ref = refs[4 + GROUP]
    rows, width = state_ref.shape
    member = place_ref[0]
    copies = []
    for side, tile_ref in enumerate(tile_refs):
        at = pl.ds((1 - side) * (width - LANES), LANES)
        copies.append(pltpu.make_async_copy(state_ref.at[:, at], tile_ref.at[pl.ds(0, rows), :], sem_ref.at[side]))
        for i, road_ref in enumerate((speed_ref, wave_ref, jam_ref, share_ref)):
            copies.append(
                pltpu.make_async_copy(
                    road_ref.at[:, at], tile_ref.at[pl.ds(rows + i, 1), :], sem_ref.at[2 + 4 * side + i]
                )
            )
    for d in range(GROUP):
        at = pl.ds(pl.multiple_of(lax.rem(member + d, GROUP) * SLOTS, LANES), SLOTS)
        copies.append(pltpu.make_async_copy(noise_ref.at[:, at], noise_refs[d], sem_ref.at[10 + d]))
    for copy in copies:
        copy.start()
    for copy in copies:
        copy.wait()
    last_ref[...] = tile_refs[0][:, LANES - TICKS :]
    first_ref[...] = tile_refs[1][:, :TICKS]


def edges(place, state, road, noise):
    rows = state.shape[0]
    edge = jax.ShapeDtypeStruct((rows + 4, TICKS), jnp.float32)
    piece = jax.ShapeDtypeStruct((rows, SLOTS), jnp.float32)
    return pl.pallas_call(
        edges_kernel,
        out_shape=(edge,) * 2 + (piece,) * GROUP,
        in_specs=[SMEM] + [HBM] * 6,
        out_specs=(VMEM,) * (2 + GROUP),
        scratch_shapes=[pltpu.VMEM((rows + 4, LANES), jnp.float32)] * 2 + [pltpu.SemaphoreType.DMA((10 + GROUP,))],
        compiler_params=room(4),
        name="edges",
    )(place, state, *road, noise)


def forecast_kernel(
    place_ref, state_ref, low_ref, high_ref, speed_ref, wave_ref, jam_ref, share_ref, cells_ref, *refs
):
    fore_refs, obs_refs = refs[:GROUP], refs[GROUP : 2 * GROUP]
    wide_ref, other_ref, side_ref, share_at, cell_ref, sem_ref = refs[2 * GROUP :]
    rows, width = state_ref.shape
    full = width + 2 * LANES
    main = slice(LANES, LANES + width)
    inner = pl.ds(LANES, width)
    roads = [
        pltpu.make_async_copy(ref, side_ref.at[pl.ds(i, 1), inner], sem_ref.at[i])
        for i, ref in enumerate((speed_ref, wave_ref, jam_ref))
    ]
    roads.append(pltpu.make_async_copy(share_ref, share_at, sem_ref.at[3]))
    arrive = pltpu.make_async_copy(state_ref, wide_ref.at[:, inner], sem_ref.at[4])
    fetch = pltpu.make_async_copy(cells_ref, cell_ref, sem_ref.at[5])
    for copy in roads + [arrive, fetch]:
        copy.start()
    member = place_ref[0]
    slab = place_ref[1]
    is_first = slab == 0
    is_last = slab == place_ref[2] - 1
    for copy in roads:
        copy.wait()
    capacity = road_capacity(side_ref[0:1, main], side_ref[1:2, main], side_ref[2:3, main], share_at[...])
    side_ref[3:4, main] = capacity
    edge = jnp.zeros((rows + 4, LANES - TICKS), jnp.float32)
    low = jnp.concatenate([edge, low_ref[...]], axis=1)
    high = jnp.concatenate([high_ref[...], edge], axis=1)
    wide_ref[:, :LANES] = low[:rows]
    wide_ref[:, LANES + width :] = high[:rows]
    lane = lax.broadcasted_iota(jnp.int32, (1, LANES), 1)
    for piece, at, inside, beyond in (
        (low, slice(0, LANES), lane >= LANES - TICKS, is_first),
        (high, slice(LANES + width, full), lane < TICKS, is_last),
    ):
        inside = inside & jnp.logical_not(beyond)
        s, w, j, c = [piece[rows + i : rows + i + 1] for i in range(4)]
        s = jnp.where(inside, s, 1.0)
        w = jnp.where(inside, w, 1.0)
        j = jnp.where(inside, j, 1.0)
        c = jnp.where(inside, c, 0.0)
        side_ref[0:1, at] = s
        side_ref[1:2, at] = w
        side_ref[2:3, at] = j
        side_ref[3:4, at] = road_capacity(s, w, j, c)

    @pl.when(is_last)
    def _():
        at = slice(LANES + width, full)
        side_ref[0:1, at] = jnp.zeros((1, LANES), jnp.float32)
        side_ref[2:3, at] = jnp.full((1, LANES), 1000.0, jnp.float32)
        side_ref[3:4, at] = jnp.broadcast_to(capacity[:, width - 1 :], (1, LANES))

    arrive.wait()

    def half(src, dst):
        for g in range(rows // 8):
            at = slice(8 * g, 8 * g + 8)
            x = src[at, :]
            cap = side_ref[3:4, :]
            demand = jnp.minimum(side_ref[0:1, :] * x, cap)
            supply = jnp.minimum(cap, side_ref[1:2, :] * (side_ref[2:3, :] - x))
            flux = jnp.minimum(demand, pltpu.roll(supply, full - 1, 1))
            dst[at, :] = x + pltpu.roll(flux, 1, 1) - flux

    def step(_, carry):
        half(wide_ref, other_ref)
        half(other_ref, wide_ref)
        return carry

    lax.fori_loop(0, TICKS // 2, step, 0)
    starts = [pl.multiple_of(LANES + lax.rem(member + d, GROUP) * CELLS, LANES) for d in range(GROUP)]
    leave = [
        pltpu.make_async_copy(wide_ref.at[:, pl.ds(starts[d], CELLS)], fore_refs[d], sem_ref.at[6 + d])
        for d in range(GROUP)
    ]
    for copy in leave:
        copy.start()
    fetch.wait()
    for d, obs_ref in enumerate(obs_refs):
        b = lax.rem(member + d, GROUP)
        start = starts[d]

        def gather(q, carry):
            cells = cell_ref[pl.ds(b * PER_BLOCK + q, 1), :]
            at_lane = jnp.broadcast_to(cells & (LANES - 1), (8, LANES))
            tile = jnp.broadcast_to(cells >> 7, (8, LANES))
            acc = [jnp.zeros((8, LANES), jnp.float32) for _ in range(rows // 8)]
            for c in range(CELLS // LANES):
                hit = tile == c
                for g in range(rows // 8):
                    piece = wide_ref[8 * g : 8 * g + 8, pl.ds(start + c * LANES, LANES)]
                    acc[g] = jnp.where(hit, jnp.take_along_axis(piece, at_lane, axis=1), acc[g])
            for g in range(rows // 8):
                obs_ref[q, 8 * g : 8 * g + 8, :] = acc[g]
            return carry

        lax.fori_loop(0, PER_BLOCK, gather, 0, unroll=True)
    for copy in leave:
        copy.wait()


def forecast(place, state, low, high, road, cells):
    rows, width = state.shape
    piece = jax.ShapeDtypeStruct((PER_BLOCK, rows, LANES), jnp.float32)
    return pl.pallas_call(
        forecast_kernel,
        out_shape=(jax.ShapeDtypeStruct((rows, CELLS), jnp.float32),) * GROUP + (piece,) * GROUP,
        in_specs=[SMEM, HBM, VMEM, VMEM] + [HBM] * 5,
        out_specs=(HBM,) * GROUP + (VMEM,) * GROUP,
        scratch_shapes=[
            pltpu.VMEM((rows, width + 2 * LANES), jnp.float32),
            pltpu.VMEM((rows, width + 2 * LANES), jnp.float32),
            pltpu.VMEM((8, width + 2 * LANES), jnp.float32),
            pltpu.VMEM((1, width), jnp.float32),
            pltpu.VMEM(cells.shape, jnp.int32),
            pltpu.SemaphoreType.DMA((6 + GROUP,)),
        ],
        compiler_params=room(12),
        name="forecast",
    )(place, state, low, high, *road, cells)


def products_kernel(*refs):
    place_ref, counts_ref = refs[:2]
    obs_refs, noise_refs = refs[2 : 2 + GROUP], refs[2 + GROUP : 2 + 2 * GROUP]
    value_ref, variance_ref, pair_ref, sum_ref, obs_ref, noise_ref, count_ref, sem_ref = refs[2 + 2 * GROUP :]
    fetch = pltpu.make_async_copy(counts_ref, count_ref, sem_ref.at[0])
    fetch.start()
    member = place_ref[0]
    rows = noise_refs[0].shape[0]
    for d in range(GROUP):
        at = pl.multiple_of(lax.rem(member - d + GROUP, GROUP) * rows, rows)
        for q in range(PER_BLOCK):
            obs_ref[pl.ds(at, rows), q * LANES : (q + 1) * LANES] = obs_refs[d][q]
        noise_ref[pl.ds(at, rows), :] = noise_refs[d][...]
    fetch.wait()
    count = count_ref[member]
    total_a = jnp.zeros((1, LANES), jnp.float32)
    total_b = jnp.zeros((1, LANES), jnp.float32)
    scaled, plain, moved = [], [], []
    for q in range(PER_BLOCK):
        at = slice(q * LANES, (q + 1) * LANES)
        x = obs_ref[:, at]
        value = value_ref[pl.ds(member * PER_BLOCK + q, 1), :]
        variance = variance_ref[pl.ds(member * PER_BLOCK + q, 1), :]
        mean = jnp.sum(x, axis=0, keepdims=True) / TALLY
        a = x - mean
        slot = lax.broadcasted_iota(jnp.int32, (1, LANES), 1) + q * LANES
        live = (slot < count).astype(jnp.float32)
        weight = live / variance
        misfit = value - mean
        spread = jnp.sum(a * a, axis=0, keepdims=True) / (TALLY - 1)
        total_a += misfit * misfit * weight
        total_b += live * (spread / variance + 1.0)
        scaled.append(a * weight)
        plain.append(a)
        moved.append(misfit + jnp.sqrt(variance) * noise_ref[:, at])
    left = jnp.concatenate(scaled, axis=1)
    right = jnp.concatenate([jnp.concatenate(plain, axis=1), jnp.concatenate(moved, axis=1)], axis=0)
    dims = (((1,), (1,)), ((), ()))
    both = lax.dot_general(left, right, dims, precision=HIGHEST, preferred_element_type=jnp.float32)
    pair_ref[0] = both[:, :TALLY]
    pair_ref[1] = both[:, TALLY:]
    lane = lax.broadcasted_iota(jnp.int32, (1, LANES), 1)
    sum_a = jnp.sum(total_a, axis=1, keepdims=True)
    sum_b = jnp.sum(total_b, axis=1, keepdims=True)
    sums = jnp.where(lane == 0, sum_a, jnp.where(lane == 1, sum_b, 0.0))
    sum_ref[...] = jnp.broadcast_to(sums[None], sum_ref.shape)


def products(place, count, obs, noise, value, variance, devices):
    rows = noise[0].shape[0]
    return pl.pallas_call(
        products_kernel,
        out_shape=(PAIR, jax.ShapeDtypeStruct((devices, 1, LANES), jnp.float32)),
        in_specs=[SMEM, HBM] + [VMEM] * (2 * GROUP + 2),
        out_specs=(VMEM, VMEM),
        scratch_shapes=[pltpu.VMEM((GROUP * rows, SLOTS), jnp.float32)] * 2
        + [pltpu.SMEM((GROUP,), jnp.int32), pltpu.SemaphoreType.DMA((1,))],
        compiler_params=room(6),
        name="products",
    )(place, count, *obs, *noise, value, variance)


def select_kernel(place_ref, list_ref, below_ref, pair_ref, above_ref, *out_refs):
    member = place_ref[0]
    slab = place_ref[1]
    for d in range(GROUP):
        target = lax.rem(member + d, GROUP)
        total = None
        for step, ref in ((0, pair_ref), (-1, below_ref), (1, above_ref)):
            name = (slab + step) * GROUP + member
            listed = (list_ref[target, 0] == name) | (list_ref[target, 1] == name) | (list_ref[target, 2] == name)
            share = jnp.where(listed, jnp.float32(1.0), jnp.float32(0.0)) * ref[...]
            total = share if total is None else total + share
        out_refs[d][...] = total


def select(place, lists, below, pair, above):
    return pl.pallas_call(
        select_kernel,
        out_shape=(PAIR,) * GROUP,
        in_specs=[SMEM, SMEM] + [VMEM] * 3,
        out_specs=(VMEM,) * GROUP,
        compiler_params=room(6),
        name="select",
    )(place, lists, below, pair, above)


def update_kernel(place_ref, part0_ref, part1_ref, part2_ref, part3_ref, sums_ref, *refs):
    fore_refs = refs[:GROUP]
    out_ref, state_ref, sem_ref = refs[GROUP:]
    rows = fore_refs[0].shape[0]
    member = place_ref[0]
    arrive = []
    for d in range(GROUP):
        at = pl.multiple_of(lax.rem(member - d + GROUP, GROUP) * rows, rows)
        arrive.append(pltpu.make_async_copy(fore_refs[d], state_ref.at[pl.ds(at, rows), :], sem_ref.at[d]))
    for copy in arrive:
        copy.start()
    sums = jnp.sum(sums_ref[...], axis=0, keepdims=True)
    scale = jnp.sqrt(sums[:, 0:1] / sums[:, 1:2])
    gram = (part0_ref[0] + part1_ref[0]) + (part2_ref[0] + part3_ref[0])
    cross = (part0_ref[1] + part1_ref[1]) + (part2_ref[1] + part3_ref[1])
    row = lax.broadcasted_iota(jnp.int32, (TALLY, TALLY), 0)
    lane = lax.broadcasted_iota(jnp.int32, (TALLY, TALLY), 1)
    eye = jnp.where(row == lane, jnp.float32(TALLY - 1), jnp.float32(0.0))
    both = jnp.concatenate([eye + (scale * scale) * gram, eye + scale * cross], axis=1)
    tiles = [both[8 * i : 8 * i + 8, :] for i in range(TALLY // 8)]
    sub = lax.broadcasted_iota(jnp.int32, (8, 2 * TALLY), 0)
    for k in range(TALLY // 8):
        panel = tiles[k]
        for j in range(8):
            at = 8 * k + j
            column = panel[:, at : at + 1]
            pivot_row = panel[j : j + 1, :]
            inverse = 1.0 / panel[j : j + 1, at : at + 1]
            pivot_row = pivot_row * inverse
            panel = jnp.where(sub == j, pivot_row, panel - column * pivot_row)
        for i in range(TALLY // 8):
            if i != k:
                tile = tiles[i]
                new = tile
                for j in range(8):
                    new = new - tile[:, 8 * k + j : 8 * k + j + 1] * panel[j : j + 1, :]
                tiles[i] = new
        tiles[k] = panel
    mixing = jnp.concatenate([tile[:, TALLY:] for tile in tiles], axis=0) * scale
    for copy in arrive:
        copy.wait()
    state = state_ref[...]
    mean = jnp.sum(state, axis=0, keepdims=True) / TALLY
    anomaly = state - mean
    dims = (((0,), (0,)), ((), ()))
    out = mean + lax.dot_general(mixing, anomaly, dims, precision=HIGHEST, preferred_element_type=jnp.float32)
    for m in range(GROUP):
        out_ref[m] = out[m * rows : (m + 1) * rows, :]


def update(place, parts, sums, fore):
    return pl.pallas_call(
        update_kernel,
        out_shape=jax.ShapeDtypeStruct((GROUP,) + fore[0].shape, jnp.float32),
        in_specs=[SMEM] + [VMEM] * 5 + [HBM] * GROUP,
        out_specs=VMEM,
        scratch_shapes=[pltpu.VMEM((TALLY, CELLS), jnp.float32), pltpu.SemaphoreType.DMA((GROUP,))],
        compiler_params=room(10),
        name="update",
    )(place, *parts, sums, *fore)


def hold(value):
    return pltpu.with_memory_space_constraint(value, pltpu.HBM)


def exchange(pieces):
    moved = {
        d: lax.ppermute(pieces[d], "member", [(i, (i + d) % GROUP) for i in range(GROUP)]) for d in (2, 1, 3)
    }
    return [pieces[0], moved[1], moved[2], moved[3]]


def body(load, free_speed, wave_speed, jam_density, capacity_share, cell, count, value, variance, noise, lists):
    rows, width = load.shape
    member = lax.axis_index("member")
    slab = lax.axis_index(RB)
    slabs = lax.axis_size(RB)
    up = [(i, i + 1) for i in range(slabs - 1)]
    down = [(b, a) for a, b in up]
    place = jnp.stack([member, slab, jnp.int32(slabs)]).astype(jnp.int32)

    road = [hold(v.reshape(1, width)) for v in (free_speed, wave_speed, jam_density, capacity_share)]
    load, noise, count, cells = [hold(v) for v in (load, noise, count, cell.reshape(-1, LANES))]
    last, first, *noises = edges(place, load, road, noise)
    low = lax.ppermute(last, RB, up)
    high = lax.ppermute(first, RB, down)
    out = forecast(place, load, low, high, road, cells)
    fore, obs = out[:GROUP], out[GROUP:]
    obs = exchange(obs)
    noises = exchange(noises)
    fore = exchange(fore)

    pair, sums = products(
        place, count, obs, noises, value.reshape(-1, LANES), variance.reshape(-1, LANES), GROUP * slabs
    )
    below = lax.ppermute(pair, RB, up)
    above = lax.ppermute(pair, RB, down)
    below, above, sums = lax.optimization_barrier((below, above, sums))
    sums = lax.all_to_all(sums, ALL, 0, 0).reshape(GROUP * slabs, LANES)
    parts = exchange(select(place, lists, below, pair, above))
    out = update(place, parts, sums, fore)
    out = lax.all_to_all(out, "member", 0, 0)
    return out.transpose(1, 0, 2).reshape(rows, width)


def solution(mesh):
    slab = P(RB)
    in_specs = (P("member", RB),) + (slab,) * 8 + (P("member", RB), P(RB, None))
    return jax.shard_map(body, mesh=mesh, in_specs=in_specs, out_specs=P("member", RB), check_vma=False)
```

time: 144 us -> 110 us (0.76)
  blocking collectives: 30.7 us -> 18.2 us
  waiting for transfers between devices: 21.3 us -> 9.81 us
  local copies, waits for them, and re-layouts: 11.8 us -> 1.08 us
  starting transfers between devices: 41.1 us -> 48.8 us
  Pallas kernels: 34.8 us -> 31.7 us
  other arithmetic: 2.8 us -> 0.08 us
    all_to_all x5 -> x1, waiting for transfers between devices: 21.3 us -> 0.01 us  [body(): sums = lax.all_to_all(sums, ALL, 0, 0).reshape(GROUP * slabs, LANES)]
    ppermute x2 -> x14, starting transfers between devices: 6 us -> 25.9 us  [the longest x12 20 us: exchange(): lax.ppermute(pieces[d], 'member', [(i, (i + d) % GROUP) for i in range(GR...]
    all_to_all x1 -> x0, blocking collectives: 13.3 us -> none  [body(): parts = lax.all_to_all(parts, 'member', 0, 0)]
    all_to_all x5 -> x1, starting transfers between devices: 29.2 us -> 17.1 us  [body(): sums = lax.all_to_all(sums, ALL, 0, 0).reshape(GROUP * slabs, LANES)]
    ppermute x2 -> x14, waiting for transfers between devices: 0.01 us -> 9.17 us  [the longest x12 9.17 us: exchange(): lax.ppermute(pieces[d], 'member', [(i, (i + d) % GROUP) for i in range(GR...]
    unnamed x32 -> x6, local copies, waits for them, and re-layouts: 5.08 us -> 0.01 us
    pallas_call x4 -> x5, Pallas kernels: 34.8 us -> 31.7 us  [the longest x1 14 us: forecast(): pl.pallas_call(forecast_kernel, out_shape=(jax.ShapeDtypeStruct((rows, CE...]
    slice x4 -> x0, local copies, waits for them, and re-layouts: 1.64 us -> none  [the longest x2 0.88 us: body(): edge_first = jnp.concatenate([load[:, :TICKS], road[:, :TICKS]], axis=0)]
  transfers between devices with their start and end apart: 9 -> 17, of which waited for: 4 -> 5; matrix products, arithmetic and copies ran while one was open for 5% -> 0% of each run, Pallas kernels for 20% -> 16%
where the time goes in v2:
time: 110 us
  starting transfers between devices  48.8 us (44%)
  Pallas kernels  31.7 us (29%)
  blocking collectives  18.2 us (17%)
  waiting for transfers between devices  9.81 us (9%)
    ppermute x12, starting transfers between devices, exchange(): lax.ppermute(pieces[d], 'member', [(i, (i + d) % GROUP) for i in range(GR...  20 us
    all_to_all x1, blocking collectives, body(): out = lax.all_to_all(out, 'member', 0, 0)  18.2 us
    all_to_all x1, starting transfers between devices, body(): sums = lax.all_to_all(sums, ALL, 0, 0).reshape(GROUP * slabs, LANES)  17.1 us
    pallas_call x1, Pallas kernels, forecast(): pl.pallas_call(forecast_kernel, out_shape=(jax.ShapeDtypeStruct((rows, CE...  14 us
    pallas_call x1, Pallas kernels, update(): pl.pallas_call(update_kernel, out_shape=jax.ShapeDtypeStruct((GROUP,) + f...  12.3 us
    ppermute x12, waiting for transfers between devices, exchange(): lax.ppermute(pieces[d], 'member', [(i, (i + d) % GROUP) for i in range(GR...  9.17 us
    ppermute x1, starting transfers between devices, body(): low = lax.ppermute(last, RB, up)  3.47 us
    ppermute x1, starting transfers between devices, body(): above = lax.ppermute(pair, RB, down)  3.22 us
  transfers between devices with their start and end apart: 17, of which 5 were waited for; matrix products, arithmetic and copies ran while one was open for 0% of the time, Pallas kernels for 16%

profile of v2, /device:TPU:8, one launch (start us, length us, event | category | flops | bytes accessed | tf_op | source)
XLA Modules:
  0.0 109.8 jit_solution(9326688737656118525)
XLA Ops:
  0.0 0.1 pad_add_fusion.place_ref.refs_0_
  0.1 1.9 %edges.1 = (f32[36,16]{1,0:T(8,128)S(1)}, f32[36,16]{1,0:T(8,128)S(1)}, f32[32,768]{1,0:T(8,128)S(1)}, f32[32,768]{1,0:T(8,128)S(1)}, f32[32,768]{1,0:T(8,128)S(1)}, /*index=5*/f32[32,768]{1,0:T(8,128)S(1)}) custom-call(s32[3]{0:T(128)S(1)} %pad_add_fusion.place_ref.refs_0_, f32[32,8192]{1,0:T(8,128)} %state_ref.3, f32[1,8192]{1,0:T(1,128)} %bitcast.17, ...), custom_call_target="tpu_custom_call" | custom-call | tf_op jit(solution)/shard_map/edges/pallas_call | solution.py:66
  2.0 1.6 %collective-permute-start.5 = (f32[32,768]{1,0:T(8,128)S(1)}, f32[32,768]{1,0:T(8,128)S(1)}, u32[]{:S(2)}, u32[]{:S(2)}) collective-permute-start(f32[32,768]{1,0:T(8,128)S(1)} %get-tuple-element.35), channel_id=1, source_target_pairs={{0,64},{64,128},{128,192},{192,0},{1,65},{65,129},{129,193},{193,1... | collective-permute-start | bytes 294920 | tf_op jit(solution)/shard_map/ppermute | solution.py:356
  3.6 3.5 %collective-permute-start = (f32[36,16]{1,0:T(8,128)S(1)}, f32[36,16]{1,0:T(8,128)S(1)}, u32[]{:S(2)}, u32[]{:S(2)}) collective-permute-start(f32[36,16]{1,0:T(8,128)S(1)} %get-tuple-element.28), channel_id=1, source_target_pairs={{0,1},{1,2},{2,3},{3,4},{4,5},{5,6},{6,7},{7,8},{8,9},{9,10},{10,1... | collective-permute-start | bytes 6920 | tf_op jit(solution)/shard_map/ppermute | solution.py:373
  7.0 2.4 %collective-permute-start.1 = (f32[36,16]{1,0:T(8,128)S(1)}, f32[36,16]{1,0:T(8,128)S(1)}, u32[]{:S(2)}, u32[]{:S(2)}) collective-permute-start(f32[36,16]{1,0:T(8,128)S(1)} %get-tuple-element.29), channel_id=1, source_target_pairs={{1,0},{2,1},{3,2},{4,3},{5,4},{6,5},{7,6},{8,7},{9,8},{10,9},{11,1... | collective-permute-start | bytes 6920 | tf_op jit(solution)/shard_map/ppermute | solution.py:374
  9.4 2.8 %collective-permute-start.6 = (f32[32,768]{1,0:T(8,128)S(1)}, f32[32,768]{1,0:T(8,128)S(1)}, u32[]{:S(2)}, u32[]{:S(2)}) collective-permute-start(f32[32,768]{1,0:T(8,128)S(1)} %get-tuple-element.36), channel_id=1, source_target_pairs={{0,128},{64,192},{128,0},{192,64},{1,129},{65,193},{129,1},{193,65... | collective-permute-start | bytes 294920 | tf_op jit(solution)/shard_map/ppermute | solution.py:356
  12.2 1.4 %collective-permute-start.7 = (f32[32,768]{1,0:T(8,128)S(1)}, f32[32,768]{1,0:T(8,128)S(1)}, u32[]{:S(2)}, u32[]{:S(2)}) collective-permute-start(f32[32,768]{1,0:T(8,128)S(1)} %get-tuple-element.37), channel_id=1, source_target_pairs={{0,192},{64,0},{128,64},{192,128},{1,193},{65,1},{129,65},{193,129... | collective-permute-start | bytes 294920 | tf_op jit(solution)/shard_map/ppermute | solution.py:356
  13.7 0.0 collective-permute-done.low_ref
  13.7 0.0 collective-permute-done.1.high_ref
  13.7 0.0 copy-start.1
  13.7 14.0 %forecast.1 = (f32[32,2048]{1,0:T(8,128)S(1)}, f32[32,2048]{1,0:T(8,128)S(1)}, f32[32,2048]{1,0:T(8,128)S(1)}, f32[32,2048]{1,0:T(8,128)S(1)}, f32[6,32,128]{2,1...) custom-call(s32[3]{0:T(128)S(1)} %pad_add_fusion.place_ref.refs_0_, ...), custom_call_target="tpu_custom_call" | custom-call | tf_op jit(solution)/shard_map/forecast/pallas_call | solution.py:183
  27.7 0.0 copy-start
  27.7 0.7 collective-permute-start.2
  28.4 1.7 %collective-permute-start.3 = (f32[6,32,128]{2,1,0:T(8,128)S(1)}, f32[6,32,128]{2,1,0:T(8,128)S(1)}, u32[]{:S(2)}, u32[]{:S(2)}) collective-permute-start(f32[6,32,128]{2,1,0:T(8,128)S(1)} %get-tuple-element.32), channel_id=1, source_target_pairs={{0,128},{64,192},{128,0},{192,64},{1,129},{65,193},{129,1},{193,65... | collective-permute-start | bytes 294920 | tf_op jit(solution)/shard_map/ppermute | solution.py:356
  30.0 0.0 collective-permute-done.5.refs_7_
  30.0 2.2 %collective-permute-start.4 = (f32[6,32,128]{2,1,0:T(8,128)S(1)}, f32[6,32,128]{2,1,0:T(8,128)S(1)}, u32[]{:S(2)}, u32[]{:S(2)}) collective-permute-start(f32[6,32,128]{2,1,0:T(8,128)S(1)} %get-tuple-element.33), channel_id=1, source_target_pairs={{0,192},{64,0},{128,64},{192,128},{1,193},{65,1},{129,65},{193,129... | collective-permute-start | bytes 294920 | tf_op jit(solution)/shard_map/ppermute | solution.py:356
  32.2 0.0 collective-permute-done.6.refs_8_
  32.2 0.0 collective-permute-start.13
  32.2 0.0 collective-permute-done.7.refs_9_
  32.2 2.3 %collective-permute-done.2.refs_3_ = f32[6,32,128]{2,1,0:T(8,128)S(1)} collective-permute-done((f32[6,32,128]{2,1,0:T(8,128)S(1)}, f32[6,32,128]{2,1,0:T(8,128)S(1)}, u32[]{:S(2)}, u32[]{:S(2)}) %collective-permute-start.2) | collective-permute-done | bytes 98336 | tf_op jit(solution)/shard_map/ppermute | solution.py:356
  34.5 1.1 collective-permute-done.3.refs_4_
  35.6 0.0 collective-permute-done.4.refs_5_
  35.6 0.0 copy-done.1
  35.6 0.0 copy-done
  35.6 2.8 %products.1 = (f32[2,128,128]{2,1,0:T(8,128)S(1)}, f32[256,1,128]{2,1,0:T(1,128)}) custom-call(s32[3]{0:T(128)S(1)} %pad_add_fusion.place_ref.refs_0_, s32[4]{0:T(128)} %refs_1_.1, f32[6,32,128]{2,1,0:T(8,128)S(1)} %get-tuple-element.30.refs_2_, f32[6,32,128]{2,1,0:T(8,128)S(1)} %collective-permute-done.2.refs_3_, ...), custom_call_target="tpu_custom_call" | custom-call | tf_op jit(solution)/shard_map/products/pallas_call | solution.py:251
  38.4 3.2 %collective-permute-start.9 = (f32[2,128,128]{2,1,0:T(8,128)S(1)}, f32[2,128,128]{2,1,0:T(8,128)S(1)}, u32[]{:S(2)}, u32[]{:S(2)}) collective-permute-start(f32[2,128,128]{2,1,0:T(8,128)S(1)} %get-tuple-element.38.pair_ref), channel_id=1, source_target_pairs={{1,0},{2,1},{3,2},{4,3},{5,4},{6,5},{7,6},{8,7},{9,8},{10,9},{11,1... | collective-permute-start | bytes 393224 | tf_op jit(solution)/shard_map/ppermute | solution.py:385
  41.6 2.6 %collective-permute-start.8 = (f32[2,128,128]{2,1,0:T(8,128)S(1)}, f32[2,128,128]{2,1,0:T(8,128)S(1)}, u32[]{:S(2)}, u32[]{:S(2)}) collective-permute-start(f32[2,128,128]{2,1,0:T(8,128)S(1)} %get-tuple-element.38.pair_ref), channel_id=1, source_target_pairs={{0,1},{1,2},{2,3},{3,4},{4,5},{5,6},{6,7},{7,8},{8,9},{9,10},{10,1... | collective-permute-start | bytes 393224 | tf_op jit(solution)/shard_map/ppermute | solution.py:384
  44.3 1.8 %collective-permute-start.14 = (f32[32,2048]{1,0:T(8,128)S(1)}, f32[32,2048]{1,0:T(8,128)S(1)}, u32[]{:S(2)}, u32[]{:S(2)}) collective-permute-start(f32[32,2048]{1,0:T(8,128)S(1)} %get-tuple-element.49), channel_id=1, source_target_pairs={{0,128},{64,192},{128,0},{192,64},{1,129},{65,193},{129,1},{193,65... | collective-permute-start | bytes 786440 | tf_op jit(solution)/shard_map/ppermute | solution.py:356
  46.1 2.1 %collective-permute-start.15 = (f32[32,2048]{1,0:T(8,128)S(1)}, f32[32,2048]{1,0:T(8,128)S(1)}, u32[]{:S(2)}, u32[]{:S(2)}) collective-permute-start(f32[32,2048]{1,0:T(8,128)S(1)} %get-tuple-element.50), channel_id=1, source_target_pairs={{0,192},{64,0},{128,64},{192,128},{1,193},{65,1},{129,65},{193,129... | collective-permute-start | bytes 786440 | tf_op jit(solution)/shard_map/ppermute | solution.py:356
  48.1 0.0 collective-permute-done.9.above_ref
  48.1 0.6 collective-permute-done.8.below_ref
  48.8 0.0 copy-start.2
  48.8 17.1 %all-to-all-start = ((f32[256,1,128]{2,1,0:T(1,128)}), f32[256,1,128]{2,1,0:T(1,128)S(1)}, u32[]{:S(2)}, u32[]{:S(2)}) async-start(f32[256,1,128]{2,1,0:T(1,128)} %get-tuple-element.46), calls=%async_computation | async-start | bytes 262144 | tf_op jit(solution)/shard_map/all_to_all | solution.py:387
  65.9 0.0 copy-done.2
  65.9 0.7 select.1
  66.6 1.7 %collective-permute-start.10 = (f32[2,128,128]{2,1,0:T(8,128)S(1)}, f32[2,128,128]{2,1,0:T(8,128)S(1)}, u32[]{:S(2)}, u32[]{:S(2)}) collective-permute-start(f32[2,128,128]{2,1,0:T(8,128)S(1)} %get-tuple-element.43), channel_id=1, source_target_pairs={{0,64},{64,128},{128,192},{192,0},{1,65},{65,129},{129,193},{193,1... | collective-permute-start | bytes 393224 | tf_op jit(solution)/shard_map/ppermute | solution.py:356
  68.3 2.7 %collective-permute-start.11 = (f32[2,128,128]{2,1,0:T(8,128)S(1)}, f32[2,128,128]{2,1,0:T(8,128)S(1)}, u32[]{:S(2)}, u32[]{:S(2)}) collective-permute-start(f32[2,128,128]{2,1,0:T(8,128)S(1)} %get-tuple-element.44), channel_id=1, source_target_pairs={{0,128},{64,192},{128,0},{192,64},{1,129},{65,193},{129,1},{193,65... | collective-permute-start | bytes 393224 | tf_op jit(solution)/shard_map/ppermute | solution.py:356
  71.0 0.0 collective-permute-done.13.refs_1_
  71.0 1.5 %collective-permute-start.12 = (f32[2,128,128]{2,1,0:T(8,128)S(1)}, f32[2,128,128]{2,1,0:T(8,128)S(1)}, u32[]{:S(2)}, u32[]{:S(2)}) collective-permute-start(f32[2,128,128]{2,1,0:T(8,128)S(1)} %get-tuple-element.45), channel_id=1, source_target_pairs={{0,192},{64,0},{128,64},{192,128},{1,193},{65,1},{129,65},{193,129... | collective-permute-start | bytes 393224 | tf_op jit(solution)/shard_map/ppermute | solution.py:356
  72.4 0.0 collective-permute-done.14.refs_2_
  72.4 0.0 collective-permute-done.15.refs_3_
  72.4 1.9 %collective-permute-done.10.part1_ref = f32[2,128,128]{2,1,0:T(8,128)S(1)} collective-permute-done((f32[2,128,128]{2,1,0:T(8,128)S(1)}, f32[2,128,128]{2,1,0:T(8,128)S(1)}, u32[]{:S(2)}, u32[]{:S(2)}) %collective-permute-start.10) | collective-permute-done | bytes 131104 | tf_op jit(solution)/shard_map/ppermute | solution.py:356
  74.4 3.9 %collective-permute-done.11.part2_ref = f32[2,128,128]{2,1,0:T(8,128)S(1)} collective-permute-done((f32[2,128,128]{2,1,0:T(8,128)S(1)}, f32[2,128,128]{2,1,0:T(8,128)S(1)}, u32[]{:S(2)}, u32[]{:S(2)}) %collective-permute-start.11) | collective-permute-done | bytes 131104 | tf_op jit(solution)/shard_map/ppermute | solution.py:356
  78.2 0.0 collective-permute-done.12.part3_ref
  78.2 0.0 all-to-all-done
  78.2 12.3 %update.1 = f32[4,32,2048]{2,1,0:T(8,128)S(1)} custom-call(s32[3]{0:T(128)S(1)} %pad_add_fusion.place_ref.refs_0_, f32[2,128,128]{2,1,0:T(8,128)S(1)} %get-tuple-element.42.part0_ref, f32[2,128,128]{2,1,0:T(8,128)S(1)} %collective-permute-done.10.part1_ref, f32[2,128,128]{2,1,0:T(8,128)S(1)} %collective-permute-done.11.part2_ref, ...), custom_call_target="tpu_custom_call" | custom-call | tf_op jit(solution)/shard_map/update/pallas_call | solution.py:339
  90.6 18.2 %all_to_all.10 = f32[4,32,2048]{2,1,0:T(8,128)S(1)} all-to-all(f32[4,32,2048]{2,1,0:T(8,128)S(1)} %update.1), channel_id=1, replica_groups=mesh['member'=4,'region'=16,'block'=4] {'member'}, dimensions={0} | all-to-all | bytes 2097152 | tf_op jit(solution)/shard_map/all_to_all | solution.py:390
  108.7 1.1 copy.16
Async XLA Ops:
  2.0 28.1 %collective-permute-start.5 = (f32[32,768]{1,0:T(8,128)S(1)}, f32[32,768]{1,0:T(8,128)S(1)}, u32[]{:S(2)}, u32[]{:S(2)}) collective-permute-start(f32[32,768]{1,0:T(8,128)S(1)} %get-tuple-element.35), channel_id=1, source_target_pairs={{0,64},{64,128},{128,192},{192,0},{1,65},{65,129},{129,193},{193,1... | collective-permute-start | bytes 294920 | tf_op jit(solution)/shard_map/ppermute | solution.py:356
  3.6 10.1 %collective-permute-start = (f32[36,16]{1,0:T(8,128)S(1)}, f32[36,16]{1,0:T(8,128)S(1)}, u32[]{:S(2)}, u32[]{:S(2)}) collective-permute-start(f32[36,16]{1,0:T(8,128)S(1)} %get-tuple-element.28), channel_id=1, source_target_pairs={{0,1},{1,2},{2,3},{3,4},{4,5},{5,6},{6,7},{7,8},{8,9},{9,10},{10,1... | collective-permute-start | bytes 6920 | tf_op jit(solution)/shard_map/ppermute | solution.py:373
  7.0 6.6 %collective-permute-start.1 = (f32[36,16]{1,0:T(8,128)S(1)}, f32[36,16]{1,0:T(8,128)S(1)}, u32[]{:S(2)}, u32[]{:S(2)}) collective-permute-start(f32[36,16]{1,0:T(8,128)S(1)} %get-tuple-element.29), channel_id=1, source_target_pairs={{1,0},{2,1},{3,2},{4,3},{5,4},{6,5},{7,6},{8,7},{9,8},{10,9},{11,1... | collective-permute-start | bytes 6920 | tf_op jit(solution)/shard_map/ppermute | solution.py:374
  9.4 22.8 %collective-permute-start.6 = (f32[32,768]{1,0:T(8,128)S(1)}, f32[32,768]{1,0:T(8,128)S(1)}, u32[]{:S(2)}, u32[]{:S(2)}) collective-permute-start(f32[32,768]{1,0:T(8,128)S(1)} %get-tuple-element.36), channel_id=1, source_target_pairs={{0,128},{64,192},{128,0},{192,64},{1,129},{65,193},{129,1},{193,65... | collective-permute-start | bytes 294920 | tf_op jit(solution)/shard_map/ppermute | solution.py:356
  12.2 20.0 %collective-permute-start.7 = (f32[32,768]{1,0:T(8,128)S(1)}, f32[32,768]{1,0:T(8,128)S(1)}, u32[]{:S(2)}, u32[]{:S(2)}) collective-permute-start(f32[32,768]{1,0:T(8,128)S(1)} %get-tuple-element.37), channel_id=1, source_target_pairs={{0,192},{64,0},{128,64},{192,128},{1,193},{65,1},{129,65},{193,129... | collective-permute-start | bytes 294920 | tf_op jit(solution)/shard_map/ppermute | solution.py:356
  13.7 21.9 %copy-start.1 = (f32[3072]{0:T(1024)S(1)}, f32[3072]{0:T(1024)}, u32[]{:S(2)}) copy-start(f32[3072]{0:T(1024)} %param.19) | copy-start | bytes 36868
  27.7 7.9 %copy-start = (f32[3072]{0:T(1024)S(1)}, f32[3072]{0:T(1024)}, u32[]{:S(2)}) copy-start(f32[3072]{0:T(1024)} %param.18) | copy-start | bytes 36868
  27.7 6.8 %collective-permute-start.2 = (f32[6,32,128]{2,1,0:T(8,128)S(1)}, f32[6,32,128]{2,1,0:T(8,128)S(1)}, u32[]{:S(2)}, u32[]{:S(2)}) collective-permute-start(f32[6,32,128]{2,1,0:T(8,128)S(1)} %get-tuple-element.31), channel_id=1, source_target_pairs={{0,64},{64,128},{128,192},{192,0},{1,65},{65,129},{129,193},{193,1... | collective-permute-start | bytes 294920 | tf_op jit(solution)/shard_map/ppermute | solution.py:356
  28.4 7.2 %collective-permute-start.3 = (f32[6,32,128]{2,1,0:T(8,128)S(1)}, f32[6,32,128]{2,1,0:T(8,128)S(1)}, u32[]{:S(2)}, u32[]{:S(2)}) collective-permute-start(f32[6,32,128]{2,1,0:T(8,128)S(1)} %get-tuple-element.32), channel_id=1, source_target_pairs={{0,128},{64,192},{128,0},{192,64},{1,129},{65,193},{129,1},{193,65... | collective-permute-start | bytes 294920 | tf_op jit(solution)/shard_map/ppermute | solution.py:356
  30.0 5.5 %collective-permute-start.4 = (f32[6,32,128]{2,1,0:T(8,128)S(1)}, f32[6,32,128]{2,1,0:T(8,128)S(1)}, u32[]{:S(2)}, u32[]{:S(2)}) collective-permute-start(f32[6,32,128]{2,1,0:T(8,128)S(1)} %get-tuple-element.33), channel_id=1, source_target_pairs={{0,192},{64,0},{128,64},{192,128},{1,193},{65,1},{129,65},{193,129... | collective-permute-start | bytes 294920 | tf_op jit(solution)/shard_map/ppermute | solution.py:356
  32.2 38.8 %collective-permute-start.13 = (f32[32,2048]{1,0:T(8,128)S(1)}, f32[32,2048]{1,0:T(8,128)S(1)}, u32[]{:S(2)}, u32[]{:S(2)}) collective-permute-start(f32[32,2048]{1,0:T(8,128)S(1)} %get-tuple-element.48), channel_id=1, source_target_pairs={{0,64},{64,128},{128,192},{192,0},{1,65},{65,129},{129,193},{193,1... | collective-permute-start | bytes 786440 | tf_op jit(solution)/shard_map/ppermute | solution.py:356
  38.4 9.7 %collective-permute-start.9 = (f32[2,128,128]{2,1,0:T(8,128)S(1)}, f32[2,128,128]{2,1,0:T(8,128)S(1)}, u32[]{:S(2)}, u32[]{:S(2)}) collective-permute-start(f32[2,128,128]{2,1,0:T(8,128)S(1)} %get-tuple-element.38.pair_ref), channel_id=1, source_target_pairs={{1,0},{2,1},{3,2},{4,3},{5,4},{6,5},{7,6},{8,7},{9,8},{10,9},{11,1... | collective-permute-start | bytes 393224 | tf_op jit(solution)/shard_map/ppermute | solution.py:385
  41.6 7.2 %collective-permute-start.8 = (f32[2,128,128]{2,1,0:T(8,128)S(1)}, f32[2,128,128]{2,1,0:T(8,128)S(1)}, u32[]{:S(2)}, u32[]{:S(2)}) collective-permute-start(f32[2,128,128]{2,1,0:T(8,128)S(1)} %get-tuple-element.38.pair_ref), channel_id=1, source_target_pairs={{0,1},{1,2},{2,3},{3,4},{4,5},{5,6},{6,7},{7,8},{8,9},{9,10},{10,1... | collective-permute-start | bytes 393224 | tf_op jit(solution)/shard_map/ppermute | solution.py:384
  44.3 28.2 %collective-permute-start.14 = (f32[32,2048]{1,0:T(8,128)S(1)}, f32[32,2048]{1,0:T(8,128)S(1)}, u32[]{:S(2)}, u32[]{:S(2)}) collective-permute-start(f32[32,2048]{1,0:T(8,128)S(1)} %get-tuple-element.49), channel_id=1, source_target_pairs={{0,128},{64,192},{128,0},{192,64},{1,129},{65,193},{129,1},{193,65... | collective-permute-start | bytes 786440 | tf_op jit(solution)/shard_map/ppermute | solution.py:356
  46.1 26.4 %collective-permute-start.15 = (f32[32,2048]{1,0:T(8,128)S(1)}, f32[32,2048]{1,0:T(8,128)S(1)}, u32[]{:S(2)}, u32[]{:S(2)}) collective-permute-start(f32[32,2048]{1,0:T(8,128)S(1)} %get-tuple-element.50), channel_id=1, source_target_pairs={{0,192},{64,0},{128,64},{192,128},{1,193},{65,1},{129,65},{193,129... | collective-permute-start | bytes 786440 | tf_op jit(solution)/shard_map/ppermute | solution.py:356
  48.8 17.1 %copy-start.2 = (s32[4,3]{1,0:T(4,128)S(1)}, s32[4,3]{1,0:T(4,128)}, u32[]{:S(2)}) copy-start(s32[4,3]{1,0:T(4,128)} %list_ref.1) | copy-start | bytes 148
  48.8 29.5 %all-to-all-start = ((f32[256,1,128]{2,1,0:T(1,128)}), f32[256,1,128]{2,1,0:T(1,128)S(1)}, u32[]{:S(2)}, u32[]{:S(2)}) async-start(f32[256,1,128]{2,1,0:T(1,128)} %get-tuple-element.46), calls=%async_computation | async-start | bytes 262144 | tf_op jit(solution)/shard_map/all_to_all | solution.py:387
  66.6 7.8 %collective-permute-start.10 = (f32[2,128,128]{2,1,0:T(8,128)S(1)}, f32[2,128,128]{2,1,0:T(8,128)S(1)}, u32[]{:S(2)}, u32[]{:S(2)}) collective-permute-start(f32[2,128,128]{2,1,0:T(8,128)S(1)} %get-tuple-element.43), channel_id=1, source_target_pairs={{0,64},{64,128},{128,192},{192,0},{1,65},{65,129},{129,193},{193,1... | collective-permute-start | bytes 393224 | tf_op jit(solution)/shard_map/ppermute | solution.py:356
  68.3 9.9 %collective-permute-start.11 = (f32[2,128,128]{2,1,0:T(8,128)S(1)}, f32[2,128,128]{2,1,0:T(8,128)S(1)}, u32[]{:S(2)}, u32[]{:S(2)}) collective-permute-start(f32[2,128,128]{2,1,0:T(8,128)S(1)} %get-tuple-element.44), channel_id=1, source_target_pairs={{0,128},{64,192},{128,0},{192,64},{1,129},{65,193},{129,1},{193,65... | collective-permute-start | bytes 393224 | tf_op jit(solution)/shard_map/ppermute | solution.py:356
  71.0 7.3 %collective-permute-start.12 = (f32[2,128,128]{2,1,0:T(8,128)S(1)}, f32[2,128,128]{2,1,0:T(8,128)S(1)}, u32[]{:S(2)}, u32[]{:S(2)}) collective-permute-start(f32[2,128,128]{2,1,0:T(8,128)S(1)} %get-tuple-element.45), channel_id=1, source_target_pairs={{0,192},{64,0},{128,64},{192,128},{1,193},{65,1},{129,65},{193,129... | collective-permute-start | bytes 393224 | tf_op jit(solution)/shard_map/ppermute | solution.py:356

commit v3 on v2

--- a/solution.py
+++ b/solution.py
@@ -32,7 +32,7 @@
 
 
 def edges_kernel(place_ref, state_ref, speed_ref, wave_ref, jam_ref, share_ref, noise_ref, *refs):
-    last_ref, first_ref = refs[:2]
+    near_ref, far_ref = refs[:2]
     noise_refs = refs[2 : 2 + GROUP]
     tile_refs = refs[2 + GROUP : 4 + GROUP]
     sem_ref = refs[4 + GROUP]
@@ -55,8 +55,10 @@
         copy.start()
     for copy in copies:
         copy.wait()
-    last_ref[...] = tile_refs[0][:, LANES - TICKS :]
-    first_ref[...] = tile_refs[1][:, :TICKS]
+    last, first = tile_refs[0][:, LANES - TICKS :], tile_refs[1][:, :TICKS]
+    even = lax.rem(place_ref[1], 2) == 0
+    near_ref[...] = jnp.where(even, last, first)
+    far_ref[...] = jnp.where(even, first, last)
 
 
 def edges(place, state, road, noise):
@@ -75,7 +77,7 @@
 
 
 def forecast_kernel(
-    place_ref, state_ref, low_ref, high_ref, speed_ref, wave_ref, jam_ref, share_ref, cells_ref, *refs
+    place_ref, state_ref, near_ref, far_ref, speed_ref, wave_ref, jam_ref, share_ref, cells_ref, *refs
 ):
     fore_refs, obs_refs = refs[:GROUP], refs[GROUP : 2 * GROUP]
     wide_ref, other_ref, side_ref, share_at, cell_ref, sem_ref = refs[2 * GROUP :]
@@ -101,8 +103,9 @@
     capacity = road_capacity(side_ref[0:1, main], side_ref[1:2, main], side_ref[2:3, main], share_at[...])
     side_ref[3:4, main] = capacity
     edge = jnp.zeros((rows + 4, LANES - TICKS), jnp.float32)
-    low = jnp.concatenate([edge, low_ref[...]], axis=1)
-    high = jnp.concatenate([high_ref[...], edge], axis=1)
+    even = lax.rem(slab, 2) == 0
+    low = jnp.concatenate([edge, jnp.where(even, far_ref[...], near_ref[...])], axis=1)
+    high = jnp.concatenate([jnp.where(even, near_ref[...], far_ref[...]), edge], axis=1)
     wide_ref[:, :LANES] = low[:rows]
     wide_ref[:, LANES + width :] = high[:rows]
     lane = lax.broadcasted_iota(jnp.int32, (1, LANES), 1)
@@ -177,7 +180,7 @@
         copy.wait()
 
 
-def forecast(place, state, low, high, road, cells):
+def forecast(place, state, near, far, road, cells):
     rows, width = state.shape
     piece = jax.ShapeDtypeStruct((PER_BLOCK, rows, LANES), jnp.float32)
     return pl.pallas_call(
@@ -195,13 +198,13 @@
         ],
         compiler_params=room(12),
         name="forecast",
-    )(place, state, low, high, *road, cells)
-
-
-def products_kernel(*refs):
+    )(place, state, near, far, *road, cells)
+
+
+def sums_kernel(*refs):
     place_ref, counts_ref = refs[:2]
     obs_refs, noise_refs = refs[2 : 2 + GROUP], refs[2 + GROUP : 2 + 2 * GROUP]
-    value_ref, variance_ref, pair_ref, sum_ref, obs_ref, noise_ref, count_ref, sem_ref = refs[2 + 2 * GROUP :]
+    value_ref, variance_ref, left_ref, right_ref, sum_ref, count_ref, sem_ref = refs[2 + 2 * GROUP :]
     fetch = pltpu.make_async_copy(counts_ref, count_ref, sem_ref.at[0])
     fetch.start()
     member = place_ref[0]
@@ -209,16 +212,15 @@
     for d in range(GROUP):
         at = pl.multiple_of(lax.rem(member - d + GROUP, GROUP) * rows, rows)
         for q in range(PER_BLOCK):
-            obs_ref[pl.ds(at, rows), q * LANES : (q + 1) * LANES] = obs_refs[d][q]
-        noise_ref[pl.ds(at, rows), :] = noise_refs[d][...]
+            left_ref[pl.ds(at, rows), q * LANES : (q + 1) * LANES] = obs_refs[d][q]
+        right_ref[pl.ds(TALLY + at, rows), :] = noise_refs[d][...]
     fetch.wait()
     count = count_ref[member]
     total_a = jnp.zeros((1, LANES), jnp.float32)
     total_b = jnp.zeros((1, LANES), jnp.float32)
-    scaled, plain, moved = [], [], []
     for q in range(PER_BLOCK):
         at = slice(q * LANES, (q + 1) * LANES)
-        x = obs_ref[:, at]
+        x = left_ref[:, at]
         value = value_ref[pl.ds(member * PER_BLOCK + q, 1), :]
         variance = variance_ref[pl.ds(member * PER_BLOCK + q, 1), :]
         mean = jnp.sum(x, axis=0, keepdims=True) / TALLY
@@ -230,15 +232,9 @@
         spread = jnp.sum(a * a, axis=0, keepdims=True) / (TALLY - 1)
         total_a += misfit * misfit * weight
         total_b += live * (spread / variance + 1.0)
-        scaled.append(a * weight)
-        plain.append(a)
-        moved.append(misfit + jnp.sqrt(variance) * noise_ref[:, at])
-    left = jnp.concatenate(scaled, axis=1)
-    right = jnp.concatenate([jnp.concatenate(plain, axis=1), jnp.concatenate(moved, axis=1)], axis=0)
-    dims = (((1,), (1,)), ((), ()))
-    both = lax.dot_general(left, right, dims, precision=HIGHEST, preferred_element_type=jnp.float32)
-    pair_ref[0] = both[:, :TALLY]
-    pair_ref[1] = both[:, TALLY:]
+        left_ref[:, at] = a * weight
+        right_ref[:TALLY, at] = a
+        right_ref[TALLY:, at] = misfit + jnp.sqrt(variance) * right_ref[TALLY:, at]
     lane = lax.broadcasted_iota(jnp.int32, (1, LANES), 1)
     sum_a = jnp.sum(total_a, axis=1, keepdims=True)
     sum_b = jnp.sum(total_b, axis=1, keepdims=True)
@@ -246,27 +242,51 @@
     sum_ref[...] = jnp.broadcast_to(sums[None], sum_ref.shape)
 
 
-def products(place, count, obs, noise, value, variance, devices):
+def observed_sums(place, count, obs, noise, value, variance, copies):
     rows = noise[0].shape[0]
     return pl.pallas_call(
+        sums_kernel,
+        out_shape=(
+            jax.ShapeDtypeStruct((GROUP * rows, SLOTS), jnp.float32),
+            jax.ShapeDtypeStruct((2 * GROUP * rows, SLOTS), jnp.float32),
+            jax.ShapeDtypeStruct((copies, 1, LANES), jnp.float32),
+        ),
+        in_specs=[SMEM, HBM] + [VMEM] * (2 * GROUP + 2),
+        out_specs=(VMEM,) * 3,
+        scratch_shapes=[pltpu.SMEM((GROUP,), jnp.int32), pltpu.SemaphoreType.DMA((1,))],
+        compiler_params=room(6),
+        name="observed_sums",
+    )(place, count, *obs, *noise, value, variance)
+
+
+def products_kernel(left_ref, right_ref, pair_ref):
+    dims = (((1,), (1,)), ((), ()))
+    both = lax.dot_general(
+        left_ref[...], right_ref[...], dims, precision=HIGHEST, preferred_element_type=jnp.float32
+    )
+    pair_ref[0] = both[:, :TALLY]
+    pair_ref[1] = both[:, TALLY:]
+
+
+def products(left, right):
+    return pl.pallas_call(
         products_kernel,
-        out_shape=(PAIR, jax.ShapeDtypeStruct((devices, 1, LANES), jnp.float32)),
-        in_specs=[SMEM, HBM] + [VMEM] * (2 * GROUP + 2),
-        out_specs=(VMEM, VMEM),
-        scratch_shapes=[pltpu.VMEM((GROUP * rows, SLOTS), jnp.float32)] * 2
-        + [pltpu.SMEM((GROUP,), jnp.int32), pltpu.SemaphoreType.DMA((1,))],
+        out_shape=PAIR,
+        in_specs=[VMEM] * 2,
+        out_specs=VMEM,
         compiler_params=room(6),
         name="products",
-    )(place, count, *obs, *noise, value, variance)
-
-
-def select_kernel(place_ref, list_ref, below_ref, pair_ref, above_ref, *out_refs):
+    )(left, right)
+
+
+def select_kernel(place_ref, list_ref, near_ref, pair_ref, far_ref, *out_refs):
     member = place_ref[0]
     slab = place_ref[1]
+    beside = 1 - 2 * lax.rem(slab, 2)
     for d in range(GROUP):
         target = lax.rem(member + d, GROUP)
         total = None
-        for step, ref in ((0, pair_ref), (-1, below_ref), (1, above_ref)):
+        for step, ref in ((0, pair_ref), (beside, near_ref), (-beside, far_ref)):
             name = (slab + step) * GROUP + member
             listed = (list_ref[target, 0] == name) | (list_ref[target, 1] == name) | (list_ref[target, 2] == name)
             share = jnp.where(listed, jnp.float32(1.0), jnp.float32(0.0)) * ref[...]
@@ -274,7 +294,7 @@
         out_refs[d][...] = total
 
 
-def select(place, lists, below, pair, above):
+def select(place, lists, near, pair, far):
     return pl.pallas_call(
         select_kernel,
         out_shape=(PAIR,) * GROUP,
@@ -282,7 +302,49 @@
         out_specs=(VMEM,) * GROUP,
         compiler_params=room(6),
         name="select",
-    )(place, lists, below, pair, above)
+    )(place, lists, near, pair, far)
+
+
+def eliminate(tiles):
+    sub = lax.broadcasted_iota(jnp.int32, (8, 2 * TALLY), 0)
+    total = len(tiles)
+    for k in range(total):
+        rows = [jnp.broadcast_to(tiles[k][j : j + 1, :], (8, 2 * TALLY)) for j in range(8)]
+        w = {}
+        for i in range(8):
+            for j in range(i, 8):
+                w[i, j] = jnp.broadcast_to(rows[i][:, 8 * k + j : 8 * k + j + 1], (8, LANES))
+        for p in range(8):
+            inverse = 1.0 / w[p, p]
+            line = {i: w[min(i, p), max(i, p)] for i in range(8) if i != p}
+            part = {i: line[i] * inverse for i in line}
+            for i in line:
+                for j in line:
+                    if i <= j:
+                        w[i, j] = w[i, j] - line[i] * part[j]
+            for i in line:
+                w[min(i, p), max(i, p)] = part[i]
+            w[p, p] = -inverse
+        fresh = []
+        for i in range(8):
+            row = None
+            for j in range(8):
+                entry = w[min(i, j), max(i, j)]
+                term = jnp.concatenate([entry, entry], axis=1) * rows[j]
+                row = term if row is None else row + term
+            fresh.append(-row)
+        for i in range(1, total + 1):
+            i = (k + i) % total
+            tile = tiles[i]
+            if i == k:
+                for j in range(8):
+                    tile = jnp.where(sub == j, fresh[j], tile)
+            else:
+                for j in range(8):
+                    column = jnp.broadcast_to(tiles[i][:, 8 * k + j : 8 * k + j + 1], (8, LANES))
+                    tile = tile - jnp.concatenate([column, column], axis=1) * fresh[j]
+            tiles[i] = tile
+    return tiles
 
 
 def update_kernel(place_ref, part0_ref, part1_ref, part2_ref, part3_ref, sums_ref, *refs):
@@ -297,32 +359,14 @@
     for copy in arrive:
         copy.start()
     sums = jnp.sum(sums_ref[...], axis=0, keepdims=True)
-    scale = jnp.sqrt(sums[:, 0:1] / sums[:, 1:2])
     gram = (part0_ref[0] + part1_ref[0]) + (part2_ref[0] + part3_ref[0])
     cross = (part0_ref[1] + part1_ref[1]) + (part2_ref[1] + part3_ref[1])
+    scale = jnp.sqrt(sums[:, 0:1] / sums[:, 1:2])
     row = lax.broadcasted_iota(jnp.int32, (TALLY, TALLY), 0)
     lane = lax.broadcasted_iota(jnp.int32, (TALLY, TALLY), 1)
     eye = jnp.where(row == lane, jnp.float32(TALLY - 1), jnp.float32(0.0))
     both = jnp.concatenate([eye + (scale * scale) * gram, eye + scale * cross], axis=1)
-    tiles = [both[8 * i : 8 * i + 8, :] for i in range(TALLY // 8)]
-    sub = lax.broadcasted_iota(jnp.int32, (8, 2 * TALLY), 0)
-    for k in range(TALLY // 8):
-        panel = tiles[k]
-        for j in range(8):
-            at = 8 * k + j
-            column = panel[:, at : at + 1]
-            pivot_row = panel[j : j + 1, :]
-            inverse = 1.0 / panel[j : j + 1, at : at + 1]
-            pivot_row = pivot_row * inverse
-            panel = jnp.where(sub == j, pivot_row, panel - column * pivot_row)
-        for i in range(TALLY // 8):
-            if i != k:
-                tile = tiles[i]
-                new = tile
-                for j in range(8):
-                    new = new - tile[:, 8 * k + j : 8 * k + j + 1] * panel[j : j + 1, :]
-                tiles[i] = new
-        tiles[k] = panel
+    tiles = eliminate([both[8 * i : 8 * i + 8, :] for i in range(TALLY // 8)])
     mixing = jnp.concatenate([tile[:, TALLY:] for tile in tiles], axis=0) * scale
     for copy in arrive:
         copy.wait()
@@ -358,34 +402,37 @@
     return [pieces[0], moved[1], moved[2], moved[3]]
 
 
+def swap(value, first):
+    slabs = lax.axis_size(RB)
+    up = [(i, i + 1) for i in range(first, slabs - 1, 2)]
+    return lax.ppermute(value, RB, up + [(b, a) for a, b in up])
+
+
 def body(load, free_speed, wave_speed, jam_density, capacity_share, cell, count, value, variance, noise, lists):
     rows, width = load.shape
     member = lax.axis_index("member")
     slab = lax.axis_index(RB)
     slabs = lax.axis_size(RB)
-    up = [(i, i + 1) for i in range(slabs - 1)]
-    down = [(b, a) for a, b in up]
     place = jnp.stack([member, slab, jnp.int32(slabs)]).astype(jnp.int32)
 
     road = [hold(v.reshape(1, width)) for v in (free_speed, wave_speed, jam_density, capacity_share)]
     load, noise, count, cells = [hold(v) for v in (load, noise, count, cell.reshape(-1, LANES))]
-    last, first, *noises = edges(place, load, road, noise)
-    low = lax.ppermute(last, RB, up)
-    high = lax.ppermute(first, RB, down)
-    out = forecast(place, load, low, high, road, cells)
+    near, far, *noises = edges(place, load, road, noise)
+    near, far = swap(near, 0), swap(far, 1)
+    out = forecast(place, load, near, far, road, cells)
     fore, obs = out[:GROUP], out[GROUP:]
     obs = exchange(obs)
     noises = exchange(noises)
     fore = exchange(fore)
 
-    pair, sums = products(
+    left, right, sums = observed_sums(
         place, count, obs, noises, value.reshape(-1, LANES), variance.reshape(-1, LANES), GROUP * slabs
     )
-    below = lax.ppermute(pair, RB, up)
-    above = lax.ppermute(pair, RB, down)
-    below, above, sums = lax.optimization_barrier((below, above, sums))
+    pair = products(left, right)
+    near, far = swap(pair, 0), swap(pair, 1)
+    near, far, sums = lax.optimization_barrier((near, far, sums))
     sums = lax.all_to_all(sums, ALL, 0, 0).reshape(GROUP * slabs, LANES)
-    parts = exchange(select(place, lists, below, pair, above))
+    parts = exchange(select(place, lists, near, pair, far))
     out = update(place, parts, sums, fore)
     out = lax.all_to_all(out, "member", 0, 0)
     return out.transpose(1, 0, 2).reshape(rows, width)

time: 110 us -> 98.9 us (0.90)
  starting transfers between devices: 48.8 us -> 41 us
  Pallas kernels: 31.7 us -> 26.3 us
  waiting for transfers between devices: 9.81 us -> 11.9 us
    pallas_call x1, Pallas kernels: 12.3 us -> 6.59 us  [update(): pl.pallas_call(update_kernel, out_shape=jax.ShapeDtypeStruct((GROUP,) + f...]
    ppermute x4, starting transfers between devices: 11.7 us -> 7.15 us  [swap(): return lax.ppermute(value, RB, up + [(b, a) for a, b in up])]
    all_to_all x1, starting transfers between devices: 17.1 us -> 14.2 us  [body(): sums = lax.all_to_all(sums, ALL, 0, 0).reshape(GROUP * slabs, LANES)]
    ppermute x4, waiting for transfers between devices: 0.64 us -> 2.44 us  [swap(): return lax.ppermute(value, RB, up + [(b, a) for a, b in up])]
    pallas_call x1 -> x2, Pallas kernels: 2.81 us -> 3.03 us  [the longest x1 2.11 us: observed_sums(): pl.pallas_call(sums_kernel, out_shape=(jax.ShapeDtypeStruct((GROUP * rows...]
  transfers between devices with their start and end apart: 17 -> 17, of which waited for: 5 -> 7; matrix products, arithmetic and copies ran while one was open for 0% -> 0% of each run, Pallas kernels for 16% -> 18%
where the time goes in v3:
time: 98.9 us; the launch traced here: 98.7 us
  starting transfers between devices  41 us (41%)
  Pallas kernels  26.3 us (27%)
  blocking collectives  18.2 us (18%)
  waiting for transfers between devices  11.9 us (12%)
  local copies, waits for them, and re-layouts  1.08 us (1%)
    ppermute x12, starting transfers between devices, exchange(): lax.ppermute(pieces[d], 'member', [(i, (i + d) % GROUP) for i in range(GR...  19.7 us
    all_to_all x1, blocking collectives, body(): out = lax.all_to_all(out, 'member', 0, 0)  18.2 us
    all_to_all x1, starting transfers between devices, body(): sums = lax.all_to_all(sums, ALL, 0, 0).reshape(GROUP * slabs, LANES)  14.2 us
    pallas_call x1, Pallas kernels, forecast(): pl.pallas_call(forecast_kernel, out_shape=(jax.ShapeDtypeStruct((rows, CE...  14 us
    ppermute x12, waiting for transfers between devices, exchange(): lax.ppermute(pieces[d], 'member', [(i, (i + d) % GROUP) for i in range(GR...  9.44 us
    ppermute x4, starting transfers between devices, swap(): return lax.ppermute(value, RB, up + [(b, a) for a, b in up])  7.15 us
    pallas_call x1, Pallas kernels, update(): pl.pallas_call(update_kernel, out_shape=jax.ShapeDtypeStruct((GROUP,) + f...  6.59 us
    ppermute x4, waiting for transfers between devices, swap(): return lax.ppermute(value, RB, up + [(b, a) for a, b in up])  2.44 us
  transfers between devices with their start and end apart: 17, of which 7 were waited for; matrix products, arithmetic and copies ran while one was open for 0% of the time, Pallas kernels for 18%

profile of v3, /device:TPU:8, one launch (start us, length us, event | category | flops | bytes accessed | tf_op | source)
XLA Modules:
  0.0 98.7 jit_solution(17947112438157916273)
XLA Ops:
  0.0 0.1 pad_add_fusion.place_ref.refs_0_
  0.1 2.0 %edges.1 = (f32[36,16]{1,0:T(8,128)S(1)}, f32[36,16]{1,0:T(8,128)S(1)}, f32[32,768]{1,0:T(8,128)S(1)}, f32[32,768]{1,0:T(8,128)S(1)}, f32[32,768]{1,0:T(8,128)S(1)}, /*index=5*/f32[32,768]{1,0:T(8,128)S(1)}) custom-call(s32[3]{0:T(128)S(1)} %pad_add_fusion.place_ref.refs_0_, f32[32,8192]{1,0:T(8,128)} %state_ref.3, f32[1,8192]{1,0:T(1,128)} %bitcast.17, ...), custom_call_target="tpu_custom_call" | custom-call | tf_op jit(solution)/shard_map/edges/pallas_call | solution.py:68
  2.1 1.6 %collective-permute-start.5 = (f32[32,768]{1,0:T(8,128)S(1)}, f32[32,768]{1,0:T(8,128)S(1)}, u32[]{:S(2)}, u32[]{:S(2)}) collective-permute-start(f32[32,768]{1,0:T(8,128)S(1)} %get-tuple-element.36), channel_id=1, source_target_pairs={{0,64},{64,128},{128,192},{192,0},{1,65},{65,129},{129,193},{193,1... | collective-permute-start | bytes 294920 | tf_op jit(solution)/shard_map/ppermute | solution.py:400
  3.6 0.8 collective-permute-start
  4.4 4.0 %collective-permute-start.1 = (f32[36,16]{1,0:T(8,128)S(1)}, f32[36,16]{1,0:T(8,128)S(1)}, u32[]{:S(2)}, u32[]{:S(2)}) collective-permute-start(f32[36,16]{1,0:T(8,128)S(1)} %get-tuple-element.30), channel_id=1, source_target_pairs={{1,2},{3,4},{5,6},{7,8},{9,10},{11,12},{13,14},{15,16},{17,18},{19... | collective-permute-start | bytes 6920 | tf_op jit(solution)/shard_map/ppermute | solution.py:408
  8.4 2.8 %collective-permute-start.6 = (f32[32,768]{1,0:T(8,128)S(1)}, f32[32,768]{1,0:T(8,128)S(1)}, u32[]{:S(2)}, u32[]{:S(2)}) collective-permute-start(f32[32,768]{1,0:T(8,128)S(1)} %get-tuple-element.37), channel_id=1, source_target_pairs={{0,128},{64,192},{128,0},{192,64},{1,129},{65,193},{129,1},{193,65... | collective-permute-start | bytes 294920 | tf_op jit(solution)/shard_map/ppermute | solution.py:400
  11.2 1.4 %collective-permute-start.7 = (f32[32,768]{1,0:T(8,128)S(1)}, f32[32,768]{1,0:T(8,128)S(1)}, u32[]{:S(2)}, u32[]{:S(2)}) collective-permute-start(f32[32,768]{1,0:T(8,128)S(1)} %get-tuple-element.38), channel_id=1, source_target_pairs={{0,192},{64,0},{128,64},{192,128},{1,193},{65,1},{129,65},{193,129... | collective-permute-start | bytes 294920 | tf_op jit(solution)/shard_map/ppermute | solution.py:400
  12.6 0.0 collective-permute-done.near_ref
  12.7 0.0 collective-permute-done.1.far_ref
  12.7 0.0 copy-start.1
  12.7 14.0 %forecast.1 = (f32[32,2048]{1,0:T(8,128)S(1)}, f32[32,2048]{1,0:T(8,128)S(1)}, f32[32,2048]{1,0:T(8,128)S(1)}, f32[32,2048]{1,0:T(8,128)S(1)}, f32[6,32,128]{2,1...) custom-call(s32[3]{0:T(128)S(1)} %pad_add_fusion.place_ref.refs_0_, ...), custom_call_target="tpu_custom_call" | custom-call | tf_op jit(solution)/shard_map/forecast/pallas_call | solution.py:186
  26.7 0.0 copy-start
  26.7 0.7 collective-permute-start.2
  27.4 1.4 %collective-permute-start.3 = (f32[6,32,128]{2,1,0:T(8,128)S(1)}, f32[6,32,128]{2,1,0:T(8,128)S(1)}, u32[]{:S(2)}, u32[]{:S(2)}) collective-permute-start(f32[6,32,128]{2,1,0:T(8,128)S(1)} %get-tuple-element.33), channel_id=1, source_target_pairs={{0,128},{64,192},{128,0},{192,64},{1,129},{65,193},{129,1},{193,65... | collective-permute-start | bytes 294920 | tf_op jit(solution)/shard_map/ppermute | solution.py:400
  28.8 0.0 collective-permute-done.5.refs_7_
  28.8 1.3 %collective-permute-start.4 = (f32[6,32,128]{2,1,0:T(8,128)S(1)}, f32[6,32,128]{2,1,0:T(8,128)S(1)}, u32[]{:S(2)}, u32[]{:S(2)}) collective-permute-start(f32[6,32,128]{2,1,0:T(8,128)S(1)} %get-tuple-element.34), channel_id=1, source_target_pairs={{0,192},{64,0},{128,64},{192,128},{1,193},{65,1},{129,65},{193,129... | collective-permute-start | bytes 294920 | tf_op jit(solution)/shard_map/ppermute | solution.py:400
  30.2 0.0 collective-permute-done.6.refs_8_
  30.2 0.8 collective-permute-start.13
  31.0 0.0 collective-permute-done.7.refs_9_
  31.0 3.3 %collective-permute-done.2.refs_3_ = f32[6,32,128]{2,1,0:T(8,128)S(1)} collective-permute-done((f32[6,32,128]{2,1,0:T(8,128)S(1)}, f32[6,32,128]{2,1,0:T(8,128)S(1)}, u32[]{:S(2)}, u32[]{:S(2)}) %collective-permute-start.2) | collective-permute-done | bytes 98336 | tf_op jit(solution)/shard_map/ppermute | solution.py:400
  34.3 0.2 collective-permute-done.3.refs_4_
  34.6 0.0 collective-permute-done.4.refs_5_
  34.6 0.0 copy-done.1
  34.6 0.0 copy-done
  34.6 2.1 %observed_sums.1 = (f32[128,768]{1,0:T(8,128)S(1)}, f32[256,768]{1,0:T(8,128)S(1)}, f32[256,1,128]{2,1,0:T(1,128)}) custom-call(s32[3]{0:T(128)S(1)} %pad_add_fusion.place_ref.refs_0_, s32[4]{0:T(128)} %refs_1_.1, f32[6,32,128]{2,1,0:T(8,128)S(1)} %get-tuple-element.31.refs_2_, f32[6,32,128]{2,1,0:T(8,128)S(1)} %collective-permute-done.2.refs_3_, ...), custom_call_target="tpu_custom_call" | custom-call | tf_op jit(solution)/shard_map/observed_sums/pallas_call | solution.py:247
  36.7 0.9 products.1.pair_ref
  37.6 2.3 %collective-permute-start.9 = (f32[2,128,128]{2,1,0:T(8,128)S(1)}, f32[2,128,128]{2,1,0:T(8,128)S(1)}, u32[]{:S(2)}, u32[]{:S(2)}) collective-permute-start(f32[2,128,128]{2,1,0:T(8,128)S(1)} %products.1.pair_ref), channel_id=1, source_target_pairs={{1,2},{3,4},{5,6},{7,8},{9,10},{11,12},{13,14},{15,16},{17,18},{19... | collective-permute-start | bytes 393224 | tf_op jit(solution)/shard_map/ppermute | solution.py:408
  39.9 0.1 collective-permute-start.8
  40.0 1.9 %collective-permute-start.14 = (f32[32,2048]{1,0:T(8,128)S(1)}, f32[32,2048]{1,0:T(8,128)S(1)}, u32[]{:S(2)}, u32[]{:S(2)}) collective-permute-start(f32[32,2048]{1,0:T(8,128)S(1)} %get-tuple-element.51), channel_id=1, source_target_pairs={{0,128},{64,192},{128,0},{192,64},{1,129},{65,193},{129,1},{193,65... | collective-permute-start | bytes 786440 | tf_op jit(solution)/shard_map/ppermute | solution.py:400
  41.9 2.1 %collective-permute-start.15 = (f32[32,2048]{1,0:T(8,128)S(1)}, f32[32,2048]{1,0:T(8,128)S(1)}, u32[]{:S(2)}, u32[]{:S(2)}) collective-permute-start(f32[32,2048]{1,0:T(8,128)S(1)} %get-tuple-element.52), channel_id=1, source_target_pairs={{0,192},{64,0},{128,64},{192,128},{1,193},{65,1},{129,65},{193,129... | collective-permute-start | bytes 786440 | tf_op jit(solution)/shard_map/ppermute | solution.py:400
  44.0 0.5 collective-permute-done.9.far_ref
  44.5 1.9 %collective-permute-done.8.near_ref = f32[2,128,128]{2,1,0:T(8,128)S(1)} collective-permute-done((f32[2,128,128]{2,1,0:T(8,128)S(1)}, f32[2,128,128]{2,1,0:T(8,128)S(1)}, u32[]{:S(2)}, u32[]{:S(2)}) %collective-permute-start.8) | collective-permute-done | bytes 131104 | tf_op jit(solution)/shard_map/ppermute | solution.py:408
  46.4 0.0 copy-start.2
  46.4 14.2 %all-to-all-start = ((f32[256,1,128]{2,1,0:T(1,128)}), f32[256,1,128]{2,1,0:T(1,128)S(1)}, u32[]{:S(2)}, u32[]{:S(2)}) async-start(f32[256,1,128]{2,1,0:T(1,128)} %get-tuple-element.48), calls=%async_computation | async-start | bytes 262144 | tf_op jit(solution)/shard_map/all_to_all | solution.py:434
  60.5 0.0 copy-done.2
  60.6 0.7 select.1
  61.3 1.5 %collective-permute-start.10 = (f32[2,128,128]{2,1,0:T(8,128)S(1)}, f32[2,128,128]{2,1,0:T(8,128)S(1)}, u32[]{:S(2)}, u32[]{:S(2)}) collective-permute-start(f32[2,128,128]{2,1,0:T(8,128)S(1)} %get-tuple-element.45), channel_id=1, source_target_pairs={{0,64},{64,128},{128,192},{192,0},{1,65},{65,129},{129,193},{193,1... | collective-permute-start | bytes 393224 | tf_op jit(solution)/shard_map/ppermute | solution.py:400
  62.8 2.7 %collective-permute-start.11 = (f32[2,128,128]{2,1,0:T(8,128)S(1)}, f32[2,128,128]{2,1,0:T(8,128)S(1)}, u32[]{:S(2)}, u32[]{:S(2)}) collective-permute-start(f32[2,128,128]{2,1,0:T(8,128)S(1)} %get-tuple-element.46), channel_id=1, source_target_pairs={{0,128},{64,192},{128,0},{192,64},{1,129},{65,193},{129,1},{193,65... | collective-permute-start | bytes 393224 | tf_op jit(solution)/shard_map/ppermute | solution.py:400
  65.5 0.0 collective-permute-done.13.refs_1_
  65.5 1.5 %collective-permute-start.12 = (f32[2,128,128]{2,1,0:T(8,128)S(1)}, f32[2,128,128]{2,1,0:T(8,128)S(1)}, u32[]{:S(2)}, u32[]{:S(2)}) collective-permute-start(f32[2,128,128]{2,1,0:T(8,128)S(1)} %get-tuple-element.47), channel_id=1, source_target_pairs={{0,192},{64,0},{128,64},{192,128},{1,193},{65,1},{129,65},{193,129... | collective-permute-start | bytes 393224 | tf_op jit(solution)/shard_map/ppermute | solution.py:400
  66.9 0.0 collective-permute-done.14.refs_2_
  66.9 0.0 collective-permute-done.15.refs_3_
  66.9 1.9 %collective-permute-done.10.part1_ref = f32[2,128,128]{2,1,0:T(8,128)S(1)} collective-permute-done((f32[2,128,128]{2,1,0:T(8,128)S(1)}, f32[2,128,128]{2,1,0:T(8,128)S(1)}, u32[]{:S(2)}, u32[]{:S(2)}) %collective-permute-start.10) | collective-permute-done | bytes 131104 | tf_op jit(solution)/shard_map/ppermute | solution.py:400
  68.8 3.9 %collective-permute-done.11.part2_ref = f32[2,128,128]{2,1,0:T(8,128)S(1)} collective-permute-done((f32[2,128,128]{2,1,0:T(8,128)S(1)}, f32[2,128,128]{2,1,0:T(8,128)S(1)}, u32[]{:S(2)}, u32[]{:S(2)}) %collective-permute-start.11) | collective-permute-done | bytes 131104 | tf_op jit(solution)/shard_map/ppermute | solution.py:400
  72.8 0.0 collective-permute-done.12.part3_ref
  72.8 0.1 all-to-all-done
  72.8 6.6 %update.1 = f32[4,32,2048]{2,1,0:T(8,128)S(1)} custom-call(s32[3]{0:T(128)S(1)} %pad_add_fusion.place_ref.refs_0_, f32[2,128,128]{2,1,0:T(8,128)S(1)} %get-tuple-element.44.part0_ref, f32[2,128,128]{2,1,0:T(8,128)S(1)} %collective-permute-done.10.part1_ref, f32[2,128,128]{2,1,0:T(8,128)S(1)} %collective-permute-done.11.part2_ref, ...), custom_call_target="tpu_custom_call" | custom-call | tf_op jit(solution)/shard_map/update/pallas_call | solution.py:383
  79.4 18.2 %all_to_all.10 = f32[4,32,2048]{2,1,0:T(8,128)S(1)} all-to-all(f32[4,32,2048]{2,1,0:T(8,128)S(1)} %update.1), channel_id=1, replica_groups=mesh['member'=4,'region'=16,'block'=4] {'member'}, dimensions={0} | all-to-all | bytes 2097152 | tf_op jit(solution)/shard_map/all_to_all | solution.py:437
  97.6 1.1 %copy.16 = f32[4,4,8,2048]{3,2,0,1:T(8,128)} copy(f32[4,4,8,2048]{3,2,1,0:T(8,128)S(1)} %bitcast.16) | data formatting | bytes 2097152 | tf_op jit(solution)/shard_map/reshape | solution.py:438
Async XLA Ops:
  2.1 26.7 %collective-permute-start.5 = (f32[32,768]{1,0:T(8,128)S(1)}, f32[32,768]{1,0:T(8,128)S(1)}, u32[]{:S(2)}, u32[]{:S(2)}) collective-permute-start(f32[32,768]{1,0:T(8,128)S(1)} %get-tuple-element.36), channel_id=1, source_target_pairs={{0,64},{64,128},{128,192},{192,0},{1,65},{65,129},{129,193},{193,1... | collective-permute-start | bytes 294920 | tf_op jit(solution)/shard_map/ppermute | solution.py:400
  3.6 9.0 %collective-permute-start = (f32[36,16]{1,0:T(8,128)S(1)}, f32[36,16]{1,0:T(8,128)S(1)}, u32[]{:S(2)}, u32[]{:S(2)}) collective-permute-start(f32[36,16]{1,0:T(8,128)S(1)} %get-tuple-element.29), channel_id=1, source_target_pairs={{0,1},{2,3},{4,5},{6,7},{8,9},{10,11},{12,13},{14,15},{16,17},{18,... | collective-permute-start | bytes 6920 | tf_op jit(solution)/shard_map/ppermute | solution.py:408
  4.4 8.2 %collective-permute-start.1 = (f32[36,16]{1,0:T(8,128)S(1)}, f32[36,16]{1,0:T(8,128)S(1)}, u32[]{:S(2)}, u32[]{:S(2)}) collective-permute-start(f32[36,16]{1,0:T(8,128)S(1)} %get-tuple-element.30), channel_id=1, source_target_pairs={{1,2},{3,4},{5,6},{7,8},{9,10},{11,12},{13,14},{15,16},{17,18},{19... | collective-permute-start | bytes 6920 | tf_op jit(solution)/shard_map/ppermute | solution.py:408
  8.4 21.8 %collective-permute-start.6 = (f32[32,768]{1,0:T(8,128)S(1)}, f32[32,768]{1,0:T(8,128)S(1)}, u32[]{:S(2)}, u32[]{:S(2)}) collective-permute-start(f32[32,768]{1,0:T(8,128)S(1)} %get-tuple-element.37), channel_id=1, source_target_pairs={{0,128},{64,192},{128,0},{192,64},{1,129},{65,193},{129,1},{193,65... | collective-permute-start | bytes 294920 | tf_op jit(solution)/shard_map/ppermute | solution.py:400
  11.2 19.8 %collective-permute-start.7 = (f32[32,768]{1,0:T(8,128)S(1)}, f32[32,768]{1,0:T(8,128)S(1)}, u32[]{:S(2)}, u32[]{:S(2)}) collective-permute-start(f32[32,768]{1,0:T(8,128)S(1)} %get-tuple-element.38), channel_id=1, source_target_pairs={{0,192},{64,0},{128,64},{192,128},{1,193},{65,1},{129,65},{193,129... | collective-permute-start | bytes 294920 | tf_op jit(solution)/shard_map/ppermute | solution.py:400
  12.7 21.9 %copy-start.1 = (f32[3072]{0:T(1024)S(1)}, f32[3072]{0:T(1024)}, u32[]{:S(2)}) copy-start(f32[3072]{0:T(1024)} %param.19) | copy-start | bytes 36868
  26.7 7.9 %copy-start = (f32[3072]{0:T(1024)S(1)}, f32[3072]{0:T(1024)}, u32[]{:S(2)}) copy-start(f32[3072]{0:T(1024)} %param.18) | copy-start | bytes 36868
  26.7 7.6 %collective-permute-start.2 = (f32[6,32,128]{2,1,0:T(8,128)S(1)}, f32[6,32,128]{2,1,0:T(8,128)S(1)}, u32[]{:S(2)}, u32[]{:S(2)}) collective-permute-start(f32[6,32,128]{2,1,0:T(8,128)S(1)} %get-tuple-element.32), channel_id=1, source_target_pairs={{0,64},{64,128},{128,192},{192,0},{1,65},{65,129},{129,193},{193,1... | collective-permute-start | bytes 294920 | tf_op jit(solution)/shard_map/ppermute | solution.py:400
  27.4 7.2 %collective-permute-start.3 = (f32[6,32,128]{2,1,0:T(8,128)S(1)}, f32[6,32,128]{2,1,0:T(8,128)S(1)}, u32[]{:S(2)}, u32[]{:S(2)}) collective-permute-start(f32[6,32,128]{2,1,0:T(8,128)S(1)} %get-tuple-element.33), channel_id=1, source_target_pairs={{0,128},{64,192},{128,0},{192,64},{1,129},{65,193},{129,1},{193,65... | collective-permute-start | bytes 294920 | tf_op jit(solution)/shard_map/ppermute | solution.py:400
  28.8 5.8 %collective-permute-start.4 = (f32[6,32,128]{2,1,0:T(8,128)S(1)}, f32[6,32,128]{2,1,0:T(8,128)S(1)}, u32[]{:S(2)}, u32[]{:S(2)}) collective-permute-start(f32[6,32,128]{2,1,0:T(8,128)S(1)} %get-tuple-element.34), channel_id=1, source_target_pairs={{0,192},{64,0},{128,64},{192,128},{1,193},{65,1},{129,65},{193,129... | collective-permute-start | bytes 294920 | tf_op jit(solution)/shard_map/ppermute | solution.py:400
  30.2 35.3 %collective-permute-start.13 = (f32[32,2048]{1,0:T(8,128)S(1)}, f32[32,2048]{1,0:T(8,128)S(1)}, u32[]{:S(2)}, u32[]{:S(2)}) collective-permute-start(f32[32,2048]{1,0:T(8,128)S(1)} %get-tuple-element.50), channel_id=1, source_target_pairs={{0,64},{64,128},{128,192},{192,0},{1,65},{65,129},{129,193},{193,1... | collective-permute-start | bytes 786440 | tf_op jit(solution)/shard_map/ppermute | solution.py:400
  37.6 6.9 %collective-permute-start.9 = (f32[2,128,128]{2,1,0:T(8,128)S(1)}, f32[2,128,128]{2,1,0:T(8,128)S(1)}, u32[]{:S(2)}, u32[]{:S(2)}) collective-permute-start(f32[2,128,128]{2,1,0:T(8,128)S(1)} %products.1.pair_ref), channel_id=1, source_target_pairs={{1,2},{3,4},{5,6},{7,8},{9,10},{11,12},{13,14},{15,16},{17,18},{19... | collective-permute-start | bytes 393224 | tf_op jit(solution)/shard_map/ppermute | solution.py:408
  39.9 6.5 %collective-permute-start.8 = (f32[2,128,128]{2,1,0:T(8,128)S(1)}, f32[2,128,128]{2,1,0:T(8,128)S(1)}, u32[]{:S(2)}, u32[]{:S(2)}) collective-permute-start(f32[2,128,128]{2,1,0:T(8,128)S(1)} %products.1.pair_ref), channel_id=1, source_target_pairs={{0,1},{2,3},{4,5},{6,7},{8,9},{10,11},{12,13},{14,15},{16,17},{18,... | collective-permute-start | bytes 393224 | tf_op jit(solution)/shard_map/ppermute | solution.py:408
  40.0 26.9 %collective-permute-start.14 = (f32[32,2048]{1,0:T(8,128)S(1)}, f32[32,2048]{1,0:T(8,128)S(1)}, u32[]{:S(2)}, u32[]{:S(2)}) collective-permute-start(f32[32,2048]{1,0:T(8,128)S(1)} %get-tuple-element.51), channel_id=1, source_target_pairs={{0,128},{64,192},{128,0},{192,64},{1,129},{65,193},{129,1},{193,65... | collective-permute-start | bytes 786440 | tf_op jit(solution)/shard_map/ppermute | solution.py:400
  41.9 25.0 %collective-permute-start.15 = (f32[32,2048]{1,0:T(8,128)S(1)}, f32[32,2048]{1,0:T(8,128)S(1)}, u32[]{:S(2)}, u32[]{:S(2)}) collective-permute-start(f32[32,2048]{1,0:T(8,128)S(1)} %get-tuple-element.52), channel_id=1, source_target_pairs={{0,192},{64,0},{128,64},{192,128},{1,193},{65,1},{129,65},{193,129... | collective-permute-start | bytes 786440 | tf_op jit(solution)/shard_map/ppermute | solution.py:400
  46.4 14.2 %copy-start.2 = (s32[4,3]{1,0:T(4,128)S(1)}, s32[4,3]{1,0:T(4,128)}, u32[]{:S(2)}) copy-start(s32[4,3]{1,0:T(4,128)} %list_ref.1) | copy-start | bytes 148
  46.4 26.4 %all-to-all-start = ((f32[256,1,128]{2,1,0:T(1,128)}), f32[256,1,128]{2,1,0:T(1,128)S(1)}, u32[]{:S(2)}, u32[]{:S(2)}) async-start(f32[256,1,128]{2,1,0:T(1,128)} %get-tuple-element.48), calls=%async_computation | async-start | bytes 262144 | tf_op jit(solution)/shard_map/all_to_all | solution.py:434
  61.3 7.6 %collective-permute-start.10 = (f32[2,128,128]{2,1,0:T(8,128)S(1)}, f32[2,128,128]{2,1,0:T(8,128)S(1)}, u32[]{:S(2)}, u32[]{:S(2)}) collective-permute-start(f32[2,128,128]{2,1,0:T(8,128)S(1)} %get-tuple-element.45), channel_id=1, source_target_pairs={{0,64},{64,128},{128,192},{192,0},{1,65},{65,129},{129,193},{193,1... | collective-permute-start | bytes 393224 | tf_op jit(solution)/shard_map/ppermute | solution.py:400
  62.8 10.0 %collective-permute-start.11 = (f32[2,128,128]{2,1,0:T(8,128)S(1)}, f32[2,128,128]{2,1,0:T(8,128)S(1)}, u32[]{:S(2)}, u32[]{:S(2)}) collective-permute-start(f32[2,128,128]{2,1,0:T(8,128)S(1)} %get-tuple-element.46), channel_id=1, source_target_pairs={{0,128},{64,192},{128,0},{192,64},{1,129},{65,193},{129,1},{193,65... | collective-permute-start | bytes 393224 | tf_op jit(solution)/shard_map/ppermute | solution.py:400
  65.5 7.3 %collective-permute-start.12 = (f32[2,128,128]{2,1,0:T(8,128)S(1)}, f32[2,128,128]{2,1,0:T(8,128)S(1)}, u32[]{:S(2)}, u32[]{:S(2)}) collective-permute-start(f32[2,128,128]{2,1,0:T(8,128)S(1)} %get-tuple-element.47), channel_id=1, source_target_pairs={{0,192},{64,0},{128,64},{192,128},{1,193},{65,1},{129,65},{193,129... | collective-permute-start | bytes 393224 | tf_op jit(solution)/shard_map/ppermute | solution.py:400

commit v4 on v3

--- a/solution.py
+++ b/solution.py
@@ -11,6 +11,8 @@
 SLOTS = 768
 LANES = 128
 GROUP = 4
+BATCH = 6
+SPAN = LANES + 2 * TICKS
 PER_BLOCK = SLOTS // LANES
 RB = ("region", "block")
 ALL = ("member", "region", "block")
@@ -76,11 +78,78 @@
     )(place, state, *road, noise)
 
 
+def advance(wide_ref, side_ref, tiles_ref, strip_ref, road_ref, here_ref, there_ref):
+    rows = wide_ref.shape[0]
+    count = wide_ref.shape[1] // LANES
+    inner = count - 2
+    pairs = rows // 2
+    right = SPAN - TICKS
+    lane = lax.broadcasted_iota(jnp.int32, (LANES, LANES), 1)
+    for i in range(4):
+        for v in range(count):
+            strip_ref[7 + v : 8 + v, :] = side_ref[i : i + 1, v * LANES : (v + 1) * LANES]
+        own, before, after = [strip_ref[n : n + inner, :] for n in (8, 7, 9)]
+        beside = jnp.where(lane[:inner] >= inner, before, after)
+        own = jnp.concatenate([own, own], axis=0).T
+        beside = jnp.concatenate([beside, beside], axis=0).T
+        for s in range(8):
+            road_ref[i, pl.ds(TICKS * 8 + s, LANES, stride=8), :] = own
+            road_ref[i, pl.ds(s, TICKS, stride=8), :] = beside[LANES - TICKS :]
+            road_ref[i, pl.ds(right * 8 + s, TICKS, stride=8), :] = beside[:TICKS]
+    for g in range(rows // 8):
+        for v in range(count):
+            at = (g * count + v) * 8
+            tiles_ref[at : at + 8, :] = wide_ref[8 * g : 8 * g + 8, v * LANES : (v + 1) * LANES]
+
+    def member_rows(p, h, shift):
+        r = p + pairs * h
+        return pl.ds((r // 8 * count + 1 + shift) * 8 + r % 8, inner, stride=8)
+
+    def pair_rows(p, shift):
+        return jnp.concatenate([tiles_ref[member_rows(p, h, shift), :] for h in (0, 1)], axis=0)
+
+    for p in range(pairs):
+        beside = jnp.where(lane >= inner, pair_rows(p, -1), pair_rows(p, 1)).T
+        here_ref[pl.ds(TICKS * pairs + p, LANES, stride=pairs), :] = pair_rows(p, 0).T
+        here_ref[pl.ds(p, TICKS, stride=pairs), :] = beside[LANES - TICKS :]
+        here_ref[pl.ds(right * pairs + p, TICKS, stride=pairs), :] = beside[:TICKS]
+
+    def half(src, dst, first):
+        for at in range(first, SPAN - first, BATCH):
+            n = min(BATCH, SPAN - first - at)
+            x = src[(at - 1) * pairs : (at + n + 1) * pairs, :].reshape(n + 2, pairs // 8, 8, LANES)
+            speed, wave, jam, cap = [
+                road_ref[i, (at - 1) * 8 : (at + n + 1) * 8, :].reshape(n + 2, 1, 8, LANES) for i in range(4)
+            ]
+            demand = jnp.minimum(speed[:-1] * x[:-1], cap[:-1])
+            supply = jnp.minimum(cap[1:], wave[1:] * (jam[1:] - x[1:]))
+            flux = jnp.minimum(demand, supply)
+            dst[at * pairs : (at + n) * pairs, :] = (x[1:-1] + flux[:-1] - flux[1:]).reshape(n * pairs, LANES)
+
+    for first in (1, 1 + TICKS // 2):
+
+        def step(_, carry):
+            half(here_ref, there_ref, first)
+            half(there_ref, here_ref, first)
+            return carry
+
+        lax.fori_loop(0, TICKS // 4, step, 0)
+    for p in range(pairs):
+        done = here_ref[pl.ds(TICKS * pairs + p, LANES, stride=pairs), :].T
+        for h in (0, 1):
+            tiles_ref[member_rows(p, h, 0), :] = done[inner * h : inner * (h + 1)]
+    for g in range(rows // 8):
+        for v in range(1, count - 1):
+            at = (g * count + v) * 8
+            wide_ref[8 * g : 8 * g + 8, v * LANES : (v + 1) * LANES] = tiles_ref[at : at + 8, :]
+
+
 def forecast_kernel(
     place_ref, state_ref, near_ref, far_ref, speed_ref, wave_ref, jam_ref, share_ref, cells_ref, *refs
 ):
     fore_refs, obs_refs = refs[:GROUP], refs[GROUP : 2 * GROUP]
-    wide_ref, other_ref, side_ref, share_at, cell_ref, sem_ref = refs[2 * GROUP :]
+    wide_ref, side_ref, share_at, cell_ref, sem_ref = refs[2 * GROUP : 2 * GROUP + 5]
+    tiles_ref, strip_ref, road_ref, here_ref, there_ref = refs[2 * GROUP + 5 :]
     rows, width = state_ref.shape
     full = width + 2 * LANES
     main = slice(LANES, LANES + width)
@@ -133,22 +202,7 @@
 
     arrive.wait()
 
-    def half(src, dst):
-        for g in range(rows // 8):
-            at = slice(8 * g, 8 * g + 8)
-            x = src[at, :]
-            cap = side_ref[3:4, :]
-            demand = jnp.minimum(side_ref[0:1, :] * x, cap)
-            supply = jnp.minimum(cap, side_ref[1:2, :] * (side_ref[2:3, :] - x))
-            flux = jnp.minimum(demand, pltpu.roll(supply, full - 1, 1))
-            dst[at, :] = x + pltpu.roll(flux, 1, 1) - flux
-
-    def step(_, carry):
-        half(wide_ref, other_ref)
-        half(other_ref, wide_ref)
-        return carry
-
-    lax.fori_loop(0, TICKS // 2, step, 0)
+    advance(wide_ref, side_ref, tiles_ref, strip_ref, road_ref, here_ref, there_ref)
     starts = [pl.multiple_of(LANES + lax.rem(member + d, GROUP) * CELLS, LANES) for d in range(GROUP)]
     leave = [
         pltpu.make_async_copy(wide_ref.at[:, pl.ds(starts[d], CELLS)], fore_refs[d], sem_ref.at[6 + d])
@@ -190,13 +244,17 @@
         out_specs=(HBM,) * GROUP + (VMEM,) * GROUP,
         scratch_shapes=[
             pltpu.VMEM((rows, width + 2 * LANES), jnp.float32),
-            pltpu.VMEM((rows, width + 2 * LANES), jnp.float32),
             pltpu.VMEM((8, width + 2 * LANES), jnp.float32),
             pltpu.VMEM((1, width), jnp.float32),
             pltpu.VMEM(cells.shape, jnp.int32),
             pltpu.SemaphoreType.DMA((6 + GROUP,)),
+            pltpu.VMEM((rows * (width // LANES + 2), LANES), jnp.float32),
+            pltpu.VMEM((width // LANES + 16, LANES), jnp.float32),
+            pltpu.VMEM((4, SPAN * 8, LANES), jnp.float32),
+            pltpu.VMEM((SPAN * rows // 2, LANES), jnp.float32),
+            pltpu.VMEM((SPAN * rows // 2, LANES), jnp.float32),
         ],
-        compiler_params=room(12),
+        compiler_params=room(14),
         name="forecast",
     )(place, state, near, far, *road, cells)
 
@@ -349,7 +407,8 @@
 
 def update_kernel(place_ref, part0_ref, part1_ref, part2_ref, part3_ref, sums_ref, *refs):
     fore_refs = refs[:GROUP]
-    out_ref, state_ref, sem_ref = refs[GROUP:]
+    out_refs = refs[GROUP : 2 * GROUP]
+    state_ref, sem_ref = refs[2 * GROUP :]
     rows = fore_refs[0].shape[0]
     member = place_ref[0]
     arrive = []
@@ -374,21 +433,50 @@
     mean = jnp.sum(state, axis=0, keepdims=True) / TALLY
     anomaly = state - mean
     dims = (((0,), (0,)), ((), ()))
-    out = mean + lax.dot_general(mixing, anomaly, dims, precision=HIGHEST, preferred_element_type=jnp.float32)
-    for m in range(GROUP):
-        out_ref[m] = out[m * rows : (m + 1) * rows, :]
+    state_ref[...] = mean + lax.dot_general(
+        mixing, anomaly, dims, precision=HIGHEST, preferred_element_type=jnp.float32
+    )
+    for d in range(GROUP):
+        at = pl.multiple_of(lax.rem(member + d, GROUP) * rows, rows)
+        out_refs[d][...] = state_ref[pl.ds(at, rows), :]
 
 
 def update(place, parts, sums, fore):
     return pl.pallas_call(
         update_kernel,
-        out_shape=jax.ShapeDtypeStruct((GROUP,) + fore[0].shape, jnp.float32),
+        out_shape=(jax.ShapeDtypeStruct(fore[0].shape, jnp.float32),) * GROUP,
         in_specs=[SMEM] + [VMEM] * 5 + [HBM] * GROUP,
-        out_specs=VMEM,
+        out_specs=(VMEM,) * GROUP,
         scratch_shapes=[pltpu.VMEM((TALLY, CELLS), jnp.float32), pltpu.SemaphoreType.DMA((GROUP,))],
         compiler_params=room(10),
         name="update",
     )(place, *parts, sums, *fore)
+
+
+def assemble_kernel(place_ref, *refs):
+    out_ref, sem_ref = refs[GROUP:]
+    copies = []
+    for d in range(GROUP):
+        b = lax.rem(place_ref[0] - d + GROUP, GROUP)
+        at = pl.ds(pl.multiple_of(b * CELLS, LANES), CELLS)
+        copies.append(pltpu.make_async_copy(refs[d], out_ref.at[:, at], sem_ref.at[d]))
+    for copy in copies:
+        copy.start()
+    for copy in copies:
+        copy.wait()
+
+
+def assemble(place, pieces):
+    rows = pieces[0].shape[0]
+    return pl.pallas_call(
+        assemble_kernel,
+        out_shape=jax.ShapeDtypeStruct((rows, GROUP * CELLS), jnp.float32),
+        in_specs=[SMEM] + [HBM] * GROUP,
+        out_specs=HBM,
+        scratch_shapes=[pltpu.SemaphoreType.DMA((GROUP,))],
+        compiler_params=room(4),
+        name="assemble",
+    )(place, *pieces)
 
 
 def hold(value):
@@ -433,9 +521,7 @@
     near, far, sums = lax.optimization_barrier((near, far, sums))
     sums = lax.all_to_all(sums, ALL, 0, 0).reshape(GROUP * slabs, LANES)
     parts = exchange(select(place, lists, near, pair, far))
-    out = update(place, parts, sums, fore)
-    out = lax.all_to_all(out, "member", 0, 0)
-    return out.transpose(1, 0, 2).reshape(rows, width)
+    return assemble(place, exchange(update(place, parts, sums, fore)))
 
 
 def solution(mesh):

time: 98.9 us -> 94.8 us (0.959); the launches traced: 98.7 us -> 93.4 us
  blocking collectives: 18.2 us -> 0 us
  waiting for transfers between devices: 11.9 us -> 22.1 us
  starting transfers between devices: 41 us -> 46 us
  Pallas kernels: 26.3 us -> 25 us
  local copies, waits for them, and re-layouts: 1.08 us -> 0.01 us
    all_to_all x1 -> x0, blocking collectives: 18.2 us -> none  [body(): out = lax.all_to_all(out, 'member', 0, 0)]
    ppermute x12 -> x15, waiting for transfers between devices: 9.44 us -> 19.6 us  [exchange(): lax.ppermute(pieces[d], 'member', [(i, (i + d) % GROUP) for i in range(GR...]
    ppermute x12 -> x15, starting transfers between devices: 19.7 us -> 24.7 us  [exchange(): lax.ppermute(pieces[d], 'member', [(i, (i + d) % GROUP) for i in range(GR...]
    pallas_call x1, Pallas kernels: 14 us -> 11 us  [forecast(): pl.pallas_call(forecast_kernel, out_shape=(jax.ShapeDtypeStruct((rows, CE...]
    pallas_call x1 -> x2, Pallas kernels: 6.59 us -> 8.26 us  [the longest x1 6.72 us: update(): pl.pallas_call(update_kernel, out_shape=(jax.ShapeDtypeStruct(fore[0].sha...]
    reshape x1 -> x0, local copies, waits for them, and re-layouts: 1.07 us -> none  [body(): return out.transpose(1, 0, 2).reshape(rows, width)]
  transfers between devices with their start and end apart: 17 -> 20, of which waited for: 7 -> 9; matrix products, arithmetic and copies ran while one was open for 0% -> 0% of each run, Pallas kernels for 18% -> 16%
where the time goes in v4:
time: 94.8 us; the launch traced here: 93.4 us
  starting transfers between devices  46 us (49%)
  Pallas kernels  25 us (26%)
  waiting for transfers between devices  22.1 us (23%)
    ppermute x15, starting transfers between devices, exchange(): lax.ppermute(pieces[d], 'member', [(i, (i + d) % GROUP) for i in range(GR...  24.7 us
    ppermute x15, waiting for transfers between devices, exchange(): lax.ppermute(pieces[d], 'member', [(i, (i + d) % GROUP) for i in range(GR...  19.6 us
    all_to_all x1, starting transfers between devices, body(): sums = lax.all_to_all(sums, ALL, 0, 0).reshape(GROUP * slabs, LANES)  14 us
    pallas_call x1, Pallas kernels, forecast(): pl.pallas_call(forecast_kernel, out_shape=(jax.ShapeDtypeStruct((rows, CE...  11 us
    ppermute x4, starting transfers between devices, swap(): return lax.ppermute(value, RB, up + [(b, a) for a, b in up])  7.34 us
    pallas_call x1, Pallas kernels, update(): pl.pallas_call(update_kernel, out_shape=(jax.ShapeDtypeStruct(fore[0].sha...  6.72 us
    ppermute x4, waiting for transfers between devices, swap(): return lax.ppermute(value, RB, up + [(b, a) for a, b in up])  2.42 us
    pallas_call x1, Pallas kernels, observed_sums(): pl.pallas_call(sums_kernel, out_shape=(jax.ShapeDtypeStruct((GROUP * rows...  2.11 us
  transfers between devices with their start and end apart: 20, of which 9 were waited for; matrix products, arithmetic and copies ran while one was open for 0% of the time, Pallas kernels for 16%

profile of v4, /device:TPU:8, one launch (start us, length us, event | category | flops | bytes accessed | tf_op | source)
XLA Modules:
  0.0 93.4 jit_solution(18285081974164930899)
XLA Ops:
  0.0 0.1 pad_add_fusion.place_ref.refs_0_
  0.1 2.0 %edges.1 = (f32[36,16]{1,0:T(8,128)S(1)}, f32[36,16]{1,0:T(8,128)S(1)}, f32[32,768]{1,0:T(8,128)S(1)}, f32[32,768]{1,0:T(8,128)S(1)}, f32[32,768]{1,0:T(8,128)S(1)}, /*index=5*/f32[32,768]{1,0:T(8,128)S(1)}) custom-call(s32[3]{0:T(128)S(1)} %pad_add_fusion.place_ref.refs_0_, f32[32,8192]{1,0:T(8,128)} %state_ref.3, f32[1,8192]{1,0:T(1,128)} %bitcast.13, ...), custom_call_target="tpu_custom_call" | custom-call | tf_op jit(solution)/shard_map/edges/pallas_call | solution.py:70
  2.1 1.6 %collective-permute-start.5 = (f32[32,768]{1,0:T(8,128)S(1)}, f32[32,768]{1,0:T(8,128)S(1)}, u32[]{:S(2)}, u32[]{:S(2)}) collective-permute-start(f32[32,768]{1,0:T(8,128)S(1)} %get-tuple-element.40), channel_id=1, source_target_pairs={{0,64},{64,128},{128,192},{192,0},{1,65},{65,129},{129,193},{193,1... | collective-permute-start | bytes 294920 | tf_op jit(solution)/shard_map/ppermute | solution.py:488
  3.6 0.8 collective-permute-start
  4.4 4.0 %collective-permute-start.1 = (f32[36,16]{1,0:T(8,128)S(1)}, f32[36,16]{1,0:T(8,128)S(1)}, u32[]{:S(2)}, u32[]{:S(2)}) collective-permute-start(f32[36,16]{1,0:T(8,128)S(1)} %get-tuple-element.34), channel_id=1, source_target_pairs={{1,2},{3,4},{5,6},{7,8},{9,10},{11,12},{13,14},{15,16},{17,18},{19... | collective-permute-start | bytes 6920 | tf_op jit(solution)/shard_map/ppermute | solution.py:496
  8.4 2.8 %collective-permute-start.6 = (f32[32,768]{1,0:T(8,128)S(1)}, f32[32,768]{1,0:T(8,128)S(1)}, u32[]{:S(2)}, u32[]{:S(2)}) collective-permute-start(f32[32,768]{1,0:T(8,128)S(1)} %get-tuple-element.41), channel_id=1, source_target_pairs={{0,128},{64,192},{128,0},{192,64},{1,129},{65,193},{129,1},{193,65... | collective-permute-start | bytes 294920 | tf_op jit(solution)/shard_map/ppermute | solution.py:488
  11.2 1.4 %collective-permute-start.7 = (f32[32,768]{1,0:T(8,128)S(1)}, f32[32,768]{1,0:T(8,128)S(1)}, u32[]{:S(2)}, u32[]{:S(2)}) collective-permute-start(f32[32,768]{1,0:T(8,128)S(1)} %get-tuple-element.42), channel_id=1, source_target_pairs={{0,192},{64,0},{128,64},{192,128},{1,193},{65,1},{129,65},{193,129... | collective-permute-start | bytes 294920 | tf_op jit(solution)/shard_map/ppermute | solution.py:488
  12.6 0.0 collective-permute-done.near_ref
  12.7 0.0 collective-permute-done.1.far_ref
  12.7 0.0 copy-start.1
  12.7 11.0 %forecast.1 = (f32[32,2048]{1,0:T(8,128)S(1)}, f32[32,2048]{1,0:T(8,128)S(1)}, f32[32,2048]{1,0:T(8,128)S(1)}, f32[32,2048]{1,0:T(8,128)S(1)}, f32[6,32,128]{2,1...) custom-call(s32[3]{0:T(128)S(1)} %pad_add_fusion.place_ref.refs_0_, ...), custom_call_target="tpu_custom_call" | custom-call | tf_op jit(solution)/shard_map/forecast/pallas_call | solution.py:240
  23.7 0.0 copy-start
  23.7 0.7 collective-permute-start.2
  24.4 1.4 %collective-permute-start.3 = (f32[6,32,128]{2,1,0:T(8,128)S(1)}, f32[6,32,128]{2,1,0:T(8,128)S(1)}, u32[]{:S(2)}, u32[]{:S(2)}) collective-permute-start(f32[6,32,128]{2,1,0:T(8,128)S(1)} %get-tuple-element.37), channel_id=1, source_target_pairs={{0,128},{64,192},{128,0},{192,64},{1,129},{65,193},{129,1},{193,65... | collective-permute-start | bytes 294920 | tf_op jit(solution)/shard_map/ppermute | solution.py:488
  25.8 0.0 collective-permute-done.5.refs_7_
  25.8 1.3 %collective-permute-start.4 = (f32[6,32,128]{2,1,0:T(8,128)S(1)}, f32[6,32,128]{2,1,0:T(8,128)S(1)}, u32[]{:S(2)}, u32[]{:S(2)}) collective-permute-start(f32[6,32,128]{2,1,0:T(8,128)S(1)} %get-tuple-element.38), channel_id=1, source_target_pairs={{0,192},{64,0},{128,64},{192,128},{1,193},{65,1},{129,65},{193,129... | collective-permute-start | bytes 294920 | tf_op jit(solution)/shard_map/ppermute | solution.py:488
  27.1 0.0 collective-permute-done.6.refs_8_
  27.1 0.8 collective-permute-start.13
  28.0 0.0 collective-permute-done.7.refs_9_
  28.0 3.3 %collective-permute-done.2.refs_3_ = f32[6,32,128]{2,1,0:T(8,128)S(1)} collective-permute-done((f32[6,32,128]{2,1,0:T(8,128)S(1)}, f32[6,32,128]{2,1,0:T(8,128)S(1)}, u32[]{:S(2)}, u32[]{:S(2)}) %collective-permute-start.2) | collective-permute-done | bytes 98336 | tf_op jit(solution)/shard_map/ppermute | solution.py:488
  31.3 0.2 collective-permute-done.3.refs_4_
  31.5 0.0 collective-permute-done.4.refs_5_
  31.6 0.0 copy-done.1
  31.6 0.0 copy-done
  31.6 2.1 %observed_sums.1 = (f32[128,768]{1,0:T(8,128)S(1)}, f32[256,768]{1,0:T(8,128)S(1)}, f32[256,1,128]{2,1,0:T(1,128)}) custom-call(s32[3]{0:T(128)S(1)} %pad_add_fusion.place_ref.refs_0_, s32[4]{0:T(128)} %refs_1_.1, f32[6,32,128]{2,1,0:T(8,128)S(1)} %get-tuple-element.35.refs_2_, f32[6,32,128]{2,1,0:T(8,128)S(1)} %collective-permute-done.2.refs_3_, ...), custom_call_target="tpu_custom_call" | custom-call | tf_op jit(solution)/shard_map/observed_sums/pallas_call | solution.py:305
  33.7 0.9 products.1.pair_ref
  34.6 2.3 %collective-permute-start.9 = (f32[2,128,128]{2,1,0:T(8,128)S(1)}, f32[2,128,128]{2,1,0:T(8,128)S(1)}, u32[]{:S(2)}, u32[]{:S(2)}) collective-permute-start(f32[2,128,128]{2,1,0:T(8,128)S(1)} %products.1.pair_ref), channel_id=1, source_target_pairs={{1,2},{3,4},{5,6},{7,8},{9,10},{11,12},{13,14},{15,16},{17,18},{19... | collective-permute-start | bytes 393224 | tf_op jit(solution)/shard_map/ppermute | solution.py:496
  36.9 0.3 collective-permute-start.8
  37.2 1.9 %collective-permute-start.14 = (f32[32,2048]{1,0:T(8,128)S(1)}, f32[32,2048]{1,0:T(8,128)S(1)}, u32[]{:S(2)}, u32[]{:S(2)}) collective-permute-start(f32[32,2048]{1,0:T(8,128)S(1)} %get-tuple-element.55), channel_id=1, source_target_pairs={{0,128},{64,192},{128,0},{192,64},{1,129},{65,193},{129,1},{193,65... | collective-permute-start | bytes 786440 | tf_op jit(solution)/shard_map/ppermute | solution.py:488
  39.1 2.1 %collective-permute-start.15 = (f32[32,2048]{1,0:T(8,128)S(1)}, f32[32,2048]{1,0:T(8,128)S(1)}, u32[]{:S(2)}, u32[]{:S(2)}) collective-permute-start(f32[32,2048]{1,0:T(8,128)S(1)} %get-tuple-element.56), channel_id=1, source_target_pairs={{0,192},{64,0},{128,64},{192,128},{1,193},{65,1},{129,65},{193,129... | collective-permute-start | bytes 786440 | tf_op jit(solution)/shard_map/ppermute | solution.py:488
  41.1 0.3 collective-permute-done.9.far_ref
  41.5 2.1 %collective-permute-done.8.near_ref = f32[2,128,128]{2,1,0:T(8,128)S(1)} collective-permute-done((f32[2,128,128]{2,1,0:T(8,128)S(1)}, f32[2,128,128]{2,1,0:T(8,128)S(1)}, u32[]{:S(2)}, u32[]{:S(2)}) %collective-permute-start.8) | collective-permute-done | bytes 131104 | tf_op jit(solution)/shard_map/ppermute | solution.py:496
  43.5 0.0 copy-start.2
  43.6 14.0 %all-to-all-start = ((f32[256,1,128]{2,1,0:T(1,128)}), f32[256,1,128]{2,1,0:T(1,128)S(1)}, u32[]{:S(2)}, u32[]{:S(2)}) async-start(f32[256,1,128]{2,1,0:T(1,128)} %get-tuple-element.52), calls=%async_computation | async-start | bytes 262144 | tf_op jit(solution)/shard_map/all_to_all | solution.py:522
  57.5 0.0 copy-done.2
  57.5 0.7 select.1
  58.2 1.5 %collective-permute-start.10 = (f32[2,128,128]{2,1,0:T(8,128)S(1)}, f32[2,128,128]{2,1,0:T(8,128)S(1)}, u32[]{:S(2)}, u32[]{:S(2)}) collective-permute-start(f32[2,128,128]{2,1,0:T(8,128)S(1)} %get-tuple-element.49), channel_id=1, source_target_pairs={{0,64},{64,128},{128,192},{192,0},{1,65},{65,129},{129,193},{193,1... | collective-permute-start | bytes 393224 | tf_op jit(solution)/shard_map/ppermute | solution.py:488
  59.8 2.7 %collective-permute-start.11 = (f32[2,128,128]{2,1,0:T(8,128)S(1)}, f32[2,128,128]{2,1,0:T(8,128)S(1)}, u32[]{:S(2)}, u32[]{:S(2)}) collective-permute-start(f32[2,128,128]{2,1,0:T(8,128)S(1)} %get-tuple-element.50), channel_id=1, source_target_pairs={{0,128},{64,192},{128,0},{192,64},{1,129},{65,193},{129,1},{193,65... | collective-permute-start | bytes 393224 | tf_op jit(solution)/shard_map/ppermute | solution.py:488
  62.5 0.0 collective-permute-done.13.refs_1_
  62.5 1.5 %collective-permute-start.12 = (f32[2,128,128]{2,1,0:T(8,128)S(1)}, f32[2,128,128]{2,1,0:T(8,128)S(1)}, u32[]{:S(2)}, u32[]{:S(2)}) collective-permute-start(f32[2,128,128]{2,1,0:T(8,128)S(1)} %get-tuple-element.51), channel_id=1, source_target_pairs={{0,192},{64,0},{128,64},{192,128},{1,193},{65,1},{129,65},{193,129... | collective-permute-start | bytes 393224 | tf_op jit(solution)/shard_map/ppermute | solution.py:488
  63.9 0.0 collective-permute-done.14.refs_2_
  63.9 0.0 collective-permute-done.15.refs_3_
  63.9 1.9 %collective-permute-done.10.part1_ref = f32[2,128,128]{2,1,0:T(8,128)S(1)} collective-permute-done((f32[2,128,128]{2,1,0:T(8,128)S(1)}, f32[2,128,128]{2,1,0:T(8,128)S(1)}, u32[]{:S(2)}, u32[]{:S(2)}) %collective-permute-start.10) | collective-permute-done | bytes 131104 | tf_op jit(solution)/shard_map/ppermute | solution.py:488
  65.8 3.9 %collective-permute-done.11.part2_ref = f32[2,128,128]{2,1,0:T(8,128)S(1)} collective-permute-done((f32[2,128,128]{2,1,0:T(8,128)S(1)}, f32[2,128,128]{2,1,0:T(8,128)S(1)}, u32[]{:S(2)}, u32[]{:S(2)}) %collective-permute-start.11) | collective-permute-done | bytes 131104 | tf_op jit(solution)/shard_map/ppermute | solution.py:488
  69.8 0.0 collective-permute-done.12.part3_ref
  69.8 0.1 all-to-all-done
  69.8 6.7 %update.1 = (f32[32,2048]{1,0:T(8,128)S(1)}, f32[32,2048]{1,0:T(8,128)S(1)}, f32[32,2048]{1,0:T(8,128)S(1)}, f32[32,2048]{1,0:T(8,128)S(1)}) custom-call(s32[3]{0:T(128)S(1)} %pad_add_fusion.place_ref.refs_0_, f32[2,128,128]{2,1,0:T(8,128)S(1)} %get-tuple-element.48.part0_ref, f32[2,128,128]{2,1,0:T(8,128)S(1)} %collective-permute-done.10.part1_ref, ...), custom_call_target="tpu_custom_call" | custom-call | tf_op jit(solution)/shard_map/update/pallas_call | solution.py:445
  76.5 1.2 %collective-permute-start.16 = (f32[32,2048]{1,0:T(8,128)S(1)}, f32[32,2048]{1,0:T(8,128)S(1)}, u32[]{:S(2)}, u32[]{:S(2)}) collective-permute-start(f32[32,2048]{1,0:T(8,128)S(1)} %get-tuple-element.58), channel_id=1, source_target_pairs={{0,64},{64,128},{128,192},{192,0},{1,65},{65,129},{129,193},{193,1... | collective-permute-start | bytes 786440 | tf_op jit(solution)/shard_map/ppermute | solution.py:488
  77.8 2.3 %collective-permute-start.17 = (f32[32,2048]{1,0:T(8,128)S(1)}, f32[32,2048]{1,0:T(8,128)S(1)}, u32[]{:S(2)}, u32[]{:S(2)}) collective-permute-start(f32[32,2048]{1,0:T(8,128)S(1)} %get-tuple-element.59), channel_id=1, source_target_pairs={{0,128},{64,192},{128,0},{192,64},{1,129},{65,193},{129,1},{193,65... | collective-permute-start | bytes 786440 | tf_op jit(solution)/shard_map/ppermute | solution.py:488
  80.1 1.5 %collective-permute-start.18 = (f32[32,2048]{1,0:T(8,128)S(1)}, f32[32,2048]{1,0:T(8,128)S(1)}, u32[]{:S(2)}, u32[]{:S(2)}) collective-permute-start(f32[32,2048]{1,0:T(8,128)S(1)} %get-tuple-element.60), channel_id=1, source_target_pairs={{0,192},{64,0},{128,64},{192,128},{1,193},{65,1},{129,65},{193,129... | collective-permute-start | bytes 786440 | tf_op jit(solution)/shard_map/ppermute | solution.py:488
  81.6 4.4 %collective-permute-done.16.refs_1_ = f32[32,2048]{1,0:T(8,128)S(1)} collective-permute-done((f32[32,2048]{1,0:T(8,128)S(1)}, f32[32,2048]{1,0:T(8,128)S(1)}, u32[]{:S(2)}, u32[]{:S(2)}) %collective-permute-start.16) | collective-permute-done | bytes 262176 | tf_op jit(solution)/shard_map/ppermute | solution.py:488
  86.0 5.7 %collective-permute-done.17.refs_2_ = f32[32,2048]{1,0:T(8,128)S(1)} collective-permute-done((f32[32,2048]{1,0:T(8,128)S(1)}, f32[32,2048]{1,0:T(8,128)S(1)}, u32[]{:S(2)}, u32[]{:S(2)}) %collective-permute-start.17) | collective-permute-done | bytes 262176 | tf_op jit(solution)/shard_map/ppermute | solution.py:488
  91.7 0.0 collective-permute-done.18.refs_3_
  91.7 1.5 %assemble.1 = f32[32,8192]{1,0:T(8,128)} custom-call(s32[3]{0:T(128)S(1)} %pad_add_fusion.place_ref.refs_0_, f32[32,2048]{1,0:T(8,128)S(1)} %get-tuple-element.57.refs_0_, f32[32,2048]{1,0:T(8,128)S(1)} %collective-permute-done.16.refs_1_, f32[32,2048]{1,0:T(8,128)S(1)} %collective-permute-done.17.refs_2_, f32[32,2048]{1,0:T(8,128)S(1)} %collective-permute-done.18.refs_3_), custom_call_target="tpu_custom_call" | custom-call | tf_op jit(solution)/shard_map/assemble/pallas_call | solution.py:471
Async XLA Ops:
  2.1 23.7 %collective-permute-start.5 = (f32[32,768]{1,0:T(8,128)S(1)}, f32[32,768]{1,0:T(8,128)S(1)}, u32[]{:S(2)}, u32[]{:S(2)}) collective-permute-start(f32[32,768]{1,0:T(8,128)S(1)} %get-tuple-element.40), channel_id=1, source_target_pairs={{0,64},{64,128},{128,192},{192,0},{1,65},{65,129},{129,193},{193,1... | collective-permute-start | bytes 294920 | tf_op jit(solution)/shard_map/ppermute | solution.py:488
  3.6 9.0 %collective-permute-start = (f32[36,16]{1,0:T(8,128)S(1)}, f32[36,16]{1,0:T(8,128)S(1)}, u32[]{:S(2)}, u32[]{:S(2)}) collective-permute-start(f32[36,16]{1,0:T(8,128)S(1)} %get-tuple-element.33), channel_id=1, source_target_pairs={{0,1},{2,3},{4,5},{6,7},{8,9},{10,11},{12,13},{14,15},{16,17},{18,... | collective-permute-start | bytes 6920 | tf_op jit(solution)/shard_map/ppermute | solution.py:496
  4.4 8.2 %collective-permute-start.1 = (f32[36,16]{1,0:T(8,128)S(1)}, f32[36,16]{1,0:T(8,128)S(1)}, u32[]{:S(2)}, u32[]{:S(2)}) collective-permute-start(f32[36,16]{1,0:T(8,128)S(1)} %get-tuple-element.34), channel_id=1, source_target_pairs={{1,2},{3,4},{5,6},{7,8},{9,10},{11,12},{13,14},{15,16},{17,18},{19... | collective-permute-start | bytes 6920 | tf_op jit(solution)/shard_map/ppermute | solution.py:496
  8.4 18.7 %collective-permute-start.6 = (f32[32,768]{1,0:T(8,128)S(1)}, f32[32,768]{1,0:T(8,128)S(1)}, u32[]{:S(2)}, u32[]{:S(2)}) collective-permute-start(f32[32,768]{1,0:T(8,128)S(1)} %get-tuple-element.41), channel_id=1, source_target_pairs={{0,128},{64,192},{128,0},{192,64},{1,129},{65,193},{129,1},{193,65... | collective-permute-start | bytes 294920 | tf_op jit(solution)/shard_map/ppermute | solution.py:488
  11.2 16.7 %collective-permute-start.7 = (f32[32,768]{1,0:T(8,128)S(1)}, f32[32,768]{1,0:T(8,128)S(1)}, u32[]{:S(2)}, u32[]{:S(2)}) collective-permute-start(f32[32,768]{1,0:T(8,128)S(1)} %get-tuple-element.42), channel_id=1, source_target_pairs={{0,192},{64,0},{128,64},{192,128},{1,193},{65,1},{129,65},{193,129... | collective-permute-start | bytes 294920 | tf_op jit(solution)/shard_map/ppermute | solution.py:488
  12.7 18.9 %copy-start.1 = (f32[3072]{0:T(1024)S(1)}, f32[3072]{0:T(1024)}, u32[]{:S(2)}) copy-start(f32[3072]{0:T(1024)} %param.19) | copy-start | bytes 36868
  23.7 7.9 %copy-start = (f32[3072]{0:T(1024)S(1)}, f32[3072]{0:T(1024)}, u32[]{:S(2)}) copy-start(f32[3072]{0:T(1024)} %param.18) | copy-start | bytes 36868
  23.7 7.6 %collective-permute-start.2 = (f32[6,32,128]{2,1,0:T(8,128)S(1)}, f32[6,32,128]{2,1,0:T(8,128)S(1)}, u32[]{:S(2)}, u32[]{:S(2)}) collective-permute-start(f32[6,32,128]{2,1,0:T(8,128)S(1)} %get-tuple-element.36), channel_id=1, source_target_pairs={{0,64},{64,128},{128,192},{192,0},{1,65},{65,129},{129,193},{193,1... | collective-permute-start | bytes 294920 | tf_op jit(solution)/shard_map/ppermute | solution.py:488
  24.4 7.2 %collective-permute-start.3 = (f32[6,32,128]{2,1,0:T(8,128)S(1)}, f32[6,32,128]{2,1,0:T(8,128)S(1)}, u32[]{:S(2)}, u32[]{:S(2)}) collective-permute-start(f32[6,32,128]{2,1,0:T(8,128)S(1)} %get-tuple-element.37), channel_id=1, source_target_pairs={{0,128},{64,192},{128,0},{192,64},{1,129},{65,193},{129,1},{193,65... | collective-permute-start | bytes 294920 | tf_op jit(solution)/shard_map/ppermute | solution.py:488
  25.8 5.8 %collective-permute-start.4 = (f32[6,32,128]{2,1,0:T(8,128)S(1)}, f32[6,32,128]{2,1,0:T(8,128)S(1)}, u32[]{:S(2)}, u32[]{:S(2)}) collective-permute-start(f32[6,32,128]{2,1,0:T(8,128)S(1)} %get-tuple-element.38), channel_id=1, source_target_pairs={{0,192},{64,0},{128,64},{192,128},{1,193},{65,1},{129,65},{193,129... | collective-permute-start | bytes 294920 | tf_op jit(solution)/shard_map/ppermute | solution.py:488
  27.1 35.3 %collective-permute-start.13 = (f32[32,2048]{1,0:T(8,128)S(1)}, f32[32,2048]{1,0:T(8,128)S(1)}, u32[]{:S(2)}, u32[]{:S(2)}) collective-permute-start(f32[32,2048]{1,0:T(8,128)S(1)} %get-tuple-element.54), channel_id=1, source_target_pairs={{0,64},{64,128},{128,192},{192,0},{1,65},{65,129},{129,193},{193,1... | collective-permute-start | bytes 786440 | tf_op jit(solution)/shard_map/ppermute | solution.py:488
  34.6 6.9 %collective-permute-start.9 = (f32[2,128,128]{2,1,0:T(8,128)S(1)}, f32[2,128,128]{2,1,0:T(8,128)S(1)}, u32[]{:S(2)}, u32[]{:S(2)}) collective-permute-start(f32[2,128,128]{2,1,0:T(8,128)S(1)} %products.1.pair_ref), channel_id=1, source_target_pairs={{1,2},{3,4},{5,6},{7,8},{9,10},{11,12},{13,14},{15,16},{17,18},{19... | collective-permute-start | bytes 393224 | tf_op jit(solution)/shard_map/ppermute | solution.py:496
  36.9 6.6 %collective-permute-start.8 = (f32[2,128,128]{2,1,0:T(8,128)S(1)}, f32[2,128,128]{2,1,0:T(8,128)S(1)}, u32[]{:S(2)}, u32[]{:S(2)}) collective-permute-start(f32[2,128,128]{2,1,0:T(8,128)S(1)} %products.1.pair_ref), channel_id=1, source_target_pairs={{0,1},{2,3},{4,5},{6,7},{8,9},{10,11},{12,13},{14,15},{16,17},{18,... | collective-permute-start | bytes 393224 | tf_op jit(solution)/shard_map/ppermute | solution.py:496
  37.2 26.7 %collective-permute-start.14 = (f32[32,2048]{1,0:T(8,128)S(1)}, f32[32,2048]{1,0:T(8,128)S(1)}, u32[]{:S(2)}, u32[]{:S(2)}) collective-permute-start(f32[32,2048]{1,0:T(8,128)S(1)} %get-tuple-element.55), channel_id=1, source_target_pairs={{0,128},{64,192},{128,0},{192,64},{1,129},{65,193},{129,1},{193,65... | collective-permute-start | bytes 786440 | tf_op jit(solution)/shard_map/ppermute | solution.py:488
  39.1 24.9 %collective-permute-start.15 = (f32[32,2048]{1,0:T(8,128)S(1)}, f32[32,2048]{1,0:T(8,128)S(1)}, u32[]{:S(2)}, u32[]{:S(2)}) collective-permute-start(f32[32,2048]{1,0:T(8,128)S(1)} %get-tuple-element.56), channel_id=1, source_target_pairs={{0,192},{64,0},{128,64},{192,128},{1,193},{65,1},{129,65},{193,129... | collective-permute-start | bytes 786440 | tf_op jit(solution)/shard_map/ppermute | solution.py:488
  43.5 14.0 %copy-start.2 = (s32[4,3]{1,0:T(4,128)S(1)}, s32[4,3]{1,0:T(4,128)}, u32[]{:S(2)}) copy-start(s32[4,3]{1,0:T(4,128)} %list_ref.1) | copy-start | bytes 148
  43.6 26.3 %all-to-all-start = ((f32[256,1,128]{2,1,0:T(1,128)}), f32[256,1,128]{2,1,0:T(1,128)S(1)}, u32[]{:S(2)}, u32[]{:S(2)}) async-start(f32[256,1,128]{2,1,0:T(1,128)} %get-tuple-element.52), calls=%async_computation | async-start | bytes 262144 | tf_op jit(solution)/shard_map/all_to_all | solution.py:522
  58.2 7.6 %collective-permute-start.10 = (f32[2,128,128]{2,1,0:T(8,128)S(1)}, f32[2,128,128]{2,1,0:T(8,128)S(1)}, u32[]{:S(2)}, u32[]{:S(2)}) collective-permute-start(f32[2,128,128]{2,1,0:T(8,128)S(1)} %get-tuple-element.49), channel_id=1, source_target_pairs={{0,64},{64,128},{128,192},{192,0},{1,65},{65,129},{129,193},{193,1... | collective-permute-start | bytes 393224 | tf_op jit(solution)/shard_map/ppermute | solution.py:488
  59.8 10.0 %collective-permute-start.11 = (f32[2,128,128]{2,1,0:T(8,128)S(1)}, f32[2,128,128]{2,1,0:T(8,128)S(1)}, u32[]{:S(2)}, u32[]{:S(2)}) collective-permute-start(f32[2,128,128]{2,1,0:T(8,128)S(1)} %get-tuple-element.50), channel_id=1, source_target_pairs={{0,128},{64,192},{128,0},{192,64},{1,129},{65,193},{129,1},{193,65... | collective-permute-start | bytes 393224 | tf_op jit(solution)/shard_map/ppermute | solution.py:488
  62.5 7.3 %collective-permute-start.12 = (f32[2,128,128]{2,1,0:T(8,128)S(1)}, f32[2,128,128]{2,1,0:T(8,128)S(1)}, u32[]{:S(2)}, u32[]{:S(2)}) collective-permute-start(f32[2,128,128]{2,1,0:T(8,128)S(1)} %get-tuple-element.51), channel_id=1, source_target_pairs={{0,192},{64,0},{128,64},{192,128},{1,193},{65,1},{129,65},{193,129... | collective-permute-start | bytes 393224 | tf_op jit(solution)/shard_map/ppermute | solution.py:488
  76.5 9.4 %collective-permute-start.16 = (f32[32,2048]{1,0:T(8,128)S(1)}, f32[32,2048]{1,0:T(8,128)S(1)}, u32[]{:S(2)}, u32[]{:S(2)}) collective-permute-start(f32[32,2048]{1,0:T(8,128)S(1)} %get-tuple-element.58), channel_id=1, source_target_pairs={{0,64},{64,128},{128,192},{192,0},{1,65},{65,129},{129,193},{193,1... | collective-permute-start | bytes 786440 | tf_op jit(solution)/shard_map/ppermute | solution.py:488
  77.8 13.9 %collective-permute-start.17 = (f32[32,2048]{1,0:T(8,128)S(1)}, f32[32,2048]{1,0:T(8,128)S(1)}, u32[]{:S(2)}, u32[]{:S(2)}) collective-permute-start(f32[32,2048]{1,0:T(8,128)S(1)} %get-tuple-element.59), channel_id=1, source_target_pairs={{0,128},{64,192},{128,0},{192,64},{1,129},{65,193},{129,1},{193,65... | collective-permute-start | bytes 786440 | tf_op jit(solution)/shard_map/ppermute | solution.py:488
  80.1 11.6 %collective-permute-start.18 = (f32[32,2048]{1,0:T(8,128)S(1)}, f32[32,2048]{1,0:T(8,128)S(1)}, u32[]{:S(2)}, u32[]{:S(2)}) collective-permute-start(f32[32,2048]{1,0:T(8,128)S(1)} %get-tuple-element.60), channel_id=1, source_target_pairs={{0,192},{64,0},{128,64},{192,128},{1,193},{65,1},{129,65},{193,129... | collective-permute-start | bytes 786440 | tf_op jit(solution)/shard_map/ppermute | solution.py:488

commit v5 on v4

--- a/solution.py
+++ b/solution.py
@@ -297,7 +297,7 @@
     sum_a = jnp.sum(total_a, axis=1, keepdims=True)
     sum_b = jnp.sum(total_b, axis=1, keepdims=True)
     sums = jnp.where(lane == 0, sum_a, jnp.where(lane == 1, sum_b, 0.0))
-    sum_ref[...] = jnp.broadcast_to(sums[None], sum_ref.shape)
+    sum_ref[...] = jnp.broadcast_to(sums, sum_ref.shape)
 
 
 def observed_sums(place, count, obs, noise, value, variance, copies):
@@ -307,7 +307,7 @@
         out_shape=(
             jax.ShapeDtypeStruct((GROUP * rows, SLOTS), jnp.float32),
             jax.ShapeDtypeStruct((2 * GROUP * rows, SLOTS), jnp.float32),
-            jax.ShapeDtypeStruct((copies, 1, LANES), jnp.float32),
+            jax.ShapeDtypeStruct((copies, LANES), jnp.float32),
         ),
         in_specs=[SMEM, HBM] + [VMEM] * (2 * GROUP + 2),
         out_specs=(VMEM,) * 3,
@@ -405,6 +405,11 @@
     return tiles
 
 
+def halves(value):
+    high = value.astype(jnp.bfloat16)
+    return high, (value - high.astype(jnp.float32)).astype(jnp.bfloat16)
+
+
 def update_kernel(place_ref, part0_ref, part1_ref, part2_ref, part3_ref, sums_ref, *refs):
     fore_refs = refs[:GROUP]
     out_refs = refs[GROUP : 2 * GROUP]
@@ -433,9 +438,11 @@
     mean = jnp.sum(state, axis=0, keepdims=True) / TALLY
     anomaly = state - mean
     dims = (((0,), (0,)), ((), ()))
-    state_ref[...] = mean + lax.dot_general(
-        mixing, anomaly, dims, precision=HIGHEST, preferred_element_type=jnp.float32
-    )
+    mix_high, mix_low = halves(mixing)
+    high, low = halves(anomaly)
+    first = lax.dot_general(mix_high, low, dims, preferred_element_type=jnp.float32)
+    first += lax.dot_general(mix_low, high, dims, preferred_element_type=jnp.float32)
+    state_ref[...] = mean + (first + lax.dot_general(mix_high, high, dims, preferred_element_type=jnp.float32))
     for d in range(GROUP):
         at = pl.multiple_of(lax.rem(member + d, GROUP) * rows, rows)
         out_refs[d][...] = state_ref[pl.ds(at, rows), :]
@@ -519,7 +526,7 @@
     pair = products(left, right)
     near, far = swap(pair, 0), swap(pair, 1)
     near, far, sums = lax.optimization_barrier((near, far, sums))
-    sums = lax.all_to_all(sums, ALL, 0, 0).reshape(GROUP * slabs, LANES)
+    sums = lax.all_to_all(sums[:, None], ALL, 0, 0).reshape(GROUP * slabs, LANES)
     parts = exchange(select(place, lists, near, pair, far))
     return assemble(place, exchange(update(place, parts, sums, fore)))
 

time: 94.8 us -> 94.3 us (level)
  no operation moved by 1% of the time
where the time goes in v5:
time: 94.3 us; the launch traced here: 92.9 us
  starting transfers between devices  46.2 us (49%)
  Pallas kernels  24.5 us (26%)
  waiting for transfers between devices  21.9 us (23%)
    ppermute x15, starting transfers between devices, exchange(): lax.ppermute(pieces[d], 'member', [(i, (i + d) % GROUP) for i in range(GR...  24.9 us
    ppermute x15, waiting for transfers between devices, exchange(): lax.ppermute(pieces[d], 'member', [(i, (i + d) % GROUP) for i in range(GR...  19.6 us
    all_to_all x1, starting transfers between devices, body(): lax.all_to_all(sums[:, None], ALL, 0, 0).reshape(GROUP * slabs, LANES)  14.2 us
    pallas_call x1, Pallas kernels, forecast(): pl.pallas_call(forecast_kernel, out_shape=(jax.ShapeDtypeStruct((rows, CE...  11 us
    ppermute x4, starting transfers between devices, swap(): return lax.ppermute(value, RB, up + [(b, a) for a, b in up])  7.15 us
    pallas_call x1, Pallas kernels, update(): pl.pallas_call(update_kernel, out_shape=(jax.ShapeDtypeStruct(fore[0].sha...  6.27 us
    ppermute x4, waiting for transfers between devices, swap(): return lax.ppermute(value, RB, up + [(b, a) for a, b in up])  2.24 us
    pallas_call x1, Pallas kernels, observed_sums(): pl.pallas_call(sums_kernel, out_shape=(jax.ShapeDtypeStruct((GROUP * rows...  2.06 us
  transfers between devices with their start and end apart: 20, of which 9 were waited for; matrix products, arithmetic and copies ran while one was open for 0% of the time, Pallas kernels for 16%

profile of v5, /device:TPU:8, one launch (start us, length us, event | category | flops | bytes accessed | tf_op | source)
XLA Modules:
  0.0 92.9 jit_solution(3958568885155601193)
XLA Ops:
  0.0 0.1 pad_add_fusion.place_ref.refs_0_
  0.1 2.0 %edges.1 = (f32[36,16]{1,0:T(8,128)S(1)}, f32[36,16]{1,0:T(8,128)S(1)}, f32[32,768]{1,0:T(8,128)S(1)}, f32[32,768]{1,0:T(8,128)S(1)}, f32[32,768]{1,0:T(8,128)S(1)}, /*index=5*/f32[32,768]{1,0:T(8,128)S(1)}) custom-call(s32[3]{0:T(128)S(1)} %pad_add_fusion.place_ref.refs_0_, f32[32,8192]{1,0:T(8,128)} %state_ref.3, f32[1,8192]{1,0:T(1,128)} %bitcast.16, ...), custom_call_target="tpu_custom_call" | custom-call | tf_op jit(solution)/shard_map/edges/pallas_call | solution.py:70
  2.1 1.6 %collective-permute-start.5 = (f32[32,768]{1,0:T(8,128)S(1)}, f32[32,768]{1,0:T(8,128)S(1)}, u32[]{:S(2)}, u32[]{:S(2)}) collective-permute-start(f32[32,768]{1,0:T(8,128)S(1)} %get-tuple-element.40), channel_id=1, source_target_pairs={{0,64},{64,128},{128,192},{192,0},{1,65},{65,129},{129,193},{193,1... | collective-permute-start | bytes 294920 | tf_op jit(solution)/shard_map/ppermute | solution.py:495
  3.6 0.8 collective-permute-start
  4.4 4.0 %collective-permute-start.1 = (f32[36,16]{1,0:T(8,128)S(1)}, f32[36,16]{1,0:T(8,128)S(1)}, u32[]{:S(2)}, u32[]{:S(2)}) collective-permute-start(f32[36,16]{1,0:T(8,128)S(1)} %get-tuple-element.34), channel_id=1, source_target_pairs={{1,2},{3,4},{5,6},{7,8},{9,10},{11,12},{13,14},{15,16},{17,18},{19... | collective-permute-start | bytes 6920 | tf_op jit(solution)/shard_map/ppermute | solution.py:503
  8.4 2.8 %collective-permute-start.6 = (f32[32,768]{1,0:T(8,128)S(1)}, f32[32,768]{1,0:T(8,128)S(1)}, u32[]{:S(2)}, u32[]{:S(2)}) collective-permute-start(f32[32,768]{1,0:T(8,128)S(1)} %get-tuple-element.41), channel_id=1, source_target_pairs={{0,128},{64,192},{128,0},{192,64},{1,129},{65,193},{129,1},{193,65... | collective-permute-start | bytes 294920 | tf_op jit(solution)/shard_map/ppermute | solution.py:495
  11.2 1.4 %collective-permute-start.7 = (f32[32,768]{1,0:T(8,128)S(1)}, f32[32,768]{1,0:T(8,128)S(1)}, u32[]{:S(2)}, u32[]{:S(2)}) collective-permute-start(f32[32,768]{1,0:T(8,128)S(1)} %get-tuple-element.42), channel_id=1, source_target_pairs={{0,192},{64,0},{128,64},{192,128},{1,193},{65,1},{129,65},{193,129... | collective-permute-start | bytes 294920 | tf_op jit(solution)/shard_map/ppermute | solution.py:495
  12.6 0.0 collective-permute-done.near_ref
  12.7 0.0 collective-permute-done.1.far_ref
  12.7 0.0 copy-start.1
  12.7 11.0 %forecast.1 = (f32[32,2048]{1,0:T(8,128)S(1)}, f32[32,2048]{1,0:T(8,128)S(1)}, f32[32,2048]{1,0:T(8,128)S(1)}, f32[32,2048]{1,0:T(8,128)S(1)}, f32[6,32,128]{2,1...) custom-call(s32[3]{0:T(128)S(1)} %pad_add_fusion.place_ref.refs_0_, ...), custom_call_target="tpu_custom_call" | custom-call | tf_op jit(solution)/shard_map/forecast/pallas_call | solution.py:240
  23.7 0.0 copy-start
  23.7 0.7 collective-permute-start.2
  24.4 1.4 %collective-permute-start.3 = (f32[6,32,128]{2,1,0:T(8,128)S(1)}, f32[6,32,128]{2,1,0:T(8,128)S(1)}, u32[]{:S(2)}, u32[]{:S(2)}) collective-permute-start(f32[6,32,128]{2,1,0:T(8,128)S(1)} %get-tuple-element.37), channel_id=1, source_target_pairs={{0,128},{64,192},{128,0},{192,64},{1,129},{65,193},{129,1},{193,65... | collective-permute-start | bytes 294920 | tf_op jit(solution)/shard_map/ppermute | solution.py:495
  25.8 0.0 collective-permute-done.5.refs_7_
  25.8 1.3 %collective-permute-start.4 = (f32[6,32,128]{2,1,0:T(8,128)S(1)}, f32[6,32,128]{2,1,0:T(8,128)S(1)}, u32[]{:S(2)}, u32[]{:S(2)}) collective-permute-start(f32[6,32,128]{2,1,0:T(8,128)S(1)} %get-tuple-element.38), channel_id=1, source_target_pairs={{0,192},{64,0},{128,64},{192,128},{1,193},{65,1},{129,65},{193,129... | collective-permute-start | bytes 294920 | tf_op jit(solution)/shard_map/ppermute | solution.py:495
  27.1 0.0 collective-permute-done.6.refs_8_
  27.1 0.8 collective-permute-start.13
  28.0 0.0 collective-permute-done.7.refs_9_
  28.0 3.3 %collective-permute-done.2.refs_3_ = f32[6,32,128]{2,1,0:T(8,128)S(1)} collective-permute-done((f32[6,32,128]{2,1,0:T(8,128)S(1)}, f32[6,32,128]{2,1,0:T(8,128)S(1)}, u32[]{:S(2)}, u32[]{:S(2)}) %collective-permute-start.2) | collective-permute-done | bytes 98336 | tf_op jit(solution)/shard_map/ppermute | solution.py:495
  31.3 0.2 collective-permute-done.3.refs_4_
  31.5 0.0 collective-permute-done.4.refs_5_
  31.6 0.0 copy-done.1
  31.6 0.0 copy-done
  31.6 2.1 %observed_sums.1 = (f32[128,768]{1,0:T(8,128)S(1)}, f32[256,768]{1,0:T(8,128)S(1)}, f32[256,128]{1,0:T(8,128)}) custom-call(s32[3]{0:T(128)S(1)} %pad_add_fusion.place_ref.refs_0_, s32[4]{0:T(128)} %refs_1_.1, f32[6,32,128]{2,1,0:T(8,128)S(1)} %get-tuple-element.35.refs_2_, f32[6,32,128]{2,1,0:T(8,128)S(1)} %collective-permute-done.2.refs_3_, ...), custom_call_target="tpu_custom_call" | custom-call | tf_op jit(solution)/shard_map/observed_sums/pallas_call | solution.py:305
  33.6 0.9 products.1.pair_ref
  34.5 2.3 %collective-permute-start.9 = (f32[2,128,128]{2,1,0:T(8,128)S(1)}, f32[2,128,128]{2,1,0:T(8,128)S(1)}, u32[]{:S(2)}, u32[]{:S(2)}) collective-permute-start(f32[2,128,128]{2,1,0:T(8,128)S(1)} %products.1.pair_ref), channel_id=1, source_target_pairs={{1,2},{3,4},{5,6},{7,8},{9,10},{11,12},{13,14},{15,16},{17,18},{19... | collective-permute-start | bytes 393224 | tf_op jit(solution)/shard_map/ppermute | solution.py:503
  36.9 0.1 collective-permute-start.8
  37.0 2.0 %collective-permute-start.14 = (f32[32,2048]{1,0:T(8,128)S(1)}, f32[32,2048]{1,0:T(8,128)S(1)}, u32[]{:S(2)}, u32[]{:S(2)}) collective-permute-start(f32[32,2048]{1,0:T(8,128)S(1)} %get-tuple-element.55), channel_id=1, source_target_pairs={{0,128},{64,192},{128,0},{192,64},{1,129},{65,193},{129,1},{193,65... | collective-permute-start | bytes 786440 | tf_op jit(solution)/shard_map/ppermute | solution.py:495
  39.0 2.1 %collective-permute-start.15 = (f32[32,2048]{1,0:T(8,128)S(1)}, f32[32,2048]{1,0:T(8,128)S(1)}, u32[]{:S(2)}, u32[]{:S(2)}) collective-permute-start(f32[32,2048]{1,0:T(8,128)S(1)} %get-tuple-element.56), channel_id=1, source_target_pairs={{0,192},{64,0},{128,64},{192,128},{1,193},{65,1},{129,65},{193,129... | collective-permute-start | bytes 786440 | tf_op jit(solution)/shard_map/ppermute | solution.py:495
  41.1 0.3 collective-permute-done.9.far_ref
  41.4 1.9 %collective-permute-done.8.near_ref = f32[2,128,128]{2,1,0:T(8,128)S(1)} collective-permute-done((f32[2,128,128]{2,1,0:T(8,128)S(1)}, f32[2,128,128]{2,1,0:T(8,128)S(1)}, u32[]{:S(2)}, u32[]{:S(2)}) %collective-permute-start.8) | collective-permute-done | bytes 131104 | tf_op jit(solution)/shard_map/ppermute | solution.py:503
  43.3 0.0 copy-start.2
  43.3 14.2 %all-to-all-start = ((f32[256,1,128]{2,1,0:T(1,128)}), f32[256,1,128]{2,1,0:T(1,128)S(1)}, u32[]{:S(2)}, u32[]{:S(2)}) async-start(f32[256,1,128]{2,1,0:T(1,128)} %bitcast.10), calls=%async_computation | async-start | bytes 262144 | tf_op jit(solution)/shard_map/all_to_all | solution.py:529
  57.5 0.0 copy-done.2
  57.5 0.7 select.1
  58.2 1.5 %collective-permute-start.10 = (f32[2,128,128]{2,1,0:T(8,128)S(1)}, f32[2,128,128]{2,1,0:T(8,128)S(1)}, u32[]{:S(2)}, u32[]{:S(2)}) collective-permute-start(f32[2,128,128]{2,1,0:T(8,128)S(1)} %get-tuple-element.49), channel_id=1, source_target_pairs={{0,64},{64,128},{128,192},{192,0},{1,65},{65,129},{129,193},{193,1... | collective-permute-start | bytes 393224 | tf_op jit(solution)/shard_map/ppermute | solution.py:495
  59.7 2.7 %collective-permute-start.11 = (f32[2,128,128]{2,1,0:T(8,128)S(1)}, f32[2,128,128]{2,1,0:T(8,128)S(1)}, u32[]{:S(2)}, u32[]{:S(2)}) collective-permute-start(f32[2,128,128]{2,1,0:T(8,128)S(1)} %get-tuple-element.50), channel_id=1, source_target_pairs={{0,128},{64,192},{128,0},{192,64},{1,129},{65,193},{129,1},{193,65... | collective-permute-start | bytes 393224 | tf_op jit(solution)/shard_map/ppermute | solution.py:495
  62.4 0.0 collective-permute-done.13.refs_1_
  62.4 1.5 %collective-permute-start.12 = (f32[2,128,128]{2,1,0:T(8,128)S(1)}, f32[2,128,128]{2,1,0:T(8,128)S(1)}, u32[]{:S(2)}, u32[]{:S(2)}) collective-permute-start(f32[2,128,128]{2,1,0:T(8,128)S(1)} %get-tuple-element.51), channel_id=1, source_target_pairs={{0,192},{64,0},{128,64},{192,128},{1,193},{65,1},{129,65},{193,129... | collective-permute-start | bytes 393224 | tf_op jit(solution)/shard_map/ppermute | solution.py:495
  63.9 0.0 collective-permute-done.14.refs_2_
  63.9 0.0 collective-permute-done.15.refs_3_
  63.9 1.9 %collective-permute-done.10.part1_ref = f32[2,128,128]{2,1,0:T(8,128)S(1)} collective-permute-done((f32[2,128,128]{2,1,0:T(8,128)S(1)}, f32[2,128,128]{2,1,0:T(8,128)S(1)}, u32[]{:S(2)}, u32[]{:S(2)}) %collective-permute-start.10) | collective-permute-done | bytes 131104 | tf_op jit(solution)/shard_map/ppermute | solution.py:495
  65.8 3.9 %collective-permute-done.11.part2_ref = f32[2,128,128]{2,1,0:T(8,128)S(1)} collective-permute-done((f32[2,128,128]{2,1,0:T(8,128)S(1)}, f32[2,128,128]{2,1,0:T(8,128)S(1)}, u32[]{:S(2)}, u32[]{:S(2)}) %collective-permute-start.11) | collective-permute-done | bytes 131104 | tf_op jit(solution)/shard_map/ppermute | solution.py:495
  69.7 0.0 collective-permute-done.12.part3_ref
  69.7 0.1 all-to-all-done
  69.8 6.3 %update.1 = (f32[32,2048]{1,0:T(8,128)S(1)}, f32[32,2048]{1,0:T(8,128)S(1)}, f32[32,2048]{1,0:T(8,128)S(1)}, f32[32,2048]{1,0:T(8,128)S(1)}) custom-call(s32[3]{0:T(128)S(1)} %pad_add_fusion.place_ref.refs_0_, f32[2,128,128]{2,1,0:T(8,128)S(1)} %get-tuple-element.48.part0_ref, f32[2,128,128]{2,1,0:T(8,128)S(1)} %collective-permute-done.10.part1_ref, ...), custom_call_target="tpu_custom_call" | custom-call | tf_op jit(solution)/shard_map/update/pallas_call | solution.py:452
  76.0 1.2 %collective-permute-start.16 = (f32[32,2048]{1,0:T(8,128)S(1)}, f32[32,2048]{1,0:T(8,128)S(1)}, u32[]{:S(2)}, u32[]{:S(2)}) collective-permute-start(f32[32,2048]{1,0:T(8,128)S(1)} %get-tuple-element.58), channel_id=1, source_target_pairs={{0,64},{64,128},{128,192},{192,0},{1,65},{65,129},{129,193},{193,1... | collective-permute-start | bytes 786440 | tf_op jit(solution)/shard_map/ppermute | solution.py:495
  77.3 2.3 %collective-permute-start.17 = (f32[32,2048]{1,0:T(8,128)S(1)}, f32[32,2048]{1,0:T(8,128)S(1)}, u32[]{:S(2)}, u32[]{:S(2)}) collective-permute-start(f32[32,2048]{1,0:T(8,128)S(1)} %get-tuple-element.59), channel_id=1, source_target_pairs={{0,128},{64,192},{128,0},{192,64},{1,129},{65,193},{129,1},{193,65... | collective-permute-start | bytes 786440 | tf_op jit(solution)/shard_map/ppermute | solution.py:495
  79.6 1.5 %collective-permute-start.18 = (f32[32,2048]{1,0:T(8,128)S(1)}, f32[32,2048]{1,0:T(8,128)S(1)}, u32[]{:S(2)}, u32[]{:S(2)}) collective-permute-start(f32[32,2048]{1,0:T(8,128)S(1)} %get-tuple-element.60), channel_id=1, source_target_pairs={{0,192},{64,0},{128,64},{192,128},{1,193},{65,1},{129,65},{193,129... | collective-permute-start | bytes 786440 | tf_op jit(solution)/shard_map/ppermute | solution.py:495
  81.1 4.4 %collective-permute-done.16.refs_1_ = f32[32,2048]{1,0:T(8,128)S(1)} collective-permute-done((f32[32,2048]{1,0:T(8,128)S(1)}, f32[32,2048]{1,0:T(8,128)S(1)}, u32[]{:S(2)}, u32[]{:S(2)}) %collective-permute-start.16) | collective-permute-done | bytes 262176 | tf_op jit(solution)/shard_map/ppermute | solution.py:495
  85.5 5.7 %collective-permute-done.17.refs_2_ = f32[32,2048]{1,0:T(8,128)S(1)} collective-permute-done((f32[32,2048]{1,0:T(8,128)S(1)}, f32[32,2048]{1,0:T(8,128)S(1)}, u32[]{:S(2)}, u32[]{:S(2)}) %collective-permute-start.17) | collective-permute-done | bytes 262176 | tf_op jit(solution)/shard_map/ppermute | solution.py:495
  91.2 0.0 collective-permute-done.18.refs_3_
  91.2 1.5 %assemble.1 = f32[32,8192]{1,0:T(8,128)} custom-call(s32[3]{0:T(128)S(1)} %pad_add_fusion.place_ref.refs_0_, f32[32,2048]{1,0:T(8,128)S(1)} %get-tuple-element.57.refs_0_, f32[32,2048]{1,0:T(8,128)S(1)} %collective-permute-done.16.refs_1_, f32[32,2048]{1,0:T(8,128)S(1)} %collective-permute-done.17.refs_2_, f32[32,2048]{1,0:T(8,128)S(1)} %collective-permute-done.18.refs_3_), custom_call_target="tpu_custom_call" | custom-call | tf_op jit(solution)/shard_map/assemble/pallas_call | solution.py:478
Async XLA Ops:
  2.1 23.7 %collective-permute-start.5 = (f32[32,768]{1,0:T(8,128)S(1)}, f32[32,768]{1,0:T(8,128)S(1)}, u32[]{:S(2)}, u32[]{:S(2)}) collective-permute-start(f32[32,768]{1,0:T(8,128)S(1)} %get-tuple-element.40), channel_id=1, source_target_pairs={{0,64},{64,128},{128,192},{192,0},{1,65},{65,129},{129,193},{193,1... | collective-permute-start | bytes 294920 | tf_op jit(solution)/shard_map/ppermute | solution.py:495
  3.6 9.0 %collective-permute-start = (f32[36,16]{1,0:T(8,128)S(1)}, f32[36,16]{1,0:T(8,128)S(1)}, u32[]{:S(2)}, u32[]{:S(2)}) collective-permute-start(f32[36,16]{1,0:T(8,128)S(1)} %get-tuple-element.33), channel_id=1, source_target_pairs={{0,1},{2,3},{4,5},{6,7},{8,9},{10,11},{12,13},{14,15},{16,17},{18,... | collective-permute-start | bytes 6920 | tf_op jit(solution)/shard_map/ppermute | solution.py:503
  4.4 8.2 %collective-permute-start.1 = (f32[36,16]{1,0:T(8,128)S(1)}, f32[36,16]{1,0:T(8,128)S(1)}, u32[]{:S(2)}, u32[]{:S(2)}) collective-permute-start(f32[36,16]{1,0:T(8,128)S(1)} %get-tuple-element.34), channel_id=1, source_target_pairs={{1,2},{3,4},{5,6},{7,8},{9,10},{11,12},{13,14},{15,16},{17,18},{19... | collective-permute-start | bytes 6920 | tf_op jit(solution)/shard_map/ppermute | solution.py:503
  8.4 18.7 %collective-permute-start.6 = (f32[32,768]{1,0:T(8,128)S(1)}, f32[32,768]{1,0:T(8,128)S(1)}, u32[]{:S(2)}, u32[]{:S(2)}) collective-permute-start(f32[32,768]{1,0:T(8,128)S(1)} %get-tuple-element.41), channel_id=1, source_target_pairs={{0,128},{64,192},{128,0},{192,64},{1,129},{65,193},{129,1},{193,65... | collective-permute-start | bytes 294920 | tf_op jit(solution)/shard_map/ppermute | solution.py:495
  11.2 16.7 %collective-permute-start.7 = (f32[32,768]{1,0:T(8,128)S(1)}, f32[32,768]{1,0:T(8,128)S(1)}, u32[]{:S(2)}, u32[]{:S(2)}) collective-permute-start(f32[32,768]{1,0:T(8,128)S(1)} %get-tuple-element.42), channel_id=1, source_target_pairs={{0,192},{64,0},{128,64},{192,128},{1,193},{65,1},{129,65},{193,129... | collective-permute-start | bytes 294920 | tf_op jit(solution)/shard_map/ppermute | solution.py:495
  12.7 18.9 %copy-start.1 = (f32[3072]{0:T(1024)S(1)}, f32[3072]{0:T(1024)}, u32[]{:S(2)}) copy-start(f32[3072]{0:T(1024)} %param.19) | copy-start | bytes 36868
  23.7 7.9 %copy-start = (f32[3072]{0:T(1024)S(1)}, f32[3072]{0:T(1024)}, u32[]{:S(2)}) copy-start(f32[3072]{0:T(1024)} %param.18) | copy-start | bytes 36868
  23.7 7.6 %collective-permute-start.2 = (f32[6,32,128]{2,1,0:T(8,128)S(1)}, f32[6,32,128]{2,1,0:T(8,128)S(1)}, u32[]{:S(2)}, u32[]{:S(2)}) collective-permute-start(f32[6,32,128]{2,1,0:T(8,128)S(1)} %get-tuple-element.36), channel_id=1, source_target_pairs={{0,64},{64,128},{128,192},{192,0},{1,65},{65,129},{129,193},{193,1... | collective-permute-start | bytes 294920 | tf_op jit(solution)/shard_map/ppermute | solution.py:495
  24.4 7.2 %collective-permute-start.3 = (f32[6,32,128]{2,1,0:T(8,128)S(1)}, f32[6,32,128]{2,1,0:T(8,128)S(1)}, u32[]{:S(2)}, u32[]{:S(2)}) collective-permute-start(f32[6,32,128]{2,1,0:T(8,128)S(1)} %get-tuple-element.37), channel_id=1, source_target_pairs={{0,128},{64,192},{128,0},{192,64},{1,129},{65,193},{129,1},{193,65... | collective-permute-start | bytes 294920 | tf_op jit(solution)/shard_map/ppermute | solution.py:495
  25.8 5.8 %collective-permute-start.4 = (f32[6,32,128]{2,1,0:T(8,128)S(1)}, f32[6,32,128]{2,1,0:T(8,128)S(1)}, u32[]{:S(2)}, u32[]{:S(2)}) collective-permute-start(f32[6,32,128]{2,1,0:T(8,128)S(1)} %get-tuple-element.38), channel_id=1, source_target_pairs={{0,192},{64,0},{128,64},{192,128},{1,193},{65,1},{129,65},{193,129... | collective-permute-start | bytes 294920 | tf_op jit(solution)/shard_map/ppermute | solution.py:495
  27.1 35.3 %collective-permute-start.13 = (f32[32,2048]{1,0:T(8,128)S(1)}, f32[32,2048]{1,0:T(8,128)S(1)}, u32[]{:S(2)}, u32[]{:S(2)}) collective-permute-start(f32[32,2048]{1,0:T(8,128)S(1)} %get-tuple-element.54), channel_id=1, source_target_pairs={{0,64},{64,128},{128,192},{192,0},{1,65},{65,129},{129,193},{193,1... | collective-permute-start | bytes 786440 | tf_op jit(solution)/shard_map/ppermute | solution.py:495
  34.5 6.9 %collective-permute-start.9 = (f32[2,128,128]{2,1,0:T(8,128)S(1)}, f32[2,128,128]{2,1,0:T(8,128)S(1)}, u32[]{:S(2)}, u32[]{:S(2)}) collective-permute-start(f32[2,128,128]{2,1,0:T(8,128)S(1)} %products.1.pair_ref), channel_id=1, source_target_pairs={{1,2},{3,4},{5,6},{7,8},{9,10},{11,12},{13,14},{15,16},{17,18},{19... | collective-permute-start | bytes 393224 | tf_op jit(solution)/shard_map/ppermute | solution.py:503
  36.9 6.4 %collective-permute-start.8 = (f32[2,128,128]{2,1,0:T(8,128)S(1)}, f32[2,128,128]{2,1,0:T(8,128)S(1)}, u32[]{:S(2)}, u32[]{:S(2)}) collective-permute-start(f32[2,128,128]{2,1,0:T(8,128)S(1)} %products.1.pair_ref), channel_id=1, source_target_pairs={{0,1},{2,3},{4,5},{6,7},{8,9},{10,11},{12,13},{14,15},{16,17},{18,... | collective-permute-start | bytes 393224 | tf_op jit(solution)/shard_map/ppermute | solution.py:503
  37.0 26.9 %collective-permute-start.14 = (f32[32,2048]{1,0:T(8,128)S(1)}, f32[32,2048]{1,0:T(8,128)S(1)}, u32[]{:S(2)}, u32[]{:S(2)}) collective-permute-start(f32[32,2048]{1,0:T(8,128)S(1)} %get-tuple-element.55), channel_id=1, source_target_pairs={{0,128},{64,192},{128,0},{192,64},{1,129},{65,193},{129,1},{193,65... | collective-permute-start | bytes 786440 | tf_op jit(solution)/shard_map/ppermute | solution.py:495
  39.0 24.9 %collective-permute-start.15 = (f32[32,2048]{1,0:T(8,128)S(1)}, f32[32,2048]{1,0:T(8,128)S(1)}, u32[]{:S(2)}, u32[]{:S(2)}) collective-permute-start(f32[32,2048]{1,0:T(8,128)S(1)} %get-tuple-element.56), channel_id=1, source_target_pairs={{0,192},{64,0},{128,64},{192,128},{1,193},{65,1},{129,65},{193,129... | collective-permute-start | bytes 786440 | tf_op jit(solution)/shard_map/ppermute | solution.py:495
  43.3 14.2 %copy-start.2 = (s32[4,3]{1,0:T(4,128)S(1)}, s32[4,3]{1,0:T(4,128)}, u32[]{:S(2)}) copy-start(s32[4,3]{1,0:T(4,128)} %list_ref.1) | copy-start | bytes 148
  43.3 26.5 %all-to-all-start = ((f32[256,1,128]{2,1,0:T(1,128)}), f32[256,1,128]{2,1,0:T(1,128)S(1)}, u32[]{:S(2)}, u32[]{:S(2)}) async-start(f32[256,1,128]{2,1,0:T(1,128)} %bitcast.10), calls=%async_computation | async-start | bytes 262144 | tf_op jit(solution)/shard_map/all_to_all | solution.py:529
  58.2 7.6 %collective-permute-start.10 = (f32[2,128,128]{2,1,0:T(8,128)S(1)}, f32[2,128,128]{2,1,0:T(8,128)S(1)}, u32[]{:S(2)}, u32[]{:S(2)}) collective-permute-start(f32[2,128,128]{2,1,0:T(8,128)S(1)} %get-tuple-element.49), channel_id=1, source_target_pairs={{0,64},{64,128},{128,192},{192,0},{1,65},{65,129},{129,193},{193,1... | collective-permute-start | bytes 393224 | tf_op jit(solution)/shard_map/ppermute | solution.py:495
  59.7 10.0 %collective-permute-start.11 = (f32[2,128,128]{2,1,0:T(8,128)S(1)}, f32[2,128,128]{2,1,0:T(8,128)S(1)}, u32[]{:S(2)}, u32[]{:S(2)}) collective-permute-start(f32[2,128,128]{2,1,0:T(8,128)S(1)} %get-tuple-element.50), channel_id=1, source_target_pairs={{0,128},{64,192},{128,0},{192,64},{1,129},{65,193},{129,1},{193,65... | collective-permute-start | bytes 393224 | tf_op jit(solution)/shard_map/ppermute | solution.py:495
  62.4 7.3 %collective-permute-start.12 = (f32[2,128,128]{2,1,0:T(8,128)S(1)}, f32[2,128,128]{2,1,0:T(8,128)S(1)}, u32[]{:S(2)}, u32[]{:S(2)}) collective-permute-start(f32[2,128,128]{2,1,0:T(8,128)S(1)} %get-tuple-element.51), channel_id=1, source_target_pairs={{0,192},{64,0},{128,64},{192,128},{1,193},{65,1},{129,65},{193,129... | collective-permute-start | bytes 393224 | tf_op jit(solution)/shard_map/ppermute | solution.py:495
  76.0 9.4 %collective-permute-start.16 = (f32[32,2048]{1,0:T(8,128)S(1)}, f32[32,2048]{1,0:T(8,128)S(1)}, u32[]{:S(2)}, u32[]{:S(2)}) collective-permute-start(f32[32,2048]{1,0:T(8,128)S(1)} %get-tuple-element.58), channel_id=1, source_target_pairs={{0,64},{64,128},{128,192},{192,0},{1,65},{65,129},{129,193},{193,1... | collective-permute-start | bytes 786440 | tf_op jit(solution)/shard_map/ppermute | solution.py:495
  77.3 14.0 %collective-permute-start.17 = (f32[32,2048]{1,0:T(8,128)S(1)}, f32[32,2048]{1,0:T(8,128)S(1)}, u32[]{:S(2)}, u32[]{:S(2)}) collective-permute-start(f32[32,2048]{1,0:T(8,128)S(1)} %get-tuple-element.59), channel_id=1, source_target_pairs={{0,128},{64,192},{128,0},{192,64},{1,129},{65,193},{129,1},{193,65... | collective-permute-start | bytes 786440 | tf_op jit(solution)/shard_map/ppermute | solution.py:495
  79.6 11.6 %collective-permute-start.18 = (f32[32,2048]{1,0:T(8,128)S(1)}, f32[32,2048]{1,0:T(8,128)S(1)}, u32[]{:S(2)}, u32[]{:S(2)}) collective-permute-start(f32[32,2048]{1,0:T(8,128)S(1)} %get-tuple-element.60), channel_id=1, source_target_pairs={{0,192},{64,0},{128,64},{192,128},{1,193},{65,1},{129,65},{193,129... | collective-permute-start | bytes 786440 | tf_op jit(solution)/shard_map/ppermute | solution.py:495
